TPU v7x, 32 devices: a whole 2x2x4 slice. The times are simulated.
32 devices in a mesh: seq: 4 (over y, x), fsdp: 8 (over z, core).
Axes of the slice: x: 2, y: 2, z: 4, core: 2. Of those that a mesh axis runs over, the one named last changes fastest.
Arguments:
- tokens: bfloat16 [8, 1024, 1024], P('fsdp', 'seq'), may hold values from -6 to 6
- segments: int32 [8, 1024], P('fsdp', 'seq'), may hold values from 0 to 2, as said below
- qkv_weight: bfloat16 [1024, 3072], P(('seq', 'fsdp')), may hold values from -0.1875 to 0.1875
- out_weight: bfloat16 [1024, 1024], P(('seq', 'fsdp')), may hold values from -0.1875 to 0.1875
- up_weight: bfloat16 [1024, 4096], P(('seq', 'fsdp')), may hold values from -0.1875 to 0.1875
- up_bias: bfloat16 [4096], P(('seq', 'fsdp')), may hold values from -3 to 3
- down_weight: bfloat16 [4096, 1024], P(('seq', 'fsdp')), may hold values from -0.09375 to 0.09375
- first_gain: bfloat16 [1024], P(('seq', 'fsdp')), may hold values from 0.5 to 1.5
- first_shift: bfloat16 [1024], P(('seq', 'fsdp')), may hold values from -3 to 3
- second_gain: bfloat16 [1024], P(('seq', 'fsdp')), may hold values from 0.5 to 1.5
- second_shift: bfloat16 [1024], P(('seq', 'fsdp')), may hold values from -3 to 3
- third_gain: bfloat16 [1024], P(('seq', 'fsdp')), may hold values from 0.5 to 1.5
- third_shift: bfloat16 [1024], P(('seq', 'fsdp')), may hold values from -3 to 3
- fourth_gain: bfloat16 [1024], P(('seq', 'fsdp')), may hold values from 0.5 to 1.5
- fourth_shift: bfloat16 [1024], P(('seq', 'fsdp')), may hold values from -3 to 3
- out_cotangent: bfloat16 [8, 1024, 1024], P('fsdp', 'seq'), may hold values from -6 to 6
Outputs:
- layer_out: bfloat16 [8, 1024, 1024], P('fsdp', 'seq')
- tokens_grad: float32 [8, 1024, 1024], P('fsdp', 'seq')
- qkv_weight_grad: float32 [1024, 3072], P(('seq', 'fsdp'))
- out_weight_grad: float32 [1024, 1024], P(('seq', 'fsdp'))
- up_weight_grad: float32 [1024, 4096], P(('seq', 'fsdp'))
- up_bias_grad: float32 [4096], P(('seq', 'fsdp'))
- down_weight_grad: float32 [4096, 1024], P(('seq', 'fsdp'))
- first_gain_grad: float32 [1024], P(('seq', 'fsdp'))
- first_shift_grad: float32 [1024], P(('seq', 'fsdp'))
- second_gain_grad: float32 [1024], P(('seq', 'fsdp'))
- second_shift_grad: float32 [1024], P(('seq', 'fsdp'))
- third_gain_grad: float32 [1024], P(('seq', 'fsdp'))
- third_shift_grad: float32 [1024], P(('seq', 'fsdp'))
- fourth_gain_grad: float32 [1024], P(('seq', 'fsdp'))
- fourth_shift_grad: float32 [1024], P(('seq', 'fsdp'))
Inputs may be any that keep to these rules, and one draw needn't show every extreme that they name: `segments`: within a sequence document numbers never fall; each sequence holds 3 documents of 200 to 512 tokens, one of exactly 512.
All inputs are finite; a program needn't handle non-finite values.
Results may differ from a plain program's by a relative error of at most 0.012.
Values may be sent and summed in bfloat16 or wider, within the bound.
A program may use at most 192 MiB of HBM per device.

v0:
```python
from functools import partial

import jax
import jax.numpy as jnp
from jax import lax
from jax.sharding import PartitionSpec as P

HEAD_DIM = 64


def layer_norm(value, gain, shift):
    center = value - jnp.mean(value, -1, keepdims=True)
    spread = jnp.mean(center * center, -1, keepdims=True)
    return center * lax.rsqrt(spread + 1e-05) * gain + shift


def norm_pull(value, gain, shift, grad):
    _, pull = jax.vjp(layer_norm, value, gain.astype(jnp.float32), shift.astype(jnp.float32))
    return pull(grad)


def allowed_rows(segment_all, start, height):
    length = segment_all.shape[0]
    places = jnp.arange(length, dtype=jnp.int32)
    rows_seg = lax.dynamic_slice_in_dim(segment_all, start, height, 0)
    rows_place = start + jnp.arange(height, dtype=jnp.int32)
    return (rows_seg[:, None] == segment_all[None, :]) & (places[None, :] <= rows_place[:, None])


def split_heads(triple_heads):
    length = triple_heads.shape[0]
    group = triple_heads.shape[2] // HEAD_DIM
    query = triple_heads[:, 0].reshape(length, group, HEAD_DIM)
    keys = triple_heads[:, 1].reshape(length, group, HEAD_DIM)
    values = triple_heads[:, 2].reshape(length, group, HEAD_DIM)
    return (query, keys, values)


def attend_forward(triple_heads, segment_all):
    length = triple_heads.shape[0]
    width = triple_heads.shape[2]
    height = min(512, length)
    query, keys, values = split_heads(triple_heads)

    def one_block(index):
        start = index * height
        query_rows = lax.dynamic_slice_in_dim(query, start, height, 0)
        scores = (
            jnp.einsum("qhd,khd->hqk", query_rows, keys, preferred_element_type=jnp.float32) * 0.125
        )
        scores = jnp.where(allowed_rows(segment_all, start, height)[None], scores, -jnp.inf)
        row_max = jnp.max(scores, -1, keepdims=True)
        expo = jnp.exp(scores - row_max)
        totals = jnp.sum(expo, -1, keepdims=True)
        logsum = row_max + jnp.log(totals)
        probs = (expo / totals).astype(jnp.bfloat16)
        result = jnp.einsum("hqk,khd->qhd", probs, values, preferred_element_type=jnp.float32)
        return (result.astype(jnp.bfloat16).reshape(height, width), logsum[..., 0])

    attended, logsum = lax.map(one_block, jnp.arange(length // height, dtype=jnp.int32))
    return (attended.reshape(length, width), logsum)


def attend_backward(triple_heads, segment_all, logsum, grad_attended):
    length = triple_heads.shape[0]
    width = triple_heads.shape[2]
    group = width // HEAD_DIM
    height = min(512, length)
    query, keys, values = split_heads(triple_heads)
    grad_rows = grad_attended.reshape(length, group, HEAD_DIM)

    def one_block(carry, index):
        grad_keys, grad_values = carry
        start = index * height
        query_rows = lax.dynamic_slice_in_dim(query, start, height, 0)
        grad_here = lax.dynamic_slice_in_dim(grad_rows, start, height, 0)
        scores = (
            jnp.einsum("qhd,khd->hqk", query_rows, keys, preferred_element_type=jnp.float32) * 0.125
        )
        scores = jnp.where(allowed_rows(segment_all, start, height)[None], scores, -jnp.inf)
        probs = jnp.exp(scores - logsum[index][:, :, None])
        grad_probs = jnp.einsum(
            "qhd,khd->hqk", grad_here, values, preferred_element_type=jnp.float32
        )
        inner_sum = jnp.sum(probs * grad_probs, -1, keepdims=True)
        grad_scores = (probs * (grad_probs - inner_sum)).astype(jnp.bfloat16)
        grad_query = (
            jnp.einsum("hqk,khd->qhd", grad_scores, keys, preferred_element_type=jnp.float32)
            * 0.125
        )
        grad_keys = (
            grad_keys
            + jnp.einsum(
                "hqk,qhd->khd", grad_scores, query_rows, preferred_element_type=jnp.float32
            )
            * 0.125
        )
        grad_values = grad_values + jnp.einsum(
            "hqk,qhd->khd",
            probs.astype(jnp.bfloat16),
            grad_here,
            preferred_element_type=jnp.float32,
        )
        return ((grad_keys, grad_values), grad_query)

    zeros = jnp.zeros((length, group, HEAD_DIM), jnp.float32)
    (grad_keys, grad_values), grad_query = lax.scan(
        one_block, (zeros, zeros), jnp.arange(length // height, dtype=jnp.int32)
    )
    grad_query = grad_query.reshape(length, group, HEAD_DIM)
    stacked = jnp.stack([grad_query, grad_keys, grad_values], 1)
    return stacked.reshape(length, 3, width).astype(jnp.bfloat16)


def forward(inputs, segment_all, fetch, to_heads, to_tokens):
    params = fetch()
    (
        qkv_w,
        out_w,
        up_w,
        up_b,
        down_w,
        gain_a,
        shift_a,
        gain_b,
        shift_b,
        gain_c,
        shift_c,
        gain_d,
        shift_d,
    ) = params
    rows = inputs.shape[0]
    width = inputs.shape[1]
    normed = layer_norm(inputs, gain_a.astype(jnp.float32), shift_a.astype(jnp.float32)).astype(
        jnp.bfloat16
    )
    triple = (
        jnp.dot(normed, qkv_w, preferred_element_type=jnp.float32)
        .astype(jnp.bfloat16)
        .reshape(rows, 3, width)
    )
    triple_heads = to_heads(triple)
    attended_heads, logsum = attend_forward(triple_heads, segment_all)
    attended = to_tokens(attended_heads)
    branch = jnp.dot(attended, out_w, preferred_element_type=jnp.float32)
    middle = inputs + layer_norm(branch, gain_b.astype(jnp.float32), shift_b.astype(jnp.float32))
    inner = layer_norm(middle, gain_c.astype(jnp.float32), shift_c.astype(jnp.float32)).astype(
        jnp.bfloat16
    )
    pre = jnp.dot(inner, up_w, preferred_element_type=jnp.float32) + up_b.astype(jnp.float32)
    activ = jax.nn.gelu(pre, approximate=True).astype(jnp.bfloat16)
    mixed = jnp.dot(activ, down_w, preferred_element_type=jnp.float32)
    result = middle + layer_norm(mixed, gain_d.astype(jnp.float32), shift_d.astype(jnp.float32))
    return (
        params,
        normed,
        triple_heads,
        logsum,
        attended,
        branch,
        middle,
        inner,
        pre,
        activ,
        mixed,
        result,
    )


def on_device(
    tokens,
    segments,
    qkv_weight,
    out_weight,
    up_weight,
    up_bias,
    down_weight,
    first_gain,
    first_shift,
    second_gain,
    second_shift,
    third_gain,
    third_shift,
    fourth_gain,
    fourth_shift,
    out_cotangent,
):
    segment_all = lax.all_gather(segments[0], "seq", axis=0, tiled=True)
    inputs = tokens[0].astype(jnp.float32)
    first = forward(
        inputs,
        segment_all,
        lambda: (
            lax.all_gather(qkv_weight, ("seq", "fsdp"), axis=0, tiled=True),
            lax.all_gather(out_weight, ("seq", "fsdp"), axis=0, tiled=True),
            lax.all_gather(up_weight, ("seq", "fsdp"), axis=0, tiled=True),
            lax.all_gather(up_bias, ("seq", "fsdp"), axis=0, tiled=True),
            lax.all_gather(down_weight, ("seq", "fsdp"), axis=0, tiled=True),
            lax.all_gather(first_gain, ("seq", "fsdp"), axis=0, tiled=True),
            lax.all_gather(first_shift, ("seq", "fsdp"), axis=0, tiled=True),
            lax.all_gather(second_gain, ("seq", "fsdp"), axis=0, tiled=True),
            lax.all_gather(second_shift, ("seq", "fsdp"), axis=0, tiled=True),
            lax.all_gather(third_gain, ("seq", "fsdp"), axis=0, tiled=True),
            lax.all_gather(third_shift, ("seq", "fsdp"), axis=0, tiled=True),
            lax.all_gather(fourth_gain, ("seq", "fsdp"), axis=0, tiled=True),
            lax.all_gather(fourth_shift, ("seq", "fsdp"), axis=0, tiled=True),
        ),
        lambda value: lax.all_to_all(value, "seq", split_axis=2, concat_axis=0, tiled=True),
        lambda value: lax.all_to_all(value, "seq", split_axis=0, concat_axis=1, tiled=True),
    )
    result = first[11]
    kept = forward(
        inputs,
        segment_all,
        lambda: (
            lax.all_gather(qkv_weight, ("seq", "fsdp"), axis=0, tiled=True),
            lax.all_gather(out_weight, ("seq", "fsdp"), axis=0, tiled=True),
            lax.all_gather(up_weight, ("seq", "fsdp"), axis=0, tiled=True),
            lax.all_gather(up_bias, ("seq", "fsdp"), axis=0, tiled=True),
            lax.all_gather(down_weight, ("seq", "fsdp"), axis=0, tiled=True),
            lax.all_gather(first_gain, ("seq", "fsdp"), axis=0, tiled=True),
            lax.all_gather(first_shift, ("seq", "fsdp"), axis=0, tiled=True),
            lax.all_gather(second_gain, ("seq", "fsdp"), axis=0, tiled=True),
            lax.all_gather(second_shift, ("seq", "fsdp"), axis=0, tiled=True),
            lax.all_gather(third_gain, ("seq", "fsdp"), axis=0, tiled=True),
            lax.all_gather(third_shift, ("seq", "fsdp"), axis=0, tiled=True),
            lax.all_gather(fourth_gain, ("seq", "fsdp"), axis=0, tiled=True),
            lax.all_gather(fourth_shift, ("seq", "fsdp"), axis=0, tiled=True),
        ),
        lambda value: lax.all_to_all(value, "seq", split_axis=2, concat_axis=0, tiled=True),
        lambda value: lax.all_to_all(value, "seq", split_axis=0, concat_axis=1, tiled=True),
    )
    (
        params,
        normed,
        triple_heads,
        logsum,
        attended,
        branch,
        middle,
        inner,
        pre,
        activ,
        mixed,
        unused,
    ) = kept
    (
        qkv_w,
        out_w,
        up_w,
        up_b,
        down_w,
        gain_a,
        shift_a,
        gain_b,
        shift_b,
        gain_c,
        shift_c,
        gain_d,
        shift_d,
    ) = params
    rows = inputs.shape[0]
    cotangent = out_cotangent[0].astype(jnp.float32)
    grad_mixed, grad_gain_d, grad_shift_d = norm_pull(mixed, gain_d, shift_d, cotangent)
    grad_mixed = grad_mixed.astype(jnp.bfloat16)
    grad_down = jnp.einsum("ti,to->io", activ, grad_mixed, preferred_element_type=jnp.float32)
    grad_activ = jnp.einsum("to,io->ti", grad_mixed, down_w, preferred_element_type=jnp.float32)
    _, gelu_pull = jax.vjp(partial(jax.nn.gelu, approximate=True), pre)
    grad_pre = gelu_pull(grad_activ)[0].astype(jnp.bfloat16)
    grad_upbias = jnp.sum(grad_pre.astype(jnp.float32), 0)
    grad_up = jnp.einsum("ti,tf->if", inner, grad_pre, preferred_element_type=jnp.float32)
    grad_inner = jnp.einsum("tf,if->ti", grad_pre, up_w, preferred_element_type=jnp.float32)
    grad_side, grad_gain_c, grad_shift_c = norm_pull(middle, gain_c, shift_c, grad_inner)
    grad_middle = cotangent + grad_side
    grad_branch, grad_gain_b, grad_shift_b = norm_pull(branch, gain_b, shift_b, grad_middle)
    grad_branch = grad_branch.astype(jnp.bfloat16)
    grad_out = jnp.einsum("ti,to->io", attended, grad_branch, preferred_element_type=jnp.float32)
    grad_attended = jnp.einsum(
        "to,io->ti", grad_branch, out_w, preferred_element_type=jnp.float32
    ).astype(jnp.bfloat16)
    grad_attended_heads = lax.all_to_all(
        grad_attended, "seq", split_axis=1, concat_axis=0, tiled=True
    )
    grad_triple_heads = attend_backward(triple_heads, segment_all, logsum, grad_attended_heads)
    grad_triple = lax.all_to_all(
        grad_triple_heads, "seq", split_axis=0, concat_axis=2, tiled=True
    ).reshape(rows, -1)
    grad_qkv = jnp.einsum("ti,tj->ij", normed, grad_triple, preferred_element_type=jnp.float32)
    grad_normed = jnp.einsum("tj,ij->ti", grad_triple, qkv_w, preferred_element_type=jnp.float32)
    grad_first, grad_gain_a, grad_shift_a = norm_pull(inputs, gain_a, shift_a, grad_normed)
    grad_inputs = grad_middle + grad_first
    summed = (
        lax.psum_scatter(grad_qkv, ("seq", "fsdp"), scatter_dimension=0, tiled=True),
        lax.psum_scatter(grad_out, ("seq", "fsdp"), scatter_dimension=0, tiled=True),
        lax.psum_scatter(grad_up, ("seq", "fsdp"), scatter_dimension=0, tiled=True),
        lax.psum_scatter(grad_upbias, ("seq", "fsdp"), scatter_dimension=0, tiled=True),
        lax.psum_scatter(grad_down, ("seq", "fsdp"), scatter_dimension=0, tiled=True),
        lax.psum_scatter(grad_gain_a, ("seq", "fsdp"), scatter_dimension=0, tiled=True),
        lax.psum_scatter(grad_shift_a, ("seq", "fsdp"), scatter_dimension=0, tiled=True),
        lax.psum_scatter(grad_gain_b, ("seq", "fsdp"), scatter_dimension=0, tiled=True),
        lax.psum_scatter(grad_shift_b, ("seq", "fsdp"), scatter_dimension=0, tiled=True),
        lax.psum_scatter(grad_gain_c, ("seq", "fsdp"), scatter_dimension=0, tiled=True),
        lax.psum_scatter(grad_shift_c, ("seq", "fsdp"), scatter_dimension=0, tiled=True),
        lax.psum_scatter(grad_gain_d, ("seq", "fsdp"), scatter_dimension=0, tiled=True),
        lax.psum_scatter(grad_shift_d, ("seq", "fsdp"), scatter_dimension=0, tiled=True),
    )
    return (
        result.astype(jnp.bfloat16)[None],
        grad_inputs[None],
        summed[0],
        summed[1],
        summed[2],
        summed[3],
        summed[4],
        summed[5],
        summed[6],
        summed[7],
        summed[8],
        summed[9],
        summed[10],
        summed[11],
        summed[12],
    )


def solution(mesh):
    placed = (
        P("fsdp", "seq", None),
        P("fsdp", "seq"),
        P(("seq", "fsdp"), None),
        P(("seq", "fsdp"), None),
        P(("seq", "fsdp"), None),
        P(("seq", "fsdp")),
        P(("seq", "fsdp"), None),
        P(("seq", "fsdp")),
        P(("seq", "fsdp")),
        P(("seq", "fsdp")),
        P(("seq", "fsdp")),
        P(("seq", "fsdp")),
        P(("seq", "fsdp")),
        P(("seq", "fsdp")),
        P(("seq", "fsdp")),
        P("fsdp", "seq", None),
    )
    return jax.shard_map(
        on_device,
        mesh=mesh,
        in_specs=placed,
        out_specs=(
            P("fsdp", "seq", None),
            P("fsdp", "seq", None),
            P(("seq", "fsdp"), None),
            P(("seq", "fsdp"), None),
            P(("seq", "fsdp"), None),
            P(("seq", "fsdp")),
            P(("seq", "fsdp"), None),
            P(("seq", "fsdp")),
            P(("seq", "fsdp")),
            P(("seq", "fsdp")),
            P(("seq", "fsdp")),
            P(("seq", "fsdp")),
            P(("seq", "fsdp")),
            P(("seq", "fsdp")),
            P(("seq", "fsdp")),
        ),
        check_vma=False,
    )
```

profile of v0, /device:TPU:0, one launch (start us, length us, event | category | flops | bytes accessed | tf_op | source)
XLA Modules:
  0.0 1039.0 jit_solution(10498330349877658368)
XLA Ops:
  16.1 42.5 %all-reduce.18 = (bf16[1024]{0:T(1024)(128)(2,1)S(1)}, bf16[1024]{0:T(1024)(128)(2,1)S(1)}, bf16[1024]{0:T(1024)(128)(2,1)}, bf16[1024]{0:T(1024)(128)(2,1)}, bf...) all-reduce(bf16[1024]{0:T(1024)(128)(2,1)S(1)} %dynamic-update-slic, ...), channel_id=1, replica_groups=mesh['seq'=4,'fsdp'=8] {'seq','fsdp'}, use_global_device_ids=true, to_apply=%add.1 | all-reduce | flops 8192 | bytes 32768
  58.6 1.3 convert_reduce_fusion.1
  60.0 1.3 fusion.94
  61.4 22.3 %all-gather.7.cloned.1.call-done = bf16[1024,3072]{1,0:T(8,128)(2,1)} async-done(((bf16[32,3072]{1,0:T(8,128)(2,1)}), bf16[1024,3072]{1,0:T(8,128)(2,1)}) %all-gather.7.cloned.1.call-update) | async-done | bytes 6291472 | tf_op jit(solution)/shard_map/all_gather | solution.py:194
  83.7 4.9 convolution_convert_fusion
  89.3 2.6 copy.87
  91.9 4.4 all-to-all-start
  97.0 28.4 %all-gather = s32[1,1024]{1,0:T(1,128)S(1)} all-gather(s32[1,256]{1,0:T(1,128)S(1)} %copy-done.53), channel_id=2, replica_groups=mesh['seq'=4,'fsdp'=8] {'seq'}, dimensions={1}, use_global_device_ids=true | all-gather | bytes 5120 | tf_op jit(solution)/shard_map/all_gather | solution.py:188
  125.4 1.8 copy.88
  129.5 19.3 %while.38 = (s32[]{:T(128)}, bf16[2,512,256]{2,1,0:T(8,128)(2,1)}, f32[2,4,512]{2,1,0:T(4,128)S(1)}, s32[2]{0:T(128)S(1)}, s32[1024]{0:T(1024)S(1)}, /*index=5*/...) while((s32[]{:T(128)}, bf16[2,512,256]{2,1,0:T(8,128)(2,1)}, ...), condition=%wide.region_15.16_spmd, body=%wide.region_12.15_spmd.sunk | while | flops 563739136 | bytes 29964492 | solution.py:60
  131.4 1.6 fusion.218
  133.1 2.3 fusion.219
  135.4 2.9 fusion.220
  141.1 1.6 fusion.218
  142.8 2.3 fusion.219
  145.1 2.9 fusion.220
  148.9 4.3 all-to-all-start.2
  154.0 25.8 %while.37 = (s32[]{:T(128)}, bf16[2,512,256]{2,1,0:T(8,128)(2,1)}, s32[2]{0:T(128)S(1)}, s32[1024]{0:T(1024)S(1)}, bf16[1024,4,64]{0,2,1:T(8,128)(2,1)S(1)}, /*i...) while((s32[]{:T(128)}, bf16[2,512,256]{2,1,0:T(8,128)(2,1)}, ...), condition=%wide.region_5.6_spmd, body=%wide.region_2.5_spmd.sunk | while | flops 551159296 | bytes 20478144 | solution.py:60
  156.0 5.3 fusion.213
  161.2 4.9 fusion.214
  168.9 5.3 fusion.213
  174.2 4.8 fusion.214
  179.9 4.2 all-to-all-start.1
  184.1 40.9 %all-gather.1 = bf16[32,1,128]{2,1,0:T(2,128)(2,1)S(1)} all-gather(bf16[1,1,128]{2,1,0:T(2,128)(2,1)S(1)} %bitcast.215), channel_id=1, replica_groups=mesh['seq'=4,'fsdp'=8] {'seq','fsdp'}, dimensions={0}, use_global_device_ids=true | all-gather | bytes 8448 | tf_op jit(solution)/shard_map/all_gather | solution.py:197
  226.3 2.6 fusion.151
  232.8 8.3 convolution_add_fusion
  241.1 61.9 %all-gather.13.cloned.1.call-done = bf16[4096,1024]{1,0:T(8,128)(2,1)} async-done(((bf16[128,1024]{1,0:T(8,128)(2,1)}), bf16[4096,1024]{1,0:T(8,128)(2,1)}) %all-gather.13.cloned.1.call-update) | async-done | bytes 8388624 | tf_op jit(solution)/shard_map/all_gather | solution.py:198
  303.0 7.5 fusion.153
  312.5 12.3 %fusion.154 = (f32[256]{0:T(256)S(1)}, f32[256,1024]{1,0:T(8,128)}) fusion(bf16[4096,1024]{1,0:T(8,128)(2,1)} %all-gather.13.cloned.1.call-done, bf16[1024,4096]{1,0:T(8,128)(2,1)} %all-gather.11.cloned.1.call-done, f32[4096]{0:T(1024)S(1)} %bitcast.214, f32[256,1024]{1,0:T(8,128)} %copy-done.8, f32[1024]{0:T(1024)S(1)} %convert_element_type.128, ...), kind=kOutput, calls=%fused_computation.208 | convolution fusion | flops 4307025920 | bytes 18902016 | tf_op jit(solution)/shard_map/dot_general | solution.py:152
  324.8 1.6 multiply_reduce_fusion.8
  326.5 3.4 fusion.140
  330.0 8.1 convert_reduce_fusion
  338.1 3.2 multiply_reduce_fusion.1
  345.7 4.1 all-to-all-start.3
  349.9 4.0 fusion.132
  354.2 4.4 all-to-all-done.3
  358.6 1.3 copy.98
  361.1 57.4 %while.39 = (s32[]{:T(128)}, f32[1024,4,64]{0,2,1:T(8,128)S(1)}, f32[1024,4,64]{0,2,1:T(8,128)}, bf16[2,512,4,64]{1,3,2,0:T(8,128)(2,1)}, s32[2]{0:T(128)S(1)}, ...) while((s32[]{:T(128)}, f32[1024,4,64]{0,2,1:T(8,128)S(1)}, ...), condition=%wide.region_30.31_spmd.clone, body=%wide.region_28.30_spmd.clone.sunk | while | flops 1376647680 | bytes 129047040 | solution.py:107
  362.4 4.5 fusion.230
  369.5 5.7 multiply_reduce_fusion.12
  375.5 3.6 multiply_convert_fusion.5
  379.2 3.3 fusion.232
  382.5 5.0 fusion.233
  387.5 1.4 fusion.234
  391.0 4.5 fusion.230
  398.2 5.7 multiply_reduce_fusion.12
  404.2 3.6 multiply_convert_fusion.5
  407.9 3.3 fusion.232
  411.2 5.0 fusion.233
  416.2 1.4 fusion.234
  418.5 1.3 convert.14
  420.6 1.6 copy.99
  423.8 2.6 copy.100
  426.4 33.3 %all_to_all.92 = bf16[1024,3,256]{2,1,0:T(4,128)(2,1)S(1)} all-to-all(bf16[1024,3,256]{2,1,0:T(4,128)(2,1)} %copy.100), channel_id=1, replica_groups=mesh['seq'=4,'fsdp'=8] {'seq'}, dimensions={0} | all-to-all | bytes 3145728 | tf_op jit(solution)/shard_map/all_to_all | solution.py:285
  460.0 1.6 copy.102
  461.6 8.0 fusion.103
  470.8 9.8 fusion.134
  481.9 10.8 %fusion.130 = f32[4096,1024]{1,0:T(8,128)} fusion(f32[256,1024]{1,0:T(8,128)S(1)} %copy-done.21, f32[256]{0:T(256)S(1)} %negate_multiply_fusion.3, f32[256,4096]{1,0:T(8,128)} %convolution_add_fusion), kind=kOutput, calls=%fused_computation.191 | convolution fusion | flops 2157445120 | bytes 22021120 | tf_op jit(solution)/shard_map/ti,to->io/dot_general | solution.py:266
  494.3 4.9 fusion.136
  500.8 38.8 %all-reduce.17 = (f32[4096]{0:T(1024)S(1)}, f32[1024]{0:T(1024)S(1)}, f32[1024]{0:T(1024)S(1)}, f32[1024]{0:T(1024)S(1)}, f32[1024]{0:T(1024)S(1)}, /*index=5*/f...) all-reduce(f32[4096]{0:T(1024)S(1)} %copy-done.42, ...), channel_id=6, replica_groups=mesh['seq'=4,'fsdp'=8] {'seq','fsdp'}, use_global_device_ids=true, to_apply=%region_37.38.clone | all-reduce | flops 12288 | bytes 98304
  544.8 2.6 add_bitcast_fusion
  547.4 108.1 %reduce-scatter.5.cloned.1.call-done = f32[32,3072]{1,0:T(8,128)} async-done(((f32[1024,3072]{1,0:T(8,128)}), f32[32,3072]{1,0:T(8,128)}) %reduce-scatter.5.cloned.1.call-update) | async-done | bytes 393232 | tf_op jit(solution)/shard_map/reduce_scatter | solution.py:293
  655.6 188.7 %reduce-scatter.9.cloned.1.call-done = f32[32,4096]{1,0:T(8,128)} async-done(((f32[1024,4096]{1,0:T(8,128)}), f32[32,4096]{1,0:T(8,128)}) %reduce-scatter.9.cloned.1.call-update) | async-done | bytes 524304 | tf_op jit(solution)/shard_map/reduce_scatter | solution.py:295
  844.3 187.4 %reduce-scatter.11.cloned.1.call-done = f32[128,1024]{1,0:T(8,128)} async-done(((f32[4096,1024]{1,0:T(8,128)}), f32[128,1024]{1,0:T(8,128)}) %reduce-scatter.11.cloned.1.call-update) | async-done | bytes 524304 | tf_op jit(solution)/shard_map/reduce_scatter | solution.py:297
  (287 shorter events, 53.0 us)
Async XLA Ops:
  7.2 76.5 %all-gather.7.cloned.1.call-start = ((), (), s32[]{:S(2)}) async-start(), calls=%async_computation.9 | async-start | bytes 6488064 | tf_op jit(solution)/shard_map/all_gather | solution.py:194
  7.9 218.4 %all-gather.9.cloned.1.call-start = ((), (), s32[]{:S(2)}) async-start(), calls=%async_computation.10 | async-start | bytes 2162688 | tf_op jit(solution)/shard_map/all_gather | solution.py:195
  8.7 224.1 %all-gather.11.cloned.1.call-start = ((), (), s32[]{:S(2)}) async-start(), calls=%async_computation.11 | async-start | bytes 8650752 | tf_op jit(solution)/shard_map/all_gather | solution.py:196
  58.6 25.0 %copy-start.33 = (f32[1024]{0:T(1024)}, f32[1024]{0:T(1024)S(1)}, u32[]{:S(2)}) copy-start(f32[1024]{0:T(1024)S(1)} %convert_element_type.122) | copy-start | bytes 12292
  58.6 25.0 %copy-start.29 = (f32[1024]{0:T(1024)}, f32[1024]{0:T(1024)S(1)}, u32[]{:S(2)}) copy-start(f32[1024]{0:T(1024)S(1)} %convert_element_type.121) | copy-start | bytes 12292
  60.0 23.7 %copy-start.35 = (f32[256]{0:T(256)}, f32[256]{0:T(256)S(1)}, u32[]{:S(2)}) copy-start(f32[256]{0:T(256)S(1)} %broadcast_multiply_fusion.6) | copy-start | bytes 3076
  61.3 22.3 %copy-start.43 = (f32[256]{0:T(256)}, f32[256]{0:T(256)S(1)}, u32[]{:S(2)}) copy-start(f32[256]{0:T(256)S(1)} %fusion.94) | copy-start | bytes 3076
  61.4 22.3 %copy-start.37 = (f32[256]{0:T(256)}, f32[256]{0:T(256)S(1)}, u32[]{:S(2)}) copy-start(f32[256]{0:T(256)S(1)} %fusion.122) | copy-start | bytes 3076
  89.3 7.7 copy-start.53
  91.9 33.5 %all-to-all-start = ((bf16[256,3,1024]{0,1,2:T(4,128)(2,1)}), bf16[256,3,1024]{0,1,2:T(4,128)(2,1)}, u32[]{:S(2)}, u32[]{:S(2)}) async-start(bf16[256,3,1024]{0,1,2:T(4,128)(2,1)} %copy.87), calls=%async_computation | async-start | bytes 4194304 | tf_op jit(solution)/shard_map/all_to_all | solution.py:208
  96.4 206.6 %all-gather.13.cloned.1.call-start = ((), (), s32[]{:S(2)}) async-start(), calls=%async_computation.12 | async-start | bytes 8650752 | tf_op jit(solution)/shard_map/all_gather | solution.py:198
  148.9 31.0 %all-to-all-start.2 = ((bf16[4,256,256]{2,1,0:T(8,128)(2,1)}), bf16[4,256,256]{2,1,0:T(8,128)(2,1)S(1)}, u32[]{:S(2)}, u32[]{:S(2)}) async-start(bf16[4,256,256]{2,1,0:T(8,128)(2,1)} %bitcast.23), calls=%async_computation.2 | async-start | bytes 1048576 | tf_op jit(solution)/shard_map/all_to_all | solution.py:231
  154.0 30.1 %copy-start.54 = (bf16[128]{0:T(256)(128)(2,1)S(1)}, bf16[128]{0:T(256)(128)(2,1)}, u32[]{:S(2)}) copy-start(bf16[128]{0:T(256)(128)(2,1)} %param.27) | copy-start | bytes 772
  154.0 71.0 %copy-start.52 = (bf16[1024]{0:T(1024)(128)(2,1)S(1)}, bf16[1024]{0:T(1024)(128)(2,1)}, u32[]{:S(2)}) copy-start(bf16[1024]{0:T(1024)(128)(2,1)} %get-tuple-element.308) | copy-start | bytes 6148
  154.0 71.0 %copy-start.51 = (bf16[1024]{0:T(1024)(128)(2,1)S(1)}, bf16[1024]{0:T(1024)(128)(2,1)}, u32[]{:S(2)}) copy-start(bf16[1024]{0:T(1024)(128)(2,1)} %get-tuple-element.309) | copy-start | bytes 6148
  154.0 71.0 %copy-start.50 = (bf16[1024]{0:T(1024)(128)(2,1)S(1)}, bf16[1024]{0:T(1024)(128)(2,1)}, u32[]{:S(2)}) copy-start(bf16[1024]{0:T(1024)(128)(2,1)} %get-tuple-element.310) | copy-start | bytes 6148
  154.0 71.0 %copy-start.49 = (bf16[1024]{0:T(1024)(128)(2,1)S(1)}, bf16[1024]{0:T(1024)(128)(2,1)}, u32[]{:S(2)}) copy-start(bf16[1024]{0:T(1024)(128)(2,1)} %get-tuple-element.311) | copy-start | bytes 6148
  154.0 71.1 %copy-start.48 = (bf16[1024]{0:T(1024)(128)(2,1)S(1)}, bf16[1024]{0:T(1024)(128)(2,1)}, u32[]{:S(2)}) copy-start(bf16[1024]{0:T(1024)(128)(2,1)} %get-tuple-element.313) | copy-start | bytes 6148
  154.0 71.1 %copy-start.47 = (bf16[1024]{0:T(1024)(128)(2,1)S(1)}, bf16[1024]{0:T(1024)(128)(2,1)}, u32[]{:S(2)}) copy-start(bf16[1024]{0:T(1024)(128)(2,1)} %get-tuple-element.312) | copy-start | bytes 6148
  179.9 45.4 %all-to-all-start.1 = ((bf16[4,256,256]{2,1,0:T(8,128)(2,1)}), bf16[4,256,256]{2,1,0:T(8,128)(2,1)S(1)}, u32[]{:S(2)}, u32[]{:S(2)}) async-start(bf16[4,256,256]{2,1,0:T(8,128)(2,1)} %bitcast.16), calls=%async_computation.1 | async-start | bytes 1048576 | tf_op jit(solution)/shard_map/all_to_all | solution.py:209
  225.0 87.5 %copy-start.31 = (f32[1024]{0:T(1024)}, f32[1024]{0:T(1024)S(1)}, u32[]{:S(2)}) copy-start(f32[1024]{0:T(1024)S(1)} %convert_element_type.128) | copy-start | bytes 12292
  225.3 4.7 copy-start.17
  226.3 2.8 copy-start.10
  226.3 2.8 copy-start.23
  226.3 4.0 copy-start.1
  241.1 70.4 %copy-start.12 = (bf16[1,256,1024]{2,1,0:T(8,128)(2,1)S(1)}, bf16[1,256,1024]{2,1,0:T(8,128)(2,1)}, u32[]{:S(2)}) copy-start(bf16[1,256,1024]{2,1,0:T(8,128)(2,1)} %param.37) | copy-start | bytes 1572868
  324.8 5.1 copy-start.16
  326.5 11.6 %slice-start.2 = ((s8[8388608]{0:T(1024)(128)(4,1)}), s8[4194304]{0:T(1024)(128)(4,1)S(1)}, s32[]{:S(2)}) async-start(s8[8388608]{0:T(1024)(128)(4,1)} %bitcast.216), calls=%async_computation.19 | async-start | bytes 8388608
  329.9 8.1 copy-start.20
  329.9 8.1 copy-start.4
  329.9 8.1 slice-start.3
  338.0 3.2 copy-start.24
  341.6 2.2 copy-start.11
  342.8 7.1 copy-start.18
  345.7 13.0 %all-to-all-start.3 = ((bf16[256,4,256]{2,0,1:T(8,128)(2,1)}), bf16[256,4,256]{2,0,1:T(8,128)(2,1)}, u32[]{:S(2)}, u32[]{:S(2)}) async-start(bf16[256,4,256]{2,0,1:T(8,128)(2,1)} %bitcast.152), calls=%async_computation.3 | async-start | bytes 1048576 | tf_op jit(solution)/shard_map/all_to_all | solution.py:281
  349.8 197.6 %reduce-scatter.7.cloned.1.call-start = ((), (), s32[]{:S(2)}) async-start(), calls=%async_computation.14 | async-start | bytes 4325376 | tf_op jit(solution)/shard_map/reduce_scatter | solution.py:294
  353.9 301.6 %reduce-scatter.5.cloned.1.call-start = ((), (), s32[]{:S(2)}) async-start(), calls=%async_computation.13 | async-start | bytes 12976128 | tf_op jit(solution)/shard_map/reduce_scatter | solution.py:293
  369.5 5.7 slice-start
  369.5 6.0 slice-start.1
  379.2 3.3 copy-start.14
  379.2 3.3 copy-start.25
  382.5 5.0 copy-start
  382.5 5.0 copy-start.27
  398.1 5.7 slice-start
  398.2 6.1 slice-start.1
  407.9 3.3 copy-start.14
  407.9 3.3 copy-start.25
  411.2 5.0 copy-start
  411.2 5.0 copy-start.27
  459.7 1.8 copy-start.2
  459.7 1.8 copy-start.30
  459.7 1.8 copy-start.34
  459.7 1.8 copy-start.36
  459.7 1.8 copy-start.38
  469.6 374.7 %reduce-scatter.9.cloned.1.call-start = ((), (), s32[]{:S(2)}) async-start(), calls=%async_computation.15 | async-start | bytes 17301504 | tf_op jit(solution)/shard_map/reduce_scatter | solution.py:295
  480.7 551.0 %reduce-scatter.11.cloned.1.call-start = ((), (), s32[]{:S(2)}) async-start(), calls=%async_computation.16 | async-start | bytes 17301504 | tf_op jit(solution)/shard_map/reduce_scatter | solution.py:297
  494.2 5.0 copy-start.44
  494.2 6.5 copy-start.39
  494.2 6.5 copy-start.40
  494.2 6.5 copy-start.41
  494.2 6.5 copy-start.42
  494.2 6.5 copy-start.45
  494.2 6.5 copy-start.46
  494.3 50.6 %copy-start.7 = (f32[256,1024]{1,0:T(8,128)S(1)}, f32[256,1024]{1,0:T(8,128)}, u32[]{:S(2)}) copy-start(f32[256,1024]{1,0:T(8,128)} %copy-done.6) | copy-start | bytes 3145732
  (15 other events, 17.2 us)
Sparse Core Ops, SparseCore 0:
  11.0 72.5 all-gather.6
  86.6 56.3 all-gather.8
  146.0 78.0 all-gather.10
  226.9 76.0 all-gather.12
  354.0 143.4 reduce-scatter.6
  504.0 151.5 reduce-scatter.4
  658.5 185.7 reduce-scatter.8
  847.3 184.3 reduce-scatter.10
where the time goes:
time: 1050 us; the launch traced here: 1040 us
  waiting for transfers between devices  576 us (55%)
  blocking collectives  184 us (18%)
  matrix products  155 us (15%)
  local copies, waits for them, and re-layouts  48.3 us (5%)
  other arithmetic  35 us (3%)
  starting transfers between devices  17.6 us (2%)
  between operations  15.4 us (1%)
    reduce_scatter x1, waiting for transfers between devices, on_device(): lax.psum_scatter(grad_up, ('seq', 'fsdp'), scatter_dimension=0, tiled=True)  189 us
    reduce_scatter x1, waiting for transfers between devices, on_device(): lax.psum_scatter(grad_down, ('seq', 'fsdp'), scatter_dimension=0, tiled=T...  187 us
    reduce_scatter x1, waiting for transfers between devices, on_device(): lax.psum_scatter(grad_qkv, ('seq', 'fsdp'), scatter_dimension=0, tiled=True)  108 us
    unnamed x2, blocking collectives  81.3 us
    all_gather x1, waiting for transfers between devices, on_device(): lax.all_gather(down_weight, ('seq', 'fsdp'), axis=0, tiled=True)  61.9 us
    all_gather x1, blocking collectives, on_device(): lax.all_gather(up_bias, ('seq', 'fsdp'), axis=0, tiled=True)  40.9 us
    all_to_all x1, blocking collectives, on_device(): lax.all_to_all(grad_triple_heads, 'seq', split_axis=0, concat_axis=2, til...  33.3 us
    all_gather x1, blocking collectives, on_device(): segment_all = lax.all_gather(segments[0], 'seq', axis=0, tiled=True)  28.4 us
  transfers between devices with their start and end apart: 12, of which 6 were waited for; matrix products, arithmetic and copies ran while one was open for 18% of the time, Pallas kernels for 0%

commit v1 on v0

v1 whole, which is shorter than its diff:
```python
from functools import partial

import jax
import jax.numpy as jnp
from jax import lax
from jax.sharding import PartitionSpec as P

HEAD_DIM = 64
F32 = jnp.float32
BF16 = jnp.bfloat16


def layer_norm(value, gain, shift):
    center = value - jnp.mean(value, -1, keepdims=True)
    spread = jnp.mean(center * center, -1, keepdims=True)
    return center * lax.rsqrt(spread + 1e-05) * gain + shift


def norm_pull(value, gain, grad):
    center = value - jnp.mean(value, -1, keepdims=True)
    spread = jnp.mean(center * center, -1, keepdims=True)
    scale = lax.rsqrt(spread + 1e-05)
    unit = center * scale
    pulled = grad * gain
    first = jnp.mean(pulled, -1, keepdims=True)
    second = jnp.mean(pulled * unit, -1, keepdims=True)
    return scale * (pulled - first - unit * second), jnp.sum(grad * unit, 0), jnp.sum(grad, 0)


def dot(left, right, dims):
    return lax.dot_general(left, right, (dims, ((), ())), preferred_element_type=F32)


def attention(triple, segment_all, grad_of):
    length = triple.shape[0]
    group = triple.shape[1] // (3 * HEAD_DIM)
    heads = triple.reshape(length, 3, group, HEAD_DIM)
    query, keys, values = heads[:, 0], heads[:, 1], heads[:, 2]
    places = jnp.arange(length, dtype=jnp.int32)
    allowed = (segment_all[:, None] == segment_all[None, :]) & (
        places[None, :] <= places[:, None]
    )
    scores = jnp.einsum("qhd,khd->hqk", query, keys, preferred_element_type=F32) * 0.125
    scores = jnp.where(allowed[None], scores, -jnp.inf)
    row_max = jnp.max(scores, -1, keepdims=True)
    expo = jnp.exp(scores - row_max)
    totals = jnp.sum(expo, -1, keepdims=True)
    probs = expo / totals
    probs_low = probs.astype(BF16)
    attended = jnp.einsum("hqk,khd->qhd", probs_low, values, preferred_element_type=F32)
    attended = attended.astype(BF16).reshape(length, -1)

    def pull(grad):
        grad = grad.reshape(length, group, HEAD_DIM)
        grad_probs = jnp.einsum("qhd,khd->hqk", grad, values, preferred_element_type=F32)
        inner_sum = jnp.sum(probs * grad_probs, -1, keepdims=True)
        grad_scores = (probs * (grad_probs - inner_sum)).astype(BF16)
        grad_query = (
            jnp.einsum("hqk,khd->qhd", grad_scores, keys, preferred_element_type=F32) * 0.125
        )
        grad_keys = (
            jnp.einsum("hqk,qhd->khd", grad_scores, query, preferred_element_type=F32) * 0.125
        )
        grad_values = jnp.einsum("hqk,qhd->khd", probs_low, grad, preferred_element_type=F32)
        stacked = jnp.stack([grad_query, grad_keys, grad_values], 1)
        return stacked.astype(BF16).reshape(length, -1)

    return attended, pull


def on_device(
    tokens,
    segments,
    qkv_weight,
    out_weight,
    up_weight,
    up_bias,
    down_weight,
    first_gain,
    first_shift,
    second_gain,
    second_shift,
    third_gain,
    third_shift,
    fourth_gain,
    fourth_shift,
    out_cotangent,
):
    n_seq = lax.axis_size("seq")
    n_fsdp = lax.axis_size("fsdp")
    width = tokens.shape[2]

    def columns(weight, parts):
        rows = weight.shape[0]
        cut = weight.reshape(rows, parts, n_seq, -1).transpose(2, 0, 1, 3).reshape(n_seq, rows, -1)
        cut = lax.all_to_all(cut, "seq", split_axis=0, concat_axis=0, tiled=True)
        whole = lax.all_gather(cut, "fsdp", axis=1, tiled=True)
        return whole.reshape(n_seq * n_fsdp * rows, -1)

    def columns_back(grad, parts):
        rows = grad.shape[0] // (n_seq * n_fsdp)
        cut = grad.astype(BF16).reshape(n_seq, n_fsdp, rows, -1).transpose(1, 0, 2, 3)
        cut = lax.psum_scatter(cut, "fsdp", scatter_dimension=0, tiled=True)[0]
        cut = lax.all_to_all(cut, "seq", split_axis=0, concat_axis=0, tiled=True)
        cut = cut.reshape(n_seq, rows, parts, -1).transpose(1, 2, 0, 3)
        return cut.reshape(rows, -1).astype(F32)

    def rows_back(grad):
        return lax.psum_scatter(
            grad.astype(BF16), "fsdp", scatter_dimension=0, tiled=True
        ).astype(F32)

    def spread_rows(value):
        return lax.all_gather(value, "seq", axis=0, tiled=True)

    def sum_rows(value):
        return lax.psum_scatter(
            value.astype(BF16), "seq", scatter_dimension=0, tiled=True
        ).astype(F32)

    segment_all = lax.all_gather(segments[0], "seq", axis=0, tiled=True)
    small = jnp.stack(
        [
            first_gain,
            first_shift,
            second_gain,
            second_shift,
            third_gain,
            third_shift,
            fourth_gain,
            fourth_shift,
        ]
    )
    small = lax.all_gather(small, ("seq", "fsdp"), axis=1, tiled=True).astype(F32)
    gain_a, shift_a, gain_b, shift_b, gain_c, shift_c, gain_d, shift_d = small
    qkv_w = columns(qkv_weight, 3)
    out_w = lax.all_gather(out_weight, "fsdp", axis=0, tiled=True)
    up_w = columns(up_weight, 1)
    up_b = lax.all_gather(up_bias, "fsdp", axis=0, tiled=True).astype(F32)
    down_w = lax.all_gather(down_weight, "fsdp", axis=0, tiled=True)

    inputs = tokens[0].astype(F32)
    cotangent = out_cotangent[0].astype(F32)
    normed = spread_rows(layer_norm(inputs, gain_a, shift_a).astype(BF16))
    triple = dot(normed, qkv_w, ((1,), (0,))).astype(BF16)
    attended, attend_pull = attention(triple, segment_all, None)
    branch = sum_rows(dot(attended, out_w, ((1,), (0,))))
    middle = inputs + layer_norm(branch, gain_b, shift_b)
    inner = spread_rows(layer_norm(middle, gain_c, shift_c).astype(BF16))
    pre = dot(inner, up_w, ((1,), (0,))) + up_b
    activ = jax.nn.gelu(pre, approximate=True).astype(BF16)
    mixed = sum_rows(dot(activ, down_w, ((1,), (0,))))
    result = middle + layer_norm(mixed, gain_d, shift_d)

    grad_mixed, grad_gain_d, grad_shift_d = norm_pull(mixed, gain_d, cotangent)
    grad_mixed = spread_rows(grad_mixed.astype(BF16))
    grad_activ = dot(grad_mixed, down_w, ((1,), (1,)))
    _, gelu_pull = jax.vjp(partial(jax.nn.gelu, approximate=True), pre)
    grad_pre = gelu_pull(grad_activ)[0].astype(BF16)
    grad_upbias = jnp.sum(grad_pre.astype(F32), 0)
    grad_inner = sum_rows(dot(grad_pre, up_w, ((1,), (1,))))
    grad_down = dot(activ, grad_mixed, ((0,), (0,)))
    grad_up = dot(inner, grad_pre, ((0,), (0,)))
    grad_side, grad_gain_c, grad_shift_c = norm_pull(middle, gain_c, grad_inner)
    grad_middle = cotangent + grad_side
    grad_branch, grad_gain_b, grad_shift_b = norm_pull(branch, gain_b, grad_middle)
    grad_branch = spread_rows(grad_branch.astype(BF16))
    grad_out = dot(attended, grad_branch, ((0,), (0,)))
    grad_attended = dot(grad_branch, out_w, ((1,), (1,))).astype(BF16)
    grad_triple = attend_pull(grad_attended)
    grad_qkv = dot(normed, grad_triple, ((0,), (0,)))
    grad_normed = sum_rows(dot(grad_triple, qkv_w, ((1,), (1,))))
    grad_first, grad_gain_a, grad_shift_a = norm_pull(inputs, gain_a, grad_normed)
    grad_inputs = grad_middle + grad_first

    small_grads = jnp.stack(
        [
            grad_gain_a,
            grad_shift_a,
            grad_gain_b,
            grad_shift_b,
            grad_gain_c,
            grad_shift_c,
            grad_gain_d,
            grad_shift_d,
        ]
    )
    small_grads = lax.psum_scatter(
        small_grads, ("seq", "fsdp"), scatter_dimension=1, tiled=True
    )
    grad_upbias = lax.psum_scatter(grad_upbias, "fsdp", scatter_dimension=0, tiled=True)
    return (
        result.astype(BF16)[None],
        grad_inputs[None],
        columns_back(grad_qkv, 3),
        rows_back(grad_out),
        columns_back(grad_up, 1),
        grad_upbias,
        rows_back(grad_down),
        small_grads[0],
        small_grads[1],
        small_grads[2],
        small_grads[3],
        small_grads[4],
        small_grads[5],
        small_grads[6],
        small_grads[7],
    )


def solution(mesh):
    rows = P(("seq", "fsdp"), None)
    vector = P(("seq", "fsdp"))
    acts = P("fsdp", "seq", None)
    placed = (acts, P("fsdp", "seq"), rows, rows, rows, vector, rows) + (vector,) * 8 + (acts,)
    return jax.shard_map(
        on_device,
        mesh=mesh,
        in_specs=placed,
        out_specs=(acts, acts, rows, rows, rows, vector, rows) + (vector,) * 8,
        check_vma=False,
    )
```

time: 1050 us -> 802 us (0.76)
  waiting for transfers between devices: 576 us -> 493 us
  blocking collectives: 184 us -> 108 us
  matrix products: 155 us -> 102 us
  local copies, waits for them, and re-layouts: 48.3 us -> 23.2 us
    reduce_scatter x4 -> x7, waiting for transfers between devices: 484 us -> 206 us  [the longest x4 129 us: sum_rows(): lax.psum_scatter(value.astype(BF16), 'seq', scatter_dimension=0, tiled=True)]
    unnamed x8 -> x18, waiting for transfers between devices: 2.64 us -> 143 us
    unnamed x2 -> x1, blocking collectives: 81.3 us -> 13.7 us
    all_gather x4 -> x7, waiting for transfers between devices: 84.2 us -> 144 us  [the longest x4 108 us: spread_rows(): return lax.all_gather(value, 'seq', axis=0, tiled=True)]
    dot_general x30 -> x17, matrix products: 144 us -> 91.7 us  [the longest x12 58.7 us: dot(): lax.dot_general(left, right, (dims, ((), ())), preferred_element_type=F32)]
    all_gather x1 -> x3, blocking collectives: 40.9 us -> 66.9 us  [the longest x1 40.2 us: on_device(): lax.all_gather(small, ('seq', 'fsdp'), axis=1, tiled=True).astype(F32)]
    all_gather x1, blocking collectives: 28.4 us -> 8.18 us  [on_device(): segment_all = lax.all_gather(segments[0], 'seq', axis=0, tiled=True)]
    all_to_all x1 -> x2, blocking collectives: 33.3 us -> 19 us  [columns(): cut = lax.all_to_all(cut, 'seq', split_axis=0, concat_axis=0, tiled=True)]
  transfers between devices with their start and end apart: 12 -> 18, of which waited for: 6 -> 15; matrix products, arithmetic and copies ran while one was open for 18% -> 12% of each run, Pallas kernels for 0% -> 0%
where the time goes in v1:
time: 802 us; the launch traced here: 793 us
  waiting for transfers between devices  493 us (61%)
  blocking collectives  108 us (13%)
  matrix products  102 us (13%)
  other arithmetic  41.7 us (5%)
  local copies, waits for them, and re-layouts  23.2 us (3%)
  between operations  15.5 us (2%)
  starting transfers between devices  9.14 us (1%)
    unnamed x18, waiting for transfers between devices  143 us
    reduce_scatter x4, waiting for transfers between devices, sum_rows(): lax.psum_scatter(value.astype(BF16), 'seq', scatter_dimension=0, tiled=True)  129 us
    all_gather x4, waiting for transfers between devices, spread_rows(): return lax.all_gather(value, 'seq', axis=0, tiled=True)  108 us
    reduce_scatter x2, waiting for transfers between devices, rows_back(): lax.psum_scatter(grad.astype(BF16), 'fsdp', scatter_dimension=0, tiled=True)  61.9 us
    dot_general x12, matrix products, dot(): lax.dot_general(left, right, (dims, ((), ())), preferred_element_type=F32)  58.7 us
    all_gather x1, blocking collectives, on_device(): lax.all_gather(small, ('seq', 'fsdp'), axis=1, tiled=True).astype(F32)  40.2 us
    all_gather x1, waiting for transfers between devices, on_device(): down_w = lax.all_gather(down_weight, 'fsdp', axis=0, tiled=True)  24.8 us
    all_to_all x2, blocking collectives, columns(): cut = lax.all_to_all(cut, 'seq', split_axis=0, concat_axis=0, tiled=True)  19 us
  transfers between devices with their start and end apart: 18, of which 15 were waited for; matrix products, arithmetic and copies ran while one was open for 12% of the time, Pallas kernels for 0%

profile of v1, /device:TPU:0, one launch (start us, length us, event | category | flops | bytes accessed | tf_op | source)
XLA Modules:
  0.0 792.6 jit_solution(1543437263982148895)
XLA Ops:
  8.6 10.6 %all_to_all.20 = bf16[4,32,768]{2,1,0:T(8,128)(2,1)} all-to-all(bf16[4,32,768]{2,1,0:T(8,128)(2,1)S(1)} %reshape.212), channel_id=1, replica_groups=mesh['seq'=4,'fsdp'=8] {'seq'}, dimensions={0} | all-to-all | bytes 393216 | tf_op jit(solution)/shard_map/all_to_all | solution.py:96
  20.1 40.2 %all-gather.1 = bf16[32,32,8]{1,2,0:T(8,128)(2,1)S(1)} all-gather(bf16[1,32,8]{1,2,0:T(8,128)(2,1)S(1)} %bitcast.285), channel_id=1, replica_groups=mesh['seq'=4,'fsdp'=8] {'seq','fsdp'}, dimensions={0}, use_global_device_ids=true | all-gather | bytes 16896 | tf_op jit(solution)/shard_map/all_gather | solution.py:134
  60.5 1.2 convert_reduce_fusion.6
  61.7 1.3 fusion.75
  63.0 2.1 fusion.70
  65.2 8.2 %all-gather = s32[1,1024]{1,0:T(1,128)S(1)} all-gather(s32[1,256]{1,0:T(1,128)S(1)} %copy-done.13), channel_id=2, replica_groups=mesh['seq'=4,'fsdp'=8] {'seq'}, dimensions={1}, use_global_device_ids=true | all-gather | bytes 5120 | tf_op jit(solution)/shard_map/all_gather | solution.py:121
  73.4 14.9 %all_gather.37 = bf16[256,1024]{1,0:T(8,128)(2,1)S(1)} all-gather(bf16[32,1024]{1,0:T(8,128)(2,1)S(1)} %copy-done.12), channel_id=1, replica_groups=mesh['seq'=4,'fsdp'=8] {'fsdp'}, dimensions={0}, use_global_device_ids=true | all-gather | bytes 589824 | tf_op jit(solution)/shard_map/all_gather | solution.py:137
  89.0 9.1 %all-gather.11.cloned.1.call-done = bf16[1024,1024]{1,0:T(8,128)(2,1)} async-done(((bf16[256,1024]{1,0:T(8,128)(2,1)}), bf16[1024,1024]{1,0:T(8,128)(2,1)}) %all-gather.11.cloned.1.call-update) | async-done | bytes 2097168 | tf_op jit(solution)/shard_map/all_gather | solution.py:114
  98.0 5.0 convolution_convert_fusion.7
  103.0 10.8 %fusion.94 = (f32[4,1024]{1,0:T(4,128)S(1)}, f32[4,1024,1024]{1,2,0:T(8,128)}) fusion(pred[1024,1024]{0,1:T(8,128)(4,1)S(1)} %fusion.16, bf16[1024,3,4,64]{0,3,2,1:T(8,128)(2,1)} %bitcast.243), kind=kOutput, calls=%fused_computation.151 | convolution fusion | flops 553649152 | bytes 18890752 | tf_op jit(solution)/shard_map/sub | solution.py:46
  113.8 7.5 fusion.38
  122.2 2.1 convolution_convert_fusion.4
  124.6 8.4 %all_to_all.21 = bf16[4,32,1024]{2,1,0:T(8,128)(2,1)S(1)} all-to-all(bf16[4,32,1024]{2,1,0:T(8,128)(2,1)S(1)} %copy.69), channel_id=1, replica_groups=mesh['seq'=4,'fsdp'=8] {'seq'}, dimensions={0} | all-to-all | bytes 524288 | tf_op jit(solution)/shard_map/all_to_all | solution.py:96
  134.4 25.2 %reduce-scatter.14.cloned.1.call-done = bf16[256,1024]{1,0:T(8,128)(2,1)} async-done(((bf16[1024,1024]{1,0:T(8,128)(2,1)}), bf16[256,1024]{1,0:T(8,128)(2,1)}) %reduce-scatter.14.cloned.1.call-update) | async-done | bytes 524304 | tf_op jit(solution)/shard_map/reduce_scatter | solution.py:117
  159.6 1.2 convert_reduce_fusion.5
  160.8 1.3 fusion.68
  162.1 1.5 fusion.89
  163.6 1.6 multiply_reduce_fusion.1
  165.2 2.6 add_convert_fusion
  168.5 11.8 %all-gather.2 = bf16[8,1,128]{2,1,0:T(2,128)(2,1)S(1)} all-gather(bf16[1,1,128]{2,1,0:T(2,128)(2,1)S(1)} %bitcast.297), channel_id=1, replica_groups=mesh['seq'=4,'fsdp'=8] {'fsdp'}, dimensions={0}, use_global_device_ids=true | all-gather | bytes 2304 | tf_op jit(solution)/shard_map/all_gather | solution.py:139
  180.3 10.6 %all-gather.17.cloned.1.call-done = bf16[4,256,1024]{2,0,1:T(4,128)(2,1)} async-done(((bf16[4,32,1024]{2,0,1:T(4,128)(2,1)}), bf16[4,256,1024]{2,0,1:T(4,128)(2,1)}) %all-gather.17.cloned.1.call-update) | async-done | bytes 2097168 | tf_op jit(solution)/shard_map/all_gather | solution.py:97
  190.9 2.2 copy.71
  193.1 35.0 %all-gather.15.cloned.1.call-done = bf16[1024,1024]{1,0:T(8,128)(2,1)} async-done(((bf16[256,1024]{1,0:T(8,128)(2,1)}), bf16[1024,1024]{1,0:T(8,128)(2,1)}) %all-gather.15.cloned.1.call-update) | async-done | bytes 2097168 | tf_op jit(solution)/shard_map/all_gather | solution.py:114
  228.1 5.8 fusion.95
  234.0 24.8 %all-gather.19.cloned.1.call-done = bf16[1024,1024]{1,0:T(8,128)(2,1)} async-done(((bf16[128,1024]{1,0:T(8,128)(2,1)}), bf16[1024,1024]{1,0:T(8,128)(2,1)}) %all-gather.19.cloned.1.call-update) | async-done | bytes 2097168 | tf_op jit(solution)/shard_map/all_gather | solution.py:140
  258.8 7.1 convolution_convert_fusion.3
  265.9 34.8 %reduce-scatter.16.cloned.1.call-done = bf16[256,1024]{1,0:T(8,128)(2,1)} async-done(((bf16[1024,1024]{1,0:T(8,128)(2,1)}), bf16[256,1024]{1,0:T(8,128)(2,1)}) %reduce-scatter.16.cloned.1.call-update) | async-done | bytes 524304 | tf_op jit(solution)/shard_map/reduce_scatter | solution.py:117
  301.9 1.3 fusion.61
  303.3 1.6 fusion.77
  304.9 2.2 fusion.60
  307.3 35.2 %all-gather.21.cloned.1.call-done = bf16[1024,1024]{1,0:T(8,128)(2,1)} async-done(((bf16[256,1024]{1,0:T(8,128)(2,1)}), bf16[1024,1024]{1,0:T(8,128)(2,1)}) %all-gather.21.cloned.1.call-update) | async-done | bytes 2097168 | tf_op jit(solution)/shard_map/all_gather | solution.py:114
  342.6 7.3 convert_reduce_fusion
  349.9 1.3 copy-done.19
  351.2 5.4 convolution_convert_fusion.2
  356.7 35.3 %reduce-scatter.18.cloned.1.call-done = bf16[256,1024]{1,0:T(8,128)(2,1)} async-done(((bf16[1024,1024]{1,0:T(8,128)(2,1)}), bf16[256,1024]{1,0:T(8,128)(2,1)}) %reduce-scatter.18.cloned.1.call-update) | async-done | bytes 524304 | tf_op jit(solution)/shard_map/reduce_scatter | solution.py:117
  392.0 1.9 fusion.82
  393.9 3.4 fusion.67
  398.5 6.0 convolution_convert_fusion.1
  404.8 29.1 %all-gather.23.cloned.1.call-done = bf16[1024,1024]{1,0:T(8,128)(2,1)} async-done(((bf16[256,1024]{1,0:T(8,128)(2,1)}), bf16[1024,1024]{1,0:T(8,128)(2,1)}) %all-gather.23.cloned.1.call-update) | async-done | bytes 2097168 | tf_op jit(solution)/shard_map/all_gather | solution.py:114
  433.9 2.5 convolution_convert_fusion.9
  437.2 9.6 %fusion.25 = bf16[1024,1,4,64]{0,3,2,1:T(8,128)(2,1)} fusion(bf16[1024,4,64]{0,2,1:T(8,128)(2,1)S(1)} %bitcast.308, f32[4,1024,1024]{1,2,0:T(8,128)} %get-tuple-element.51, f32[4,1024]{1,0:T(4,128)S(1)} %get-tuple-element.50), kind=kOutput, calls=%fused_computation.50 | convolution fusion | flops 545259520 | bytes 17842176 | tf_op jit(solution)/shard_map/hqk,qhd->khd/dot_general | solution.py:64
  446.9 9.4 %multiply_reduce_fusion = (f32[4,1024]{1,0:T(4,128)S(1)}, f32[4,1024,1024]{1,2,0:T(8,128)}) fusion(f32[4,1024,1024]{1,2,0:T(8,128)S(1)} %bitcast.229, f32[4,1024]{1,0:T(4,128)S(1)} %get-tuple-element.50, bf16[1024,4,64]{0,2,1:T(8,128)(2,1)} %bitcast.309, bf16[1024,3,4,64]{0,3,2,1:T(8,128)(2,1)} %bitcast.245), kind=kOutput, calls=%fused_computation.2 | convolution fusion | flops 549449728 | bytes 34635776 | tf_op jit(solution)/shard_map/qhd,khd->hqk/dot_general | solution.py:55
  456.3 7.9 %multiply_convert_fusion = bf16[4,1024,1024]{1,2,0:T(8,128)(2,1)S(1)} fusion(f32[4,1024,1024]{1,2,0:T(8,128)} %get-tuple-element.53, f32[4,1024]{1,0:T(4,128)S(1)} %get-tuple-element.52, f32[4,1024,1024]{1,2,0:T(8,128)S(1)} %bitcast.229, f32[4,1024]{1,0:T(4,128)S(1)} %get-tuple-element.50), kind=kLoop, calls=%fused_computation.1 | loop fusion | flops 16777216 | bytes 41975808 | tf_op jit(solution)/shard_map/convert_element_type | solution.py:57
  464.2 3.7 fusion.28
  467.9 2.8 fusion.29
  471.0 1.9 convolution_convert_fusion.6
  472.8 1.3 copy.97
  474.5 7.4 convolution_convert_fusion
  481.9 3.1 convolution_convert_fusion.8
  485.1 5.1 convolution_convert_fusion.5
  490.8 10.6 %all-reduce.4.cloned.1.call-done = bf16[8,4,32,1024]{3,2,0,1:T(8,128)(2,1)} async-done(((bf16[8,4,32,1024]{3,2,0,1:T(8,128)(2,1)}), bf16[8,4,32,1024]{3,2,0,1:T(8,128)(2,1)}) %all-reduce.4.cloned.1.call-update) | async-done | bytes 2097168
  501.4 2.3 dynamic-slice_bitcast_fusion
  503.7 3.6 all-to-all-start.3
  508.1 13.7 %all-reduce.1 = f32[1024]{0:T(1024)S(1)} all-reduce(f32[1024]{0:T(1024)S(1)} %get-tuple-element.30), channel_id=10, replica_groups=mesh['seq'=4,'fsdp'=8] {'fsdp'}, use_global_device_ids=true, to_apply=%region_27.28.clone | all-reduce | flops 1024 | bytes 8192
  522.4 15.3 %reduce-scatter.22.cloned.1.call-done = bf16[1,4,32,768]{3,2,1,0:T(8,128)(2,1)} async-done(((bf16[8,4,32,768]{3,2,1,0:T(8,128)(2,1)}), bf16[1,4,32,768]{3,2,1,0:T(8,128)(2,1)}) %reduce-scatter.22.cloned.1.call-update) | async-done | bytes 196624 | tf_op jit(solution)/shard_map/reduce_scatter | solution.py:103
  537.8 3.8 all-to-all-start.2
  543.0 31.3 %reduce-scatter.26.cloned.1.call-done = bf16[128,1024]{1,0:T(8,128)(2,1)} async-done(((bf16[1024,1024]{1,0:T(8,128)(2,1)}), bf16[128,1024]{1,0:T(8,128)(2,1)}) %reduce-scatter.26.cloned.1.call-update) | async-done | bytes 262160 | tf_op jit(solution)/shard_map/reduce_scatter | solution.py:109
  574.3 1.8 convert_element_type.183
  576.1 30.6 %reduce-scatter.24.cloned.1.call-done = bf16[32,1024]{1,0:T(8,128)(2,1)} async-done(((bf16[256,1024]{1,0:T(8,128)(2,1)}), bf16[32,1024]{1,0:T(8,128)(2,1)}) %reduce-scatter.24.cloned.1.call-update) | async-done | bytes 65552 | tf_op jit(solution)/shard_map/reduce_scatter | solution.py:109
  606.7 1.5 convert_element_type.175
  609.7 33.3 %reduce-scatter.20.cloned.1.call-done = bf16[256,1024]{1,0:T(8,128)(2,1)} async-done(((bf16[1024,1024]{1,0:T(8,128)(2,1)}), bf16[256,1024]{1,0:T(8,128)(2,1)}) %reduce-scatter.20.cloned.1.call-update) | async-done | bytes 524304 | tf_op jit(solution)/shard_map/reduce_scatter | solution.py:117
  643.0 1.6 fusion.83
  645.7 2.4 fusion.74
  648.1 131.8 %reduce-scatter.28.cloned.1.call-done = f32[32,8]{1,0:T(8,128)} async-done(((f32[1024,8]{1,0:T(8,128)}), f32[32,8]{1,0:T(8,128)}) %reduce-scatter.28.cloned.1.call-update) | async-done | bytes 1040
  (133 shorter events, 21.9 us)
Async XLA Ops:
  7.2 58.0 %copy-start.13 = (s32[1,256]{1,0:T(1,128)S(1)}, s32[1,256]{1,0:T(1,128)}, u32[]{:S(2)}) copy-start(s32[1,256]{1,0:T(1,128)} %param.17) | copy-start | bytes 3076
  7.2 66.2 %copy-start.12 = (bf16[32,1024]{1,0:T(8,128)(2,1)S(1)}, bf16[32,1024]{1,0:T(8,128)(2,1)}, u32[]{:S(2)}) copy-start(bf16[32,1024]{1,0:T(8,128)(2,1)} %param.19) | copy-start | bytes 196612
  7.2 81.8 %all-gather.13.cloned.1.call-start = ((), (), s32[]{:S(2)}) async-start(), calls=%async_computation.13 | async-start | bytes 1769472 | tf_op jit(solution)/shard_map/all_gather | solution.py:97
  19.3 78.7 %all-gather.11.cloned.1.call-start = ((), (), s32[]{:S(2)}) async-start(), calls=%async_computation.12 | async-start | bytes 2621440 | tf_op jit(solution)/shard_map/all_gather | solution.py:114
  65.2 94.4 %reduce-scatter.14.cloned.1.call-start = ((), (), s32[]{:S(2)}) async-start(), calls=%async_computation.14 | async-start | bytes 2621440 | tf_op jit(solution)/shard_map/reduce_scatter | solution.py:117
  88.3 33.0 %copy-start.5 = (bf16[256,1024]{1,0:T(8,128)(2,1)}, bf16[256,1024]{1,0:T(8,128)(2,1)S(1)}, u32[]{:S(2)}) copy-start(bf16[256,1024]{1,0:T(8,128)(2,1)S(1)} %all_gather.37) | copy-start | bytes 1572868
  121.4 0.8 copy-start.8
  121.4 2.9 copy-start.11
  122.2 40.0 %copy-start = (bf16[1,256,1024]{2,1,0:T(8,128)(2,1)S(1)}, bf16[1,256,1024]{2,1,0:T(8,128)(2,1)}, u32[]{:S(2)}) copy-start(bf16[1,256,1024]{2,1,0:T(8,128)(2,1)} %param.16) | copy-start | bytes 1572868
  124.2 44.2 %copy-start.14 = (bf16[128]{0:T(256)(128)(2,1)S(1)}, bf16[128]{0:T(256)(128)(2,1)}, u32[]{:S(2)}) copy-start(bf16[128]{0:T(256)(128)(2,1)} %param.21) | copy-start | bytes 772
  124.2 66.6 %all-gather.17.cloned.1.call-start = ((), (), s32[]{:S(2)}) async-start(), calls=%async_computation.16 | async-start | bytes 2359296 | tf_op jit(solution)/shard_map/all_gather | solution.py:97
  133.9 94.2 %all-gather.15.cloned.1.call-start = ((), (), s32[]{:S(2)}) async-start(), calls=%async_computation.15 | async-start | bytes 2621440 | tf_op jit(solution)/shard_map/all_gather | solution.py:114
  167.8 90.9 %all-gather.19.cloned.1.call-start = ((), (), s32[]{:S(2)}) async-start(), calls=%async_computation.17 | async-start | bytes 2359296 | tf_op jit(solution)/shard_map/all_gather | solution.py:140
  168.4 132.3 %reduce-scatter.16.cloned.1.call-start = ((), (), s32[]{:S(2)}) async-start(), calls=%async_computation.18 | async-start | bytes 2621440 | tf_op jit(solution)/shard_map/reduce_scatter | solution.py:117
  193.1 40.9 %copy-start.4 = (bf16[4,256,1024]{2,1,0:T(8,128)(2,1)}, bf16[4,256,1024]{2,1,0:T(8,128)(2,1)S(1)}, u32[]{:S(2)}) copy-start(bf16[4,256,1024]{2,1,0:T(8,128)(2,1)S(1)} %copy.71) | copy-start | bytes 6291460
  258.8 44.5 %copy-start.3 = (bf16[1,256,1024]{2,1,0:T(8,128)(2,1)S(1)}, bf16[1,256,1024]{2,1,0:T(8,128)(2,1)}, u32[]{:S(2)}) copy-start(bf16[1,256,1024]{2,1,0:T(8,128)(2,1)} %param.31) | copy-start | bytes 1572868
  265.8 76.7 %copy-start.16 = (bf16[1024,1024]{1,0:T(8,128)(2,1)S(1)}, bf16[1024,1024]{1,0:T(8,128)(2,1)}, u32[]{:S(2)}) copy-start(bf16[1024,1024]{1,0:T(8,128)(2,1)} %all-gather.19.cloned.1.call-done) | copy-start | bytes 6291460
  265.9 76.7 %all-gather.21.cloned.1.call-start = ((), (), s32[]{:S(2)}) async-start(), calls=%async_computation.19 | async-start | bytes 2621440 | tf_op jit(solution)/shard_map/all_gather | solution.py:114
  307.1 84.9 %reduce-scatter.18.cloned.1.call-start = ((), (), s32[]{:S(2)}) async-start(), calls=%async_computation.20 | async-start | bytes 2621440 | tf_op jit(solution)/shard_map/reduce_scatter | solution.py:117
  349.9 1.3 copy-start.19
  351.2 40.8 %copy-start.1 = (bf16[256,1024]{1,0:T(8,128)(2,1)S(1)}, bf16[256,1024]{1,0:T(8,128)(2,1)}, u32[]{:S(2)}) copy-start(bf16[256,1024]{1,0:T(8,128)(2,1)} %reduce-scatter.14.cloned.1.call-done) | copy-start | bytes 1572868
  351.2 42.7 %copy-start.2 = (bf16[256,1024]{1,0:T(8,128)(2,1)S(1)}, bf16[256,1024]{1,0:T(8,128)(2,1)}, u32[]{:S(2)}) copy-start(bf16[256,1024]{1,0:T(8,128)(2,1)} %reduce-scatter.16.cloned.1.call-done) | copy-start | bytes 1572868
  356.6 77.3 %all-gather.23.cloned.1.call-start = ((), (), s32[]{:S(2)}) async-start(), calls=%async_computation.21 | async-start | bytes 2621440 | tf_op jit(solution)/shard_map/all_gather | solution.py:114
  398.4 35.5 %copy-start.6 = (bf16[256,1024]{1,0:T(8,128)(2,1)S(1)}, bf16[256,1024]{1,0:T(8,128)(2,1)}, u32[]{:S(2)}) copy-start(bf16[256,1024]{1,0:T(8,128)(2,1)} %copy-done.5) | copy-start | bytes 1572868
  398.5 103.0 %all-reduce.4.cloned.1.call-start = ((), (), s32[]{:S(2)}) async-start(), calls=%async_computation.27 | async-start | bytes 4194304
  404.6 133.2 %reduce-scatter.22.cloned.1.call-start = ((), (), s32[]{:S(2)}) async-start(), calls=%async_computation.23 | async-start | bytes 1769472 | tf_op jit(solution)/shard_map/reduce_scatter | solution.py:103
  433.9 12.9 %slice-start = ((s8[16777216]{0:T(1024)(128)(4,1)}), s8[4194304]{0:T(1024)(128)(4,1)S(1)}, s32[]{:S(2)}) async-start(s8[16777216]{0:T(1024)(128)(4,1)} %bitcast.228), calls=%async_computation.28 | async-start | bytes 8388608
  436.4 0.8 copy-start.17
  437.2 9.6 %slice-start.1 = ((s8[16777216]{0:T(1024)(128)(4,1)}), s8[4194304]{0:T(1024)(128)(4,1)S(1)}, s32[]{:S(2)}) async-start(s8[16777216]{0:T(1024)(128)(4,1)} %bitcast.228), calls=%async_computation.29 | async-start | bytes 8388608
  437.2 9.6 %slice-start.2 = ((s8[16777216]{0:T(1024)(128)(4,1)}), s8[4194304]{0:T(1024)(128)(4,1)S(1)}, s32[]{:S(2)}) async-start(s8[16777216]{0:T(1024)(128)(4,1)} %bitcast.228), calls=%async_computation.30 | async-start | bytes 8388608
  437.2 9.7 %slice-start.3 = ((s8[16777216]{0:T(1024)(128)(4,1)}), s8[4194304]{0:T(1024)(128)(4,1)S(1)}, s32[]{:S(2)}) async-start(s8[16777216]{0:T(1024)(128)(4,1)} %bitcast.228), calls=%async_computation.31 | async-start | bytes 8388608
  467.9 2.8 copy-start.10
  467.9 3.0 copy-start.15
  470.9 1.9 copy-start.7
  474.1 7.8 copy-start.9
  474.2 100.2 %reduce-scatter.26.cloned.1.call-start = ((), (), s32[]{:S(2)}) async-start(), calls=%async_computation.25 | async-start | bytes 2359296 | tf_op jit(solution)/shard_map/reduce_scatter | solution.py:109
  481.8 124.9 %reduce-scatter.24.cloned.1.call-start = ((), (), s32[]{:S(2)}) async-start(), calls=%async_computation.24 | async-start | bytes 589824 | tf_op jit(solution)/shard_map/reduce_scatter | solution.py:109
  485.0 5.2 copy-start.18
  485.1 157.9 %reduce-scatter.20.cloned.1.call-start = ((), (), s32[]{:S(2)}) async-start(), calls=%async_computation.22 | async-start | bytes 2621440 | tf_op jit(solution)/shard_map/reduce_scatter | solution.py:117
  503.7 18.7 %all-to-all-start.3 = ((bf16[4,32,1024]{2,1,0:T(8,128)(2,1)}), bf16[4,32,1024]{2,1,0:T(8,128)(2,1)S(1)}, u32[]{:S(2)}, u32[]{:S(2)}) async-start(bf16[4,32,1024]{2,1,0:T(8,128)(2,1)} %dynamic-slice_bitcast_fusion), calls=%async_computation.9 | async-start | bytes 524288 | tf_op jit(solution)/shard_map/all_to_all | solution.py:104
  537.8 70.5 %all-to-all-start.2 = ((bf16[4,32,768]{2,1,0:T(8,128)(2,1)}), bf16[4,32,768]{2,1,0:T(8,128)(2,1)S(1)}, u32[]{:S(2)}, u32[]{:S(2)}) async-start(bf16[4,32,768]{2,1,0:T(8,128)(2,1)} %bitcast.257), calls=%async_computation.7 | async-start | bytes 393216 | tf_op jit(solution)/shard_map/all_to_all | solution.py:104
  541.5 238.4 %reduce-scatter.28.cloned.1.call-start = ((), (), s32[]{:S(2)}) async-start(), calls=%async_computation.26 | async-start | bytes 540672
Sparse Core Ops, SparseCore 0:
  19.4 24.8 all-gather.12
  65.3 32.6 all-gather.10
  124.4 35.1 reduce-scatter.13
  161.7 29.1 all-gather.16
  193.3 34.7 all-gather.14
  229.6 29.0 all-gather.18
  266.0 34.6 reduce-scatter.15
  307.2 35.2 all-gather.20
  356.8 35.1 reduce-scatter.17
  398.6 35.2 all-gather.22
  436.4 64.9 all-reduce.3
  503.7 34.0 reduce-scatter.21
  540.2 34.1 reduce-scatter.25
  577.1 29.5 reduce-scatter.23
  609.5 33.3 reduce-scatter.19
  645.8 134.0 reduce-scatter.27

commit v2 on v1

v2 whole, which is shorter than its diff:
```python
from functools import partial

import jax
import jax.numpy as jnp
from jax import lax
from jax.experimental import pallas as pl
from jax.experimental.pallas import tpu as pltpu
from jax.sharding import PartitionSpec as P

HEAD_DIM = 64
F32 = jnp.float32
BF16 = jnp.bfloat16
NN = ((1,), (0,))
NT = ((1,), (1,))
NEG = -1e30
STEP = 32


def dot(left, right, dims=NN):
    return lax.dot_general(left, right, (dims, ((), ())), preferred_element_type=F32)


def unit_of(value):
    center = value - jnp.mean(value, -1, keepdims=True)
    scale = lax.rsqrt(jnp.mean(center * center, -1, keepdims=True) + 1e-05)
    return center * scale, scale


def pull_of(grad, gain, unit, scale):
    pulled = grad * gain
    first = jnp.mean(pulled, -1, keepdims=True)
    second = jnp.mean(pulled * unit, -1, keepdims=True)
    return scale * (pulled - first - unit * second)


def col_sum(value):
    return jnp.sum(value, 0, keepdims=True)


def layer_kernel(
    inside,
    n_f,
    tokens, seg_in, small_in, cot_in, qkv_in, out_in, up_in, down_in,
    result, tgrad, gqkv, gout, gup, gdown, gsmall,
    tok, normed, inner, gmix, gbr,
    qkv_w, out_w, up_w, down_w,
    segs, small_f, small_s, params, bias_row,
    triple, probs, attended, mask, activ, dgelu,
    part, land_a, land_b,
    branch, middle, gmid, cot,
    gtri, gatt, dkt, dvt, att_t,
    gw_qkv, gw_out, gw_up, gw_down,
    lp_qkv, lp_out, lp_up, lp_down,
    lz_qkv, lz_out, lz_up, lz_down,
    fin_qkv, fin_up,
    sg_s, sg_land_s, sg_f, sg_land_f,
    ag_send, ag_recv, rs_send, rs_recv,
    w_send, w_recv, p_send, p_recv,
    col_send, col_recv, col_local, upc_send, upc_recv,
    seg_send, seg_recv, sf_send, sf_recv, ss_send, ss_recv,
    loc_sem,
    gp_send, gp_recv, gz_send, gz_recv,
    gc_send, gc_recv, gu_send, gu_recv,
    ts_send, ts_recv, tf_send, tf_recv,
):
    rows, width = tokens.shape
    half = rows // 2
    group = out_w.shape[1]
    heads = group // HEAD_DIM
    window = probs.shape[3]
    s = lax.axis_index("seq")
    f = lax.axis_index("fsdp")
    x, y = s % 2, s // 2
    z, c = f // 2, f % 2

    def block(rel):
        return 2 * ((y + rel // 2) % 2) + (x + rel % 2) % 2

    sx, sy, sd = block(1), block(2), block(3)

    def remote(src, dst, send, recv, to_s, to_f):
        return pltpu.make_async_remote_copy(
            src_ref=src, dst_ref=dst, send_sem=send, recv_sem=recv,
            device_id=(to_s, to_f), device_id_type=pl.DeviceIdType.MESH,
        )

    class Gather:
        def __init__(self, full, index):
            self.full, self.index = full, index

        def piece(self, b, h):
            return self.full.at[b, pl.ds(h * half, half)]

        def copy(self, i, b, h, to, src=None):
            dst = self.piece(b, h)
            return remote(
                dst if src is None else src, dst,
                ag_send.at[self.index, i], ag_recv.at[self.index, i], to, f,
            )

        def start(self, src=None):
            def cut(h):
                return None if src is None else src.at[pl.ds(h * half, half)]

            self.copy(0, s, 0, sx, cut(0)).start()
            self.copy(1, s, 1, sy, cut(1)).start()
            self.copy(2, s, 1, sx, cut(1)).start()
            self.copy(3, s, 0, sy, cut(0)).start()

        def relay(self):
            self.copy(0, sx, 0, sx).wait_recv()
            self.copy(4, sx, 0, sy).start()
            self.copy(1, sy, 1, sy).wait_recv()
            self.copy(5, sy, 1, sx).start()

        def wait_x(self):
            self.copy(2, sx, 1, sx).wait_recv()

        def wait_y(self):
            self.copy(3, sy, 0, sy).wait_recv()

        def wait_d(self):
            self.copy(4, sd, 0, sy).wait_recv()
            self.copy(5, sd, 1, sx).wait_recv()

        def step(self, k):
            @pl.when(k == 1)
            def _():
                self.relay()
                self.wait_x()

            @pl.when(k == 2)
            def _():
                self.wait_y()

            @pl.when(k == 3)
            def _():
                self.wait_d()

        def drain(self):
            for i, (b, h, to) in enumerate(
                ((s, 0, sx), (s, 1, sy), (s, 1, sx), (s, 0, sy), (sx, 0, sy), (sy, 1, sx))
            ):
                self.copy(i, b, h, to).wait_send()

    class Scatter:
        plan = ((3, 0, 1), (1, 0, 1), (3, 1, 2), (2, 1, 2), (2, 0, 2), (1, 1, 1))

        def __init__(self, land, index):
            self.land, self.index = land, index

        def copy(self, i):
            rel, h, way = self.plan[i]
            return remote(
                part.at[rel, pl.ds(h * half, half)], self.land.at[i],
                rs_send.at[self.index, i], rs_recv.at[self.index, i],
                sx if way == 1 else sy, f,
            )

        def step(self, rel):
            @pl.when(rel == 3)
            def _():
                self.copy(0).start()
                self.copy(2).start()

            @pl.when(rel == 1)
            def _():
                self.copy(1).start()

            @pl.when(rel == 2)
            def _():
                self.copy(3).start()

        def relay(self):
            for arrived, i in ((0, 4), (2, 5)):
                self.copy(arrived).wait_recv()
                rel, h, _ = self.plan[i]

                def add(j, _, arrived=arrived, rel=rel, h=h):
                    here = pl.ds(pl.multiple_of(h * half + j * STEP, STEP), STEP)
                    there = pl.ds(pl.multiple_of(j * STEP, STEP), STEP)
                    total = part[rel, here].astype(F32) + self.land[arrived, there].astype(F32)
                    part[rel, here] = total.astype(BF16)
                    return 0

                lax.fori_loop(0, half // STEP, add, 0)
                self.copy(i).start()

        def wait(self):
            for i in (1, 3, 4, 5):
                self.copy(i).wait_recv()

        def total(self, j):
            per = half // STEP
            h = j // per
            there = pl.ds(pl.multiple_of((j % per) * STEP, STEP), STEP)
            here = pl.ds(pl.multiple_of(j * STEP, STEP), STEP)
            return (
                part[0, here].astype(F32)
                + self.land[1 + 2 * h, there].astype(F32)
                + self.land[4 + h, there].astype(F32)
            )

        def drain(self):
            for i in range(6):
                self.copy(i).wait_send()

    def by_rows(ref, size):
        def view(who):
            return ref.at[pl.ds(pl.multiple_of(who * size, size), size)]

        return view

    def by_cut(ref, size):
        def view(who):
            return ref.at[:, pl.ds(pl.multiple_of(who * size, size), size)]

        return view

    def peer(d):
        return 2 * ((z + d) % (n_f // 2)) + c

    def source(d):
        return 2 * ((z + n_f // 2 - d) % (n_f // 2)) + c

    partner = 2 * z + 1 - c
    far = range(1, n_f // 2)

    class Weight:
        def __init__(self, index, view):
            self.index, self.view = index, view

        def direct(self, d, who):
            return remote(
                self.view(who), self.view(who),
                w_send.at[self.index, d], w_recv.at[self.index, d], s, peer(d),
            )

        def across(self, d, who):
            return remote(
                self.view(who), self.view(who),
                p_send.at[self.index, d], p_recv.at[self.index, d], s, partner,
            )

        def start(self):
            for d in far:
                self.direct(d, f).start()
            self.across(0, f).start()

        def forward(self):
            for d in far:
                self.direct(d, source(d)).wait_recv()
                self.across(d, source(d)).start()

        def finish(self):
            self.across(0, partner).wait_recv()
            for d in far:
                who = source(d) + 1 - 2 * c
                self.across(d, who).wait_recv()

        def drain(self):
            for d in far:
                self.direct(d, f).wait_send()
                self.across(d, source(d)).wait_send()
            self.across(0, f).wait_send()

    class Shed:
        def __init__(self, index, gw, land_p, land_z):
            self.index, self.gw, self.land_p, self.land_z = index, gw, land_p, land_z

        def pair(self, to_z):
            return remote(
                self.gw.at[2 * to_z + 1 - c], self.land_p.at[to_z],
                gp_send.at[self.index, to_z], gp_recv.at[self.index, to_z], s, partner,
            )

        def along(self, d):
            return remote(
                self.gw.at[peer(d)], self.land_z.at[d - 1],
                gz_send.at[self.index, d], gz_recv.at[self.index, d], s, peer(d),
            )

        def add_pair(self, to_z):
            self.pair(to_z).wait_recv()
            who = 2 * to_z + c
            height = self.gw.shape[1]

            def add(j, _):
                at = pl.ds(pl.multiple_of(j * STEP, STEP), STEP)
                total = self.gw[who, at].astype(F32) + self.land_p[to_z, at].astype(F32)
                self.gw[who, at] = total.astype(BF16)
                return 0

            lax.fori_loop(0, height // STEP, add, 0)

        def middle(self):
            for d in far:
                self.add_pair((z + d) % (n_f // 2))
                self.along(d).start()
            self.add_pair(z)

        def wait(self):
            for d in far:
                self.along(d).wait_recv()

        def total(self, at):
            value = self.gw[f, at].astype(F32)
            for d in far:
                value = value + self.land_z[d - 1, at].astype(F32)
            return value

        def drain(self):
            def one(to_z, _):
                self.pair(to_z).wait_send()
                return 0

            lax.fori_loop(0, n_f // 2, one, 0)
            for d in far:
                self.along(d).wait_send()

    barrier = pltpu.get_barrier_semaphore()
    for who in (sx, sy, sd):
        pl.semaphore_signal(barrier, inc=1, device_id=(who, f), device_id_type=pl.DeviceIdType.MESH)
    n_peers = 3
    if inside:
        for d in range(1, n_f):
            pl.semaphore_signal(
                barrier, inc=1, device_id=(s, (f + d) % n_f), device_id_type=pl.DeviceIdType.MESH
            )
        n_peers += n_f - 1
    pl.semaphore_wait(barrier, n_peers)

    others = (sx, sy, sd)
    ag_tok = Gather(tok, 0)
    if inside:
        high = qkv_in.shape[0]
        high_d = down_in.shape[0]
        w_qkv = Weight(0, by_cut(qkv_w, high))
        w_out = Weight(1, by_rows(out_w.at[0], high))
        w_up = Weight(2, by_cut(up_w, high))
        w_down = Weight(3, by_rows(down_w, high_d))

        def qkv_copy(k, p, to):
            start = pl.multiple_of(p * width + to * group, 128)
            src = qkv_in.at[:, pl.ds(start, group)]
            dst = qkv_w.at[s, pl.ds(pl.multiple_of(f * high, high), high), pl.ds(p * group, group)]
            if k < 0:
                return pltpu.make_async_copy(src, dst, col_local.at[p])
            return remote(src, dst, col_send.at[k, p], col_recv.at[k, p], to, f)

        ff = up_w.shape[2]

        def up_copy(k, to):
            src = up_in.at[:, pl.ds(pl.multiple_of(to * ff, 128), ff)]
            dst = up_w.at[s, pl.ds(pl.multiple_of(f * high, high), high)]
            if k < 0:
                return pltpu.make_async_copy(src, dst, col_local.at[3])
            return remote(src, dst, upc_send.at[k], upc_recv.at[k], to, f)

        out_own = pltpu.make_async_copy(out_in, w_out.view(f), loc_sem.at[0])
        down_own = pltpu.make_async_copy(down_in, w_down.view(f), loc_sem.at[1])
        out_own.start()
        down_own.start()
        for p in range(3):
            for k, to in enumerate(others):
                qkv_copy(k, p, to).start()
            qkv_copy(-1, p, s).start()
    else:
        loads = [
            pltpu.make_async_copy(qkv_in, qkv_w, col_local.at[0]),
            pltpu.make_async_copy(up_in, up_w, col_local.at[3]),
            pltpu.make_async_copy(out_in, out_w, loc_sem.at[0]),
            pltpu.make_async_copy(down_in, down_w, loc_sem.at[1]),
        ]
        for load in loads:
            load.start()
    ag_tok.start(tokens)
    tok_own = pltpu.make_async_copy(tokens, tok.at[s], loc_sem.at[2])
    tok_own.start()
    cot_own = pltpu.make_async_copy(cot_in, cot, loc_sem.at[3])
    cot_own.start()
    seg_own = pltpu.make_async_copy(seg_in, segs.at[s], loc_sem.at[4])
    seg_own.start()

    def seg_copy(k, to):
        return remote(seg_in, segs.at[s], seg_send.at[k], seg_recv.at[k], to, f)

    for k, to in enumerate(others):
        seg_copy(k, to).start()

    if inside:
        small_f[f] = small_in[...]

        def small_copy(d):
            return remote(
                small_in, small_f.at[f], sf_send.at[d], sf_recv.at[d], s, (f + d) % n_f
            )

        for d in range(1, n_f):
            small_copy(d).start()
        out_own.wait()
        w_out.start()
        for p in range(3):
            qkv_copy(-1, p, s).wait()
            for k, to in enumerate(others):
                qkv_copy(k, p, to).wait_recv()
        w_qkv.start()
        for k, to in enumerate(others):
            up_copy(k, to).start()
        up_copy(-1, s).start()
        for d in range(1, n_f):
            remote(
                small_in, small_f.at[(f + n_f - d) % n_f], sf_send.at[d], sf_recv.at[d],
                s, (f + d) % n_f,
            ).wait_recv()
        per = n_f * high // 128
        each = n_f // per
        for t in range(per):
            value = small_f[t * each, 0:8]
            for e in range(1, each):
                value = value + small_f[t * each + e, 0:8]
            small_s[s, t] = value
        for e in range(n_f):
            bias_row[0:1, pl.ds(e * 128, 128)] = small_f[e, 8:9]

        def small_wide(k, to):
            return remote(small_s.at[s], small_s.at[s], ss_send.at[k], ss_recv.at[k], to, f)

        for k, to in enumerate(others):
            small_wide(k, to).start()
        for k, who in enumerate(others):
            remote(
                small_s.at[who], small_s.at[who], ss_send.at[k], ss_recv.at[k], who, f
            ).wait_recv()
        for b in range(4):
            for t in range(per):
                params[:, pl.ds((b * per + t) * 128, 128)] = small_s[b, t]
    else:
        params[...] = small_in[0:8]
        bias_row[...] = small_in[8:9, 0 : bias_row.shape[1]]

    def param(i):
        return params[i : i + 1, :]

    tok_own.wait()
    ag_tok.relay()

    def first_norm(b):
        def run(j, _):
            at = pl.ds(pl.multiple_of(j * STEP, STEP), STEP)
            unit, _s = unit_of(tok[b, at].astype(F32))
            normed[b, at] = (unit * param(0) + param(1)).astype(BF16)
            return 0

        lax.fori_loop(0, rows // STEP, run, 0)

    def norm_step(k, _):
        @pl.when(k == 1)
        def _():
            ag_tok.wait_x()

        @pl.when(k == 2)
        def _():
            ag_tok.wait_y()

        @pl.when(k == 3)
        def _():
            ag_tok.wait_d()

        first_norm(block(k))
        return 0

    lax.fori_loop(0, 4, norm_step, 0)
    if inside:
        w_qkv.forward()
        up_copy(-1, s).wait()
        for k, to in enumerate(others):
            up_copy(k, to).wait_recv()
        w_up.start()
        w_out.forward()
        w_qkv.finish()
    else:
        for load in loads:
            load.wait()

    def make_triple(b, _):
        value = dot(normed[b], qkv_w[...].reshape(width, 3 * group))
        triple[b, :, 0:group] = (value[:, 0:group] * 0.125).astype(BF16)
        triple[b, :, group : 3 * group] = value[:, group : 3 * group].astype(BF16)
        return 0

    lax.fori_loop(0, 4, make_triple, 0)
    if inside:
        w_out.finish()
        down_own.wait()
        w_down.start()

    seg_own.wait()
    for k, who in enumerate(others):
        remote(seg_in, segs.at[who], seg_send.at[k], seg_recv.at[k], who, f).wait_recv()
    seg_all = segs[...]

    def below(level):
        count = jnp.sum((seg_all < level).astype(F32), axis=0)
        return jnp.sum(count, axis=1, keepdims=True)

    bound_1, bound_2 = below(1), below(2)
    lane = lax.broadcasted_iota(jnp.int32, (1, 128), 1)
    left = (lane < HEAD_DIM).astype(F32)
    sides = (left.astype(BF16), (1.0 - left).astype(BF16))
    pick = lax.broadcasted_iota(jnp.int32, (rows, 128), 1) < HEAD_DIM
    blocks = window // rows

    def set_mask(r, first):
        i = (r * rows + lax.broadcasted_iota(jnp.int32, (rows, 128), 0)).astype(F32)
        start = jnp.where(i >= bound_2, bound_2, jnp.where(i >= bound_1, bound_1, 0.0))
        for t in range(window // 128):
            j = first * rows + t * 128 + lax.broadcasted_iota(jnp.int32, (rows, 128), 1)
            j = j.astype(F32)
            mask[:, t * 128 : (t + 1) * 128] = jnp.where((j <= i) & (j >= start), 0.0, NEG)

    def cut(r, part_at, p, count):
        at = pl.ds(part_at * group + p * 128, 128)
        return triple[pl.ds(r, count), :, at].reshape(count * rows, 128)

    rs_1 = Scatter(land_a, 0)

    def attend(i, _):
        rel = (1 - i // 2) + 2 * (1 - i % 2)
        r = block(rel)
        first = r // 3
        set_mask(r, first)
        for p in range(group // 128):
            query, keys, vals = cut(r, 0, p, 1), cut(first, 1, p, blocks), cut(first, 2, p, blocks)
            outs = []
            for e in range(2):
                scores = dot(query * sides[e], keys, NT) + mask[...]
                expo = jnp.exp(scores - jnp.max(scores, -1, keepdims=True))
                low = (expo * (1.0 / jnp.sum(expo, -1, keepdims=True))).astype(BF16)
                probs[r, 2 * p + e] = low
                outs.append(dot(low, vals))
            attended[r, :, p * 128 : (p + 1) * 128] = jnp.where(pick, outs[0], outs[1]).astype(BF16)
        part[rel] = dot(attended[r], out_w[0]).astype(BF16)
        rs_1.step(rel)
        return 0

    lax.fori_loop(0, 4, attend, 0)
    rs_1.relay()
    if inside:
        w_up.forward()
    rs_1.wait()

    def mid_norm(j, _):
        at = pl.ds(pl.multiple_of(j * STEP, STEP), STEP)
        value = rs_1.total(j)
        branch[at] = value
        unit, _s = unit_of(value)
        mid = tok[s, at].astype(F32) + (unit * param(2) + param(3))
        middle[at] = mid
        unit, _s = unit_of(mid)
        inner[s, at] = (unit * param(4) + param(5)).astype(BF16)
        return 0

    lax.fori_loop(0, rows // STEP, mid_norm, 0)
    ag_inner = Gather(inner, 1)
    ag_inner.start()
    rs_1.drain()
    if inside:
        w_up.finish()

    ff = up_w.shape[2]
    tile = 256
    rs_2 = Scatter(land_b, 1)

    def forward_step(k, _):
        ag_inner.step(k)
        r = block(k)

        def column(n, _):
            at = pl.ds(pl.multiple_of(n * tile, tile), tile)
            pre = dot(inner[r], up_w[:, :, at].reshape(width, tile)) + bias_row[:, at]
            square = pre * pre
            bend = jnp.tanh(0.7978845608028654 * pre * (1.0 + 0.044715 * square))
            near = 0.5 * (1.0 + bend)
            activ[r, :, at] = (pre * near).astype(BF16)
            slope = near + 0.5 * pre * (1.0 - bend * bend) * (
                0.7978845608028654 * (1.0 + 0.134145 * square)
            )
            dgelu[r, :, at] = slope.astype(BF16)
            return 0

        lax.fori_loop(0, ff // tile, column, 0)

        if inside:
            @pl.when(k == 0)
            def _():
                w_down.forward()
                w_down.finish()

        def column_b(n, _):
            at = pl.ds(pl.multiple_of(n * tile, tile), tile)
            part[k, :, at] = dot(activ[r], down_w[:, at]).astype(BF16)
            return 0

        lax.fori_loop(0, width // tile, column_b, 0)
        rs_2.step(k)
        return 0

    lax.fori_loop(0, 4, forward_step, 0)
    rs_2.relay()
    cot_own.wait()
    rs_2.wait()

    zero_row = jnp.zeros((1, width), F32)

    def last_norm(j, carry):
        at = pl.ds(pl.multiple_of(j * STEP, STEP), STEP)
        unit, scale = unit_of(rs_2.total(j))
        result[at] = (middle[at] + (unit * param(6) + param(7))).astype(BF16)
        grad = cot[at].astype(F32)
        gmix[s, at] = pull_of(grad, param(6), unit, scale).astype(BF16)
        return carry[0] + col_sum(grad * unit), carry[1] + col_sum(grad)

    grad_gain_d, grad_shift_d = lax.fori_loop(
        0, rows // STEP, last_norm, (zero_row, zero_row)
    )
    sg_rows = [None] * 8
    sg_rows[6], sg_rows[7] = grad_gain_d, grad_shift_d
    ag_mix = Gather(gmix, 2)
    ag_mix.start()
    rs_2.drain()

    rs_3 = Scatter(land_a, 2)
    sg_bias = bias_row

    def clear(n, _):
        at = pl.ds(pl.multiple_of(n * tile, tile), tile)
        sg_bias[:, at] = jnp.zeros((1, tile), F32)
        return 0

    lax.fori_loop(0, ff // tile, clear, 0)

    def back_step(k, _):
        ag_mix.step(k)
        r = block(k)

        def column(n, _):
            at = pl.ds(pl.multiple_of(n * tile, tile), tile)
            grad = dot(gmix[r], down_w[at], NT)
            low = (dgelu[r, :, at].astype(F32) * grad).astype(BF16)
            dgelu[r, :, at] = low
            sg_bias[:, at] = sg_bias[:, at] + col_sum(low.astype(F32))
            return 0

        lax.fori_loop(0, ff // tile, column, 0)

        def column_b(n, _):
            at = pl.ds(pl.multiple_of(n * tile, tile), tile)
            part[k, :, at] = dot(dgelu[r], up_w[n], NT).astype(BF16)
            return 0

        lax.fori_loop(0, width // tile, column_b, 0)
        rs_3.step(k)
        return 0

    lax.fori_loop(0, 4, back_step, 0)

    turned = tok

    def turn(source_ref, target):
        def run(b, _):
            def tiles(n, _):
                at = pl.ds(pl.multiple_of(n * tile, tile), tile)
                there = pl.ds(pl.multiple_of(b * rows, rows), rows)
                target[n, :, there] = source_ref[b, :, at].T
                return 0

            lax.fori_loop(0, target.shape[0], tiles, 0)
            return 0

        lax.fori_loop(0, 4, run, 0)

    def order(j):
        late = j // (n_f // 2)
        return 2 * (j % (n_f // 2)) + (1 - c) + late * (2 * c - 1)

    def cut_rows(who):
        at = pl.ds(pl.multiple_of(who * high, high), high)
        return turned[:, at, :].reshape(4 * high, 4 * rows)

    def plain_rows(who):
        per_block = rows // high_d
        at = pl.ds(pl.multiple_of((who % per_block) * high_d, high_d), high_d)
        return turned[who // per_block, at, :]

    def weight_grads(left_of, right, gw, shed):
        def run(j, _):
            who = order(j)
            value = dot(left_of(who), right[...].reshape(4 * rows, right.shape[2]))
            gw[who] = value.astype(BF16)

            @pl.when(j < n_f // 2)
            def _():
                shed.pair(j).start()

            return 0

        lax.fori_loop(0, n_f, run, 0)

    rs_3.relay()
    if inside:
        shed_down = Shed(0, gw_down, lp_down, lz_down)
        shed_up = Shed(1, gw_up, lp_up, lz_up)
        shed_out = Shed(2, gw_out, lp_out, lz_out)
        shed_qkv = Shed(3, gw_qkv, lp_qkv, lz_qkv)
        ag_tok.drain()
    rs_3.wait()

    def mid_back(j, carry):
        at = pl.ds(pl.multiple_of(j * STEP, STEP), STEP)
        grad = rs_3.total(j)
        unit, scale = unit_of(middle[at])
        total = cot[at].astype(F32) + pull_of(grad, param(4), unit, scale)
        gmid[at] = total
        out = [carry[0] + col_sum(grad * unit), carry[1] + col_sum(grad)]
        unit, scale = unit_of(branch[at])
        gbr[s, at] = pull_of(total, param(2), unit, scale).astype(BF16)
        return out[0], out[1], carry[2] + col_sum(total * unit), carry[3] + col_sum(total)

    sg_rows[4], sg_rows[5], sg_rows[2], sg_rows[3] = lax.fori_loop(
        0, rows // STEP, mid_back, (zero_row,) * 4
    )
    ag_br = Gather(gbr, 3)
    ag_br.start()
    tok_again = pltpu.make_async_copy(tokens, cot, loc_sem.at[5])
    tok_again.start()
    rs_3.drain()
    if inside:
        turn(activ, turned)
        weight_grads(plain_rows, gmix, gw_down, shed_down)
    ag_br.relay()
    if inside:
        shed_down.middle()
        turn(inner, turned)
        weight_grads(cut_rows, dgelu, gw_up, shed_up)
        shed_up.middle()
    ag_br.wait_x()
    ag_br.wait_y()
    ag_br.wait_d()

    def zero_acc(j, _):
        at = pl.ds(pl.multiple_of(j * STEP, STEP), STEP)
        dkt[at] = jnp.zeros((STEP, 4 * rows), F32)
        dvt[at] = jnp.zeros((STEP, 4 * rows), F32)
        return 0

    lax.fori_loop(0, group // STEP, zero_acc, 0)

    def attend_back(r, _):
        first = r // 3
        gatt[...] = dot(gbr[r], out_w[0], NT).astype(BF16)
        span = pl.ds(pl.multiple_of(first * rows, rows), window)
        for p in range(group // 128):
            query, keys, vals = cut(r, 0, p, 1), cut(first, 1, p, blocks), cut(first, 2, p, blocks)
            grad = gatt[:, p * 128 : (p + 1) * 128]
            query_t = query.T
            grad_t = grad.T
            outs = []
            for e in range(2):
                low = probs[r, 2 * p + e]
                grad_probs = dot(grad * sides[e], vals, NT)
                full = low.astype(F32)
                inner_sum = jnp.sum(full * grad_probs, -1, keepdims=True)
                grad_scores = (full * (grad_probs - inner_sum)).astype(BF16)
                outs.append(dot(grad_scores, keys))
                here = slice((2 * p + e) * HEAD_DIM, (2 * p + e + 1) * HEAD_DIM)
                side = slice(e * HEAD_DIM, (e + 1) * HEAD_DIM)
                dkt[here, span] = dkt[here, span] + dot(query_t[side], grad_scores)
                dvt[here, span] = dvt[here, span] + dot(grad_t[side], low)
            gtri[r, :, p * 128 : (p + 1) * 128] = (
                jnp.where(pick, outs[0], outs[1]) * 0.125
            ).astype(BF16)
        return 0

    lax.fori_loop(0, 4, attend_back, 0)

    def turn_back(b, _):
        at = pl.ds(pl.multiple_of(b * rows, rows), rows)
        gtri[b, :, group : 2 * group] = dkt[:, at].astype(BF16).T
        gtri[b, :, 2 * group : 3 * group] = dvt[:, at].astype(BF16).T
        return 0

    lax.fori_loop(0, 4, turn_back, 0)

    rs_4 = Scatter(land_b, 3)

    def normed_step(i, _):
        rel = (1 - i // 2) + 2 * (1 - i % 2)
        r = block(rel)
        part[rel] = dot(gtri[r], qkv_w[...].reshape(width, 3 * group), NT).astype(BF16)
        rs_4.step(rel)
        return 0

    lax.fori_loop(0, 4, normed_step, 0)
    if inside:
        turn(attended, att_t)
        gw_out[...] = (
            dot(att_t[0], gbr[...].reshape(4 * rows, width)).astype(BF16).reshape(gw_out.shape)
        )

        def out_pairs(j, _):
            shed_out.pair(j).start()
            return 0

        lax.fori_loop(0, n_f // 2, out_pairs, 0)
        turn(normed, turned)
        weight_grads(cut_rows, gtri, gw_qkv, shed_qkv)
    rs_4.relay()
    if inside:
        shed_out.middle()
        shed_qkv.middle()
    rs_4.wait()

    def first_back(j, carry):
        at = pl.ds(pl.multiple_of(j * STEP, STEP), STEP)
        grad = rs_4.total(j)
        value = cot[at].astype(F32)
        unit, scale = unit_of(value)
        tgrad[at] = gmid[at] + pull_of(grad, param(0), unit, scale)
        return carry[0] + col_sum(grad * unit), carry[1] + col_sum(grad)

    tok_again.wait()
    sg_rows[0], sg_rows[1] = lax.fori_loop(0, rows // STEP, first_back, (zero_row, zero_row))

    if inside:
        per = n_f * high // 128
        for b in range(4):
            for t in range(per):
                at = slice((b * per + t) * 128, (b * per + t + 1) * 128)
                for i in range(8):
                    sg_s[b, t, i : i + 1, :] = sg_rows[i][:, at]

        def ts_copy(k, to):
            return remote(sg_s.at[to], sg_land_s.at[k], ts_send.at[k], ts_recv.at[k], to, f)

        for k, to in enumerate(others):
            ts_copy(k, to).start()

        shed_down.wait()
        for j in range(high_d // STEP):
            at = pl.ds(j * STEP, STEP)
            gdown[at] = shed_down.total(at)
        shed_up.wait()

        def up_total(b, _):
            at = pl.ds(pl.multiple_of(b * high, high), high)
            fin_up[b] = shed_up.total(at)
            return 0

        lax.fori_loop(0, 4, up_total, 0)

        def gu_copy(k, to):
            dst = gup.at[:, pl.ds(pl.multiple_of(s * ff, 128), ff)]
            return remote(fin_up.at[to], dst, gu_send.at[k], gu_recv.at[k], to, f)

        for k, to in enumerate(others):
            gu_copy(k, to).start()
        gup[:, pl.ds(pl.multiple_of(s * ff, 128), ff)] = fin_up[s]

        for k, to in enumerate(others):
            ts_copy(k, to).wait_recv()
        for who in range(n_f):
            t = who * high // 128
            sg_f[who, 0:8] = (
                sg_s[s, t] + sg_land_s[0, t] + sg_land_s[1, t] + sg_land_s[2, t]
            )
            sg_f[who, 8:9] = sg_bias[:, who * 128 : (who + 1) * 128]

        def tf_copy(d):
            to = (f + d) % n_f
            return remote(
                sg_f.at[to], sg_land_f.at[d - 1], tf_send.at[d], tf_recv.at[d], s, to
            )

        for d in range(1, n_f):
            tf_copy(d).start()

        shed_out.wait()
        gout[...] = shed_out.total(slice(None))
        shed_qkv.wait()

        def qkv_total(b, _):
            at = pl.ds(pl.multiple_of(b * high, high), high)
            fin_qkv[b] = shed_qkv.total(at)
            return 0

        lax.fori_loop(0, 4, qkv_total, 0)

        def gc_copy(k, p, to):
            dst = gqkv.at[:, pl.ds(pl.multiple_of(p * width + s * group, 128), group)]
            return remote(
                fin_qkv.at[to, :, pl.ds(p * group, group)], dst,
                gc_send.at[k, p], gc_recv.at[k, p], to, f,
            )

        for p in range(3):
            for k, to in enumerate(others):
                gc_copy(k, p, to).start()
            at = pl.ds(pl.multiple_of(p * width + s * group, 128), group)
            gqkv[:, at] = fin_qkv[s, :, p * group : (p + 1) * group]
        for d in range(1, n_f):
            tf_copy(d).wait_recv()
        value = sg_f[f]
        for d in range(1, n_f):
            value = value + sg_land_f[d - 1]
        gsmall[...] = value

        for k, who in enumerate(others):
            remote(
                fin_up.at[0], gup.at[:, pl.ds(pl.multiple_of(who * ff, 128), ff)],
                gu_send.at[k], gu_recv.at[k], who, f,
            ).wait_recv()
            for p in range(3):
                remote(
                    fin_qkv.at[0, :, pl.ds(p * group, group)],
                    gqkv.at[:, pl.ds(pl.multiple_of(p * width + who * group, 128), group)],
                    gc_send.at[k, p], gc_recv.at[k, p], who, f,
                ).wait_recv()
        for k, to in enumerate(others):
            gu_copy(k, to).wait_send()
            ts_copy(k, to).wait_send()
            for p in range(3):
                gc_copy(k, p, to).wait_send()
                qkv_copy(k, p, to).wait_send()
            up_copy(k, to).wait_send()
            small_wide(k, to).wait_send()
        for d in range(1, n_f):
            tf_copy(d).wait_send()
            small_copy(d).wait_send()
        for weight in (w_qkv, w_out, w_up, w_down):
            weight.drain()
        for shed in (shed_down, shed_up, shed_out, shed_qkv):
            shed.drain()
    else:
        for i in range(8):
            gsmall[i : i + 1, :] = sg_rows[i]
        gsmall[8:9, 0:ff] = sg_bias[...]
    for k, to in enumerate(others):
        seg_copy(k, to).wait_send()
    for gather in (ag_inner, ag_mix, ag_br) + (() if inside else (ag_tok,)):
        gather.drain()
    rs_4.drain()


def on_device(n_seq, n_f, *args):
    (tokens, segments, qkv_weight, out_weight, up_weight, up_bias, down_weight) = args[:7]
    vectors, cotangent = args[7:15], args[15]
    rows, width = tokens.shape[1:]
    high, high_d = qkv_weight.shape[0], down_weight.shape[0]
    length = n_seq * rows
    group = qkv_weight.shape[1] // 3 // n_seq
    heads = group // HEAD_DIM
    ff = up_weight.shape[1] // n_seq
    half = rows // 2
    window = rows * min(n_seq, 1 + -(-511 // rows))
    inside = n_f == 8 and high % 32 == 0
    f = lax.axis_index("fsdp")
    small = jnp.stack([v.astype(F32) for v in vectors])
    if inside:
        each = 128 // high
        lane = lax.broadcasted_iota(jnp.int32, (8, 128), 1) // high
        small = jnp.where(lane == f % each, jnp.tile(small, (1, each)), 0.0)
        small = jnp.concatenate([small, up_bias.astype(F32)[None], jnp.zeros((7, 128), F32)])
        weights = (qkv_weight, out_weight, up_weight, down_weight)
    else:
        small = lax.all_gather(small, ("seq", "fsdp"), axis=1, tiled=True)
        bias = lax.all_gather(up_bias.astype(F32), "fsdp", axis=0, tiled=True)
        bias = jnp.pad(bias[None], ((0, 7), (0, width - ff)))
        small = jnp.concatenate([small, bias])

        def columns(weight, parts):
            cut = weight.reshape(high, parts, n_seq, -1).transpose(2, 0, 1, 3)
            cut = cut.reshape(n_seq, high, -1)
            cut = lax.all_to_all(cut, "seq", split_axis=0, concat_axis=0, tiled=True)
            return lax.all_gather(cut, "fsdp", axis=1, tiled=True)

        weights = (
            columns(qkv_weight, 3),
            lax.all_gather(out_weight, "fsdp", axis=0, tiled=True)[None],
            columns(up_weight, 1),
            lax.all_gather(down_weight, "fsdp", axis=0, tiled=True),
        )
    vmem, anywhere, dma = pltpu.VMEM, pl.BlockSpec(memory_space=pl.ANY), pltpu.SemaphoreType.DMA
    whole = pl.BlockSpec(memory_space=pltpu.VMEM)
    full = (4, rows, width)
    saved = {
        "normed": (full, BF16), "inner": (full, BF16), "gmix": (full, BF16), "gbr": (full, BF16),
        "attended": ((4, rows, group), BF16), "activ": ((4, rows, ff), BF16),
        "dgelu": ((4, rows, ff), BF16), "gtri": ((4, rows, 3 * group), BF16),
    }
    pieces = {"qkv": (n_seq * high, 3 * group), "out": (high, width),
              "up": (n_seq * high, ff), "down": (high_d, width)}
    scratch = {
        "tok": vmem(full, BF16), "normed": None, "inner": None, "gmix": None, "gbr": None,
        "qkv_w": vmem((n_seq, rows, 3 * group), BF16), "out_w": vmem((1, group, width), BF16),
        "up_w": vmem((n_seq, rows, ff), BF16), "down_w": vmem((ff, width), BF16),
        "segs": vmem((4, 1, rows), jnp.int32),
        "small_f": vmem((n_f if inside else 1, 16, 128), F32), "small_s": vmem((4, width // 512, 8, 128), F32),
        "params": vmem((8, width), F32), "bias_row": vmem((1, ff), F32),
        "triple": vmem((4, rows, 3 * group), BF16), "probs": vmem((4, heads, rows, window), BF16),
        "attended": None, "mask": vmem((rows, window), F32), "activ": None, "dgelu": None,
        "part": vmem(full, BF16), "land_a": vmem((6, half, width), BF16),
        "land_b": vmem((6, half, width), BF16),
        "branch": vmem((rows, width), F32), "middle": vmem((rows, width), F32),
        "gmid": vmem((rows, width), F32), "cot": vmem((rows, width), BF16),
        "gtri": None, "gatt": vmem((rows, group), BF16), "dkt": vmem((group, length), F32),
        "dvt": vmem((group, length), F32), "att_t": vmem((1, group, length), BF16),
    }
    for name, (tall, wide) in pieces.items():
        scratch["gw_" + name] = vmem((n_f if inside else 1, tall if inside else 16, wide), BF16)
    for name, (tall, wide) in pieces.items():
        scratch["lp_" + name] = vmem((n_f // 2 if inside else 1, tall if inside else 16, wide), BF16)
    for name, (tall, wide) in pieces.items():
        scratch["lz_" + name] = vmem((n_f // 2 - 1 if inside else 1, tall if inside else 16, wide), BF16)
    scratch["fin_qkv"] = vmem((4, high, 3 * group), F32)
    scratch["fin_up"] = vmem((4, high, ff), F32)
    tiles = width // 512
    scratch["sg_s"] = vmem((4, tiles, 8, 128), F32)
    scratch["sg_land_s"] = vmem((3, tiles, 8, 128), F32)
    scratch["sg_f"] = vmem((n_f if inside else 1, 16, 128), F32)
    scratch["sg_land_f"] = vmem((n_f - 1 if inside else 1, 16, 128), F32)
    for name, shape in (
        ("ag_send", (4, 6)), ("ag_recv", (4, 6)), ("rs_send", (4, 6)), ("rs_recv", (4, 6)),
        ("w_send", (4, 4)), ("w_recv", (4, 4)), ("p_send", (4, 4)), ("p_recv", (4, 4)),
        ("col_send", (3, 3)), ("col_recv", (3, 3)), ("col_local", (4,)),
        ("upc_send", (3,)), ("upc_recv", (3,)), ("seg_send", (3,)), ("seg_recv", (3,)),
        ("sf_send", (8,)), ("sf_recv", (8,)), ("ss_send", (3,)), ("ss_recv", (3,)),
        ("loc_sem", (6,)),
        ("gp_send", (4, 4)), ("gp_recv", (4, 4)), ("gz_send", (4, 4)), ("gz_recv", (4, 4)),
        ("gc_send", (3, 3)), ("gc_recv", (3, 3)), ("gu_send", (3,)), ("gu_recv", (3,)),
        ("ts_send", (3,)), ("ts_recv", (3,)), ("tf_send", (8,)), ("tf_recv", (8,)),
    ):
        scratch[name] = dma(shape)
    outs = {
        "result": ((rows, width), BF16), "tgrad": ((rows, width), F32),
        "gqkv": ((high, n_seq * 3 * group), F32), "gout": ((high, width), F32),
        "gup": ((high, n_seq * ff), F32), "gdown": ((high_d, width), F32),
        "gsmall": ((16, 128 if inside else width), F32),
    }
    if inside:
        for name, shape in saved.items():
            scratch[name] = vmem(*shape)
        extra = []
    else:
        extra = list(saved)
    names = list(scratch)

    def kernel(*refs):
        given = refs[:8]
        made = refs[8 : 8 + len(outs)]
        more = dict(zip(extra, refs[8 + len(outs) :]))
        rest = refs[8 + len(outs) + len(extra) :]
        more.update(zip([n for n in names if scratch[n] is not None], rest))
        layer_kernel(inside, n_f, *given, *made, *[more[n] for n in names])

    shapes = [*outs.values(), *[saved[n] for n in extra]]
    made = pl.pallas_call(
        kernel,
        out_shape=[jax.ShapeDtypeStruct(*shape) for shape in shapes],
        in_specs=[anywhere, anywhere, whole, anywhere] + [anywhere] * 4,
        out_specs=[whole] * len(shapes),
        scratch_shapes=[scratch[n] for n in names if scratch[n] is not None],
        compiler_params=pltpu.CompilerParams(
            collective_id=0, has_side_effects=True, vmem_limit_bytes=67043328
        ),
    )(tokens[0], segments, small, cotangent[0], *weights)
    result, tgrad, gqkv, gout, gup, gdown, gsmall = made[:7]
    if inside:
        start = (f % (128 // high)) * high
        vectors = lax.dynamic_slice(gsmall[:8], (0, start), (8, high))
        gbias = gsmall[8]
    else:
        kept = {n: v.reshape(length, -1) for n, v in zip(extra, made[7:])}

        def turned_dot(left, right):
            return lax.dot_general(
                kept[left], kept[right], (((0,), (0,)), ((), ())), preferred_element_type=F32
            ).astype(BF16)

        def shed(value):
            return lax.psum_scatter(value, "fsdp", scatter_dimension=0, tiled=True)

        def columns_back(value, parts):
            cut = value.reshape(n_seq, n_f, high, -1).transpose(1, 0, 2, 3)
            cut = lax.all_to_all(shed(cut)[0], "seq", split_axis=0, concat_axis=0, tiled=True)
            cut = cut.reshape(n_seq, high, parts, -1).transpose(1, 2, 0, 3)
            return cut.reshape(high, -1).astype(F32)

        gqkv = columns_back(turned_dot("normed", "gtri"), 3)
        gout = shed(turned_dot("attended", "gbr")).astype(F32)
        gup = columns_back(turned_dot("inner", "dgelu"), 1)
        gdown = shed(turned_dot("activ", "gmix")).astype(F32)
        vectors = lax.psum_scatter(gsmall[:8], ("seq", "fsdp"), scatter_dimension=1, tiled=True)
        gbias = shed(gsmall[8, :ff])
    return (result[None], tgrad[None], gqkv, gout, gup, gbias, gdown, *vectors)


def solution(mesh):
    rows = P(("seq", "fsdp"), None)
    vector = P(("seq", "fsdp"))
    acts = P("fsdp", "seq", None)
    return jax.shard_map(
        partial(on_device, mesh.shape["seq"], mesh.shape["fsdp"]),
        mesh=mesh,
        in_specs=(acts, P("fsdp", "seq"), rows, rows, rows, vector, rows, *(vector,) * 8, acts),
        out_specs=(acts, acts, rows, rows, rows, vector, rows, *(vector,) * 8),
        check_vma=False,
    )
```

time: 802 us -> 245 us (0.31); the launches traced: 793 us -> 245 us
  waiting for transfers between devices: 493 us -> 0 us
  Pallas kernels: 0 us -> 232 us
  blocking collectives: 108 us -> 0 us
  matrix products: 102 us -> 0 us
  other arithmetic: 41.7 us -> 0.69 us
  between operations: 15.5 us -> 0.76 us
  local copies, waits for them, and re-layouts: 23.2 us -> 10.9 us
  starting transfers between devices: 9.14 us -> 0 us
    pallas_call x0 -> x1, Pallas kernels: none -> 232 us  [on_device(): pl.pallas_call(kernel, out_shape=[jax.ShapeDtypeStruct(*shape) for shape...]
    reduce_scatter x7 -> x0, waiting for transfers between devices: 206 us -> none  [the longest x4 129 us: sum_rows(): lax.psum_scatter(value.astype(BF16), 'seq', scatter_dimension=0, tiled=True)]
    all_gather x7 -> x0, waiting for transfers between devices: 144 us -> none  [the longest x4 108 us: spread_rows(): return lax.all_gather(value, 'seq', axis=0, tiled=True)]
    unnamed x18 -> x0, waiting for transfers between devices: 143 us -> none
    dot_general x17 -> x0, matrix products: 91.7 us -> none  [the longest x12 58.7 us: dot(): lax.dot_general(left, right, (dims, ((), ())), preferred_element_type=F32)]
    all_gather x4 -> x0, blocking collectives: 75.1 us -> none  [the longest x1 40.2 us: on_device(): lax.all_gather(small, ('seq', 'fsdp'), axis=1, tiled=True).astype(F32)]
    convert_element_type x10 -> x0, other arithmetic: 19.6 us -> none  [the longest x1 7.95 us: pull(): grad_scores = (probs * (grad_probs - inner_sum)).astype(BF16)]
    reduce_sum x13 -> x0, other arithmetic: 19.1 us -> none  [the longest x4 8.43 us: norm_pull(): jnp.sum(grad * unit, 0)]
  transfers between devices with their start and end apart: 18 -> 0, of which waited for: 15 -> 0; matrix products, arithmetic and copies ran while one was open for 12% -> 0% of each run, Pallas kernels for 0% -> 0%
where the time goes in v2:
time: 245 us
  Pallas kernels  232 us (95%)
  local copies, waits for them, and re-layouts  10.9 us (4%)
    pallas_call x1, Pallas kernels, on_device(): pl.pallas_call(kernel, out_shape=[jax.ShapeDtypeStruct(*shape) for shape...  232 us
    unnamed x34, local copies, waits for them, and re-layouts  8.13 us

profile of v2, /device:TPU:0, one launch (start us, length us, event | category | flops | bytes accessed | tf_op | source)
XLA Modules:
  0.0 244.7 jit_solution(3038919486384430608)
XLA Ops:
  0.7 0.0 copy-start.13
  0.7 0.6 copy-done.13
  1.3 0.1 pad.2.clone
  1.4 0.0 copy-start.12
  1.4 0.0 copy-start.8
  1.4 0.0 copy-start.9
  1.4 0.0 copy-start.10
  1.5 0.0 copy-start.11
  1.5 0.0 copy-start.5
  1.5 0.0 copy-start.6
  1.5 0.0 copy-start.7
  1.5 0.6 copy-done.12
  2.1 0.0 copy-done.8
  2.1 0.0 copy-done.9
  2.1 0.0 copy-done.10
  2.1 0.0 copy-done.11
  2.1 0.0 copy-done.5
  2.1 0.0 copy-done.6
  2.2 0.0 copy-done.7
  2.2 0.1 tile.10
  2.3 0.7 maximum_maximum_fusion.refs_2_
  3.0 232.4 %shard_map.271 = (bf16[256,1024]{1,0:T(8,128)(2,1)}, f32[256,1024]{1,0:T(8,128)}, f32[32,3072]{1,0:T(8,128)}, f32[32,1024]{1,0:T(8,128)}, f32[32,4096]{1,0:T(8,1...) custom-call(bf16[256,1024]{1,0:T(8,128)(2,1)} %bitcast.34, s32[1,256]{1,0:T(1,128)} %refs_1_.1, ...), custom_call_target="tpu_custom_call" | custom-call | tf_op jit(solution)/shard_map/pallas_call | solution.py:1067
  235.4 0.0 copy-start
  235.4 1.3 slice_bitcast_fusion.8
  236.7 0.7 slice.7
  237.3 0.1 constant_dynamic-slice_fusion
  237.4 0.5 slice_bitcast_fusion
  238.0 1.9 copy.37
  239.8 0.0 copy-done
  239.8 0.0 copy-start.3
  239.8 1.0 copy.38
  240.8 0.3 copy-done.3
  241.1 0.0 copy-start.4
  241.1 0.0 copy-start.2
  241.1 0.7 copy.39
  241.8 0.2 copy-done.4
  242.1 0.7 copy.40
  242.7 0.0 copy-done.2
  242.7 0.0 copy-start.1
  242.7 0.8 copy.41
  243.5 0.4 copy-done.1
  243.9 0.8 copy.42
  (7 shorter events, 0.1 us)
Async XLA Ops:
  0.7 0.7 copy-start.13
  1.4 0.7 copy-start.12
  1.4 0.7 copy-start.8
  1.4 0.7 copy-start.9
  1.4 0.7 copy-start.10
  1.5 0.7 copy-start.11
  1.5 0.7 copy-start.5
  1.5 0.7 copy-start.6
  1.5 0.7 copy-start.7
  235.4 4.4 %copy-start = (f32[256,1024]{1,0:T(8,128)S(1)}, f32[256,1024]{1,0:T(8,128)}, u32[]{:S(2)}) copy-start(f32[256,1024]{1,0:T(8,128)} %get-tuple-element.23) | copy-start | bytes 3145732
  239.8 1.2 copy-start.3
  241.1 1.0 copy-start.4
  241.1 1.7 copy-start.2
  242.7 1.2 copy-start.1

commit v3 on v2

v3 whole, which is shorter than its diff:
```python
from functools import partial

import jax
import jax.numpy as jnp
from jax import lax
from jax.experimental import pallas as pl
from jax.experimental.pallas import tpu as pltpu
from jax.sharding import PartitionSpec as P

HEAD_DIM = 64
F32 = jnp.float32
BF16 = jnp.bfloat16
NN = ((1,), (0,))
NT = ((1,), (1,))
NEG = -1e30


def dot(left, right, dims=NN):
    return lax.dot_general(left, right, (dims, ((), ())), preferred_element_type=F32)


def unit_of(value):
    center = value - jnp.mean(value, -1, keepdims=True)
    scale = lax.rsqrt(jnp.mean(center * center, -1, keepdims=True) + 1e-05)
    return center * scale, scale


def pull_of(grad, gain, unit, scale):
    pulled = grad * gain
    first = jnp.mean(pulled, -1, keepdims=True)
    second = jnp.mean(pulled * unit, -1, keepdims=True)
    return scale * (pulled - first - unit * second)


def col_sum(value):
    return jnp.sum(value, 0, keepdims=True)


def layer_kernel(
    inside,
    n_f,
    tokens, seg_in, small_in, cot_in, qkv_in, out_in, up_in, down_in,
    result, tgrad, gqkv, gout, gup, gdown, gsmall,
    tok, normed, inner, gmix, gbr,
    qkv_w, out_w, up_w, down_w,
    segs, small_f, small_s, params, bias_row,
    triple, probs, attended, starts, activ, dgelu,
    part, land_a, land_b,
    branch, middle, gmid, cot,
    gtri, gatt, dkt, dvt,
    gw_q0, gw_q1, gw_out, gw_up, gw_down,
    lp_q0, lp_q1, lp_out, lp_up, lp_down,
    lz_q0, lz_q1, lz_out, lz_up, lz_down,
    result_v, fin_qkv, fin_up, fin_down, fin_out, gup_v, gqkv_v, small_sum,
    sg_s, sg_land_s, sg_f, sg_land_f,
    ag_send, ag_recv, rs_send, rs_recv,
    w_send, w_recv, p_send, p_recv,
    col_send, col_recv, col_local, upc_send, upc_recv,
    seg_send, seg_recv, sf_send, sf_recv, ss_send, ss_recv,
    loc_sem, o_sem,
    gp_send, gp_recv, gz_send, gz_recv,
    gc_send, gc_recv, gu_send, gu_recv,
    ts_send, ts_recv, tf_send, tf_recv,
):
    gw_qkv, lp_qkv, lz_qkv = (gw_q0, gw_q1), (lp_q0, lp_q1), (lz_q0, lz_q1)
    rows, width = tokens.shape
    half = rows // 2
    group = out_w.shape[1]
    pairs = group // 128
    window = probs.shape[3]
    s = lax.axis_index("seq")
    f = lax.axis_index("fsdp")
    x, y = s % 2, s // 2
    z, c = f // 2, f % 2

    def block(rel):
        return 2 * ((y + rel // 2) % 2) + (x + rel % 2) % 2

    sx, sy, sd = block(1), block(2), block(3)

    def remote(src, dst, send, recv, to_s, to_f):
        return pltpu.make_async_remote_copy(
            src_ref=src, dst_ref=dst, send_sem=send, recv_sem=recv,
            device_id=(to_s, to_f), device_id_type=pl.DeviceIdType.MESH,
        )

    class Gather:
        def __init__(self, full, index):
            self.full, self.index = full, index

        def piece(self, b, h):
            return self.full.at[b, pl.ds(h * half, half)]

        def copy(self, i, b, h, to, src=None):
            dst = self.piece(b, h)
            return remote(
                dst if src is None else src, dst,
                ag_send.at[self.index, i], ag_recv.at[self.index, i], to, f,
            )

        def start(self, src=None):
            def cut(h):
                return None if src is None else src.at[pl.ds(h * half, half)]

            self.copy(0, s, 0, sx, cut(0)).start()
            self.copy(1, s, 1, sy, cut(1)).start()
            self.copy(2, s, 1, sx, cut(1)).start()
            self.copy(3, s, 0, sy, cut(0)).start()

        def relay(self):
            self.copy(0, sx, 0, sx).wait_recv()
            self.copy(4, sx, 0, sy).start()
            self.copy(1, sy, 1, sy).wait_recv()
            self.copy(5, sy, 1, sx).start()

        def wait_x(self):
            self.copy(2, sx, 1, sx).wait_recv()

        def wait_y(self):
            self.copy(3, sy, 0, sy).wait_recv()

        def wait_d(self):
            self.copy(4, sd, 0, sy).wait_recv()
            self.copy(5, sd, 1, sx).wait_recv()

        def step(self, k):
            @pl.when(k == 1)
            def _():
                self.relay()
                self.wait_x()

            @pl.when(k == 2)
            def _():
                self.wait_y()

            @pl.when(k == 3)
            def _():
                self.wait_d()

        def drain(self):
            for i, (b, h, to) in enumerate(
                ((s, 0, sx), (s, 1, sy), (s, 1, sx), (s, 0, sy), (sx, 0, sy), (sy, 1, sx))
            ):
                self.copy(i, b, h, to).wait_send()

    def half_rows(h):
        return pl.ds(pl.multiple_of(h * half, half), half)

    class Scatter:
        plan = ((3, 0, 1), (1, 0, 1), (3, 1, 2), (2, 1, 2), (2, 0, 2), (1, 1, 1))

        def __init__(self, land, index):
            self.land, self.index = land, index

        def copy(self, i):
            rel, h, way = self.plan[i]
            return remote(
                part.at[rel, pl.ds(h * half, half)], self.land.at[i],
                rs_send.at[self.index, i], rs_recv.at[self.index, i],
                sx if way == 1 else sy, f,
            )

        def step(self, rel):
            @pl.when(rel == 3)
            def _():
                self.copy(0).start()
                self.copy(2).start()

            @pl.when(rel == 1)
            def _():
                self.copy(1).start()

            @pl.when(rel == 2)
            def _():
                self.copy(3).start()

        def relay(self):
            for arrived, i in ((0, 4), (2, 5)):
                self.copy(arrived).wait_recv()
                rel, h, _ = self.plan[i]

                here = pl.ds(h * half, half)
                total = part[rel, here].astype(F32) + self.land[arrived].astype(F32)
                part[rel, here] = total.astype(BF16)
                self.copy(i).start()

        def wait(self):
            for i in (1, 3, 4, 5):
                self.copy(i).wait_recv()

        def total(self, h):
            return (
                part[0, half_rows(h)].astype(F32)
                + self.land[1 + 2 * h].astype(F32)
                + self.land[4 + h].astype(F32)
            )

        def drain(self):
            for i in range(6):
                self.copy(i).wait_send()

    def by_rows(ref, size):
        def view(who):
            return ref.at[pl.ds(pl.multiple_of(who * size, size), size)]

        return view

    def by_cut(ref, size):
        def view(who):
            return ref.at[:, pl.ds(pl.multiple_of(who * size, size), size)]

        return view

    partner = 2 * z + 1 - c
    side = z // 2
    near = 4 * side + 1 - z
    mid_o, end_o = 2 - side, 3 - 3 * side
    is_mid = (z + side) % 2
    seen_as = 2 - is_mid
    owners = (near, mid_o, end_o)

    class Weight:
        def __init__(self, index, view):
            self.index, self.view = index, view

        def piece(self, to_z, i, k, owner_z, own=None):
            dst = self.view(2 * owner_z + c)
            return remote(
                dst if own is None else own, dst,
                w_send.at[self.index, i], w_recv.at[self.index, k], s, 2 * to_z + c,
            )

        def across(self, k, owner, own=None):
            dst = self.view(owner)
            return remote(
                dst if own is None else own, dst,
                p_send.at[self.index, k], p_recv.at[self.index, k], s, partner,
            )

        def start_far(self, own=None):
            self.piece(mid_o, 1, seen_as, z, own).start()

            @pl.when(is_mid == 0)
            def _():
                self.piece(near, 0, 0, z, own).start()

            self.across(3, f, own).start()

        def start_near(self, own=None):
            @pl.when(is_mid == 1)
            def _():
                self.piece(near, 0, 0, z, own).start()

        def start(self, own=None):
            self.start_far(own)
            self.start_near(own)

        def relay(self):
            @pl.when(is_mid == 1)
            def _():
                for k in (1, 2):
                    self.piece(z, 0, k, owners[k]).wait_recv()
                    self.piece(near, 1 + k, k, owners[k]).start()
                for k in (1, 2):
                    self.across(k, 2 * owners[k] + c).start()

        def rest(self):
            self.piece(z, 0, 0, near).wait_recv()
            self.across(0, 2 * near + c).start()

            @pl.when(is_mid == 0)
            def _():
                for k in (1, 2):
                    self.piece(z, 0, k, owners[k]).wait_recv()
                    self.across(k, 2 * owners[k] + c).start()

        def finish(self):
            self.across(3, partner).wait_recv()
            for k in (0, 1, 2):
                self.across(k, 2 * owners[k] + 1 - c).wait_recv()

        def drain(self):
            self.piece(mid_o, 1, seen_as, z).wait_send()
            self.piece(near, 0, 0, z).wait_send()
            self.across(3, f).wait_send()

            @pl.when(is_mid == 1)
            def _():
                for k in (1, 2):
                    self.piece(near, 1 + k, k, owners[k]).wait_send()

            for k in (0, 1, 2):
                self.across(k, 2 * owners[k] + c).wait_send()

    class Shed:
        def __init__(self, index, gw, land_p, land_z):
            self.index, self.gw, self.land_p, self.land_z = index, gw, land_p, land_z

        def pair(self, to_z):
            return remote(
                self.gw.at[2 * to_z + 1 - c], self.land_p.at[to_z],
                gp_send.at[self.index, to_z], gp_recv.at[self.index, to_z], s, partner,
            )

        def along(self, i, to_z, of_z, slot):
            return remote(
                self.gw.at[2 * of_z + c], self.land_z.at[slot],
                gz_send.at[self.index, i], gz_recv.at[self.index, slot], s, 2 * to_z + c,
            )

        def add(self, who, land, slot):
            self.gw[who] = (self.gw[who].astype(F32) + land[slot].astype(F32)).astype(BF16)

        def add_pair(self, to_z):
            self.pair(to_z).wait_recv()
            self.add(2 * to_z + c, self.land_p, to_z)

        def first(self):
            for slot, of_z in ((1, mid_o), (2, end_o), (0, near)):
                self.add_pair(of_z)

                @pl.when(is_mid == 0)
                def _(slot=slot, of_z=of_z):
                    self.along(slot, near, of_z, slot).start()

            @pl.when(is_mid == 1)
            def _():
                self.along(0, near, near, 0).start()

            self.add_pair(z)

        def second(self):
            @pl.when(is_mid == 1)
            def _():
                for i, of_z in ((1, mid_o), (2, end_o)):
                    self.along(i, near, of_z, i).wait_recv()
                    self.add(2 * of_z + c, self.land_z, i)
                    self.along(i, of_z, of_z, 3).start()

        def wait(self):
            self.along(0, near, z, 0).wait_recv()
            self.along(1, near, z, 3).wait_recv()

        def total(self, at):
            value = self.gw[f, at].astype(F32)
            return value + self.land_z[0, at].astype(F32) + self.land_z[3, at].astype(F32)

        def drain(self):
            def one(to_z, _):
                self.pair(to_z).wait_send()
                return 0

            lax.fori_loop(0, n_f // 2, one, 0)
            for i in range(3):
                self.along(i, near, near, 0).wait_send()

    barrier = pltpu.get_barrier_semaphore()
    for who in (sx, sy, sd):
        pl.semaphore_signal(barrier, inc=1, device_id=(who, f), device_id_type=pl.DeviceIdType.MESH)
    n_peers = 3
    if inside:
        for d in range(1, n_f):
            pl.semaphore_signal(
                barrier, inc=1, device_id=(s, (f + d) % n_f), device_id_type=pl.DeviceIdType.MESH
            )
        n_peers += n_f - 1
    pl.semaphore_wait(barrier, n_peers)

    others = (sx, sy, sd)
    ag_tok = Gather(tok, 0)
    if inside:
        high = qkv_in.shape[0]
        high_d = down_in.shape[0]
        w_qkv = [
            Weight(0, by_cut(qkv_w.at[0:2], high)), Weight(4, by_cut(qkv_w.at[2:4], high))
        ]
        w_out = Weight(1, by_rows(out_w.at[0], high))
        w_up = Weight(2, by_cut(up_w, high))
        w_down = Weight(3, by_rows(down_w, high_d))

        def qkv_copy(k, p, to):
            start = pl.multiple_of((p % 3) * width + to * group + (p // 3) * 128, 128)
            src = qkv_in.at[:, pl.ds(start, 128)]
            dst = qkv_w.at[s, pl.ds(pl.multiple_of(f * high, high), high), pl.ds(p * 128, 128)]
            if k < 0:
                return pltpu.make_async_copy(src, dst, col_local.at[p])
            return remote(src, dst, col_send.at[k, p], col_recv.at[k, p], to, f)

        n_cut = 3 * pairs

        ff = up_w.shape[2]

        def up_copy(k, to):
            src = up_in.at[:, pl.ds(pl.multiple_of(to * ff, 128), ff)]
            dst = up_w.at[s, pl.ds(pl.multiple_of(f * high, high), high)]
            if k < 0:
                return pltpu.make_async_copy(src, dst, loc_sem.at[6])
            return remote(src, dst, upc_send.at[k], upc_recv.at[k], to, f)

        out_own = pltpu.make_async_copy(out_in, w_out.view(f), loc_sem.at[0])
        down_own = pltpu.make_async_copy(down_in, w_down.view(f), loc_sem.at[1])

        def small_copy(d):
            return remote(
                small_in, small_f.at[f], sf_send.at[d], sf_recv.at[d], s, (f + d) % n_f
            )

        for d in range(1, n_f):
            small_copy(d).start()
        for p in range(n_cut):
            for k, to in enumerate(others):
                qkv_copy(k, p, to).start()
        for k, to in enumerate(others):
            up_copy(k, to).start()
        for p in range(n_cut):
            qkv_copy(-1, p, s).start()
        up_copy(-1, s).start()
        out_own.start()
        down_own.start()
        small_f[f] = small_in[...]
    else:
        loads = [
            pltpu.make_async_copy(qkv_in, qkv_w, col_local.at[0]),
            pltpu.make_async_copy(up_in, up_w, loc_sem.at[6]),
            pltpu.make_async_copy(out_in, out_w, loc_sem.at[0]),
            pltpu.make_async_copy(down_in, down_w, loc_sem.at[1]),
        ]
        for load in loads:
            load.start()
    tok_own = pltpu.make_async_copy(tokens, tok.at[s], loc_sem.at[2])
    tok_own.start()
    cot_own = pltpu.make_async_copy(cot_in, cot, loc_sem.at[3])
    cot_own.start()
    seg_own = pltpu.make_async_copy(seg_in, segs.at[s], loc_sem.at[4])
    seg_own.start()

    def seg_copy(k, to):
        return remote(seg_in, segs.at[s], seg_send.at[k], seg_recv.at[k], to, f)

    for k, to in enumerate(others):
        seg_copy(k, to).start()

    if inside:
        for d in range(1, n_f):
            remote(
                small_in, small_f.at[(f + n_f - d) % n_f], sf_send.at[d], sf_recv.at[d],
                s, (f + d) % n_f,
            ).wait_recv()
        per = n_f * high // 128
        each = n_f // per
        for t in range(per):
            value = small_f[t * each, 0:8]
            for e in range(1, each):
                value = value + small_f[t * each + e, 0:8]
            small_s[s, t] = value
        for e in range(n_f):
            bias_row[0:1, pl.ds(e * 128, 128)] = small_f[e, 8:9]

        def small_wide(k, to):
            return remote(small_s.at[s], small_s.at[s], ss_send.at[k], ss_recv.at[k], to, f)

        for k, to in enumerate(others):
            small_wide(k, to).start()
        ag_tok.start(tokens)
        for p in range(n_cut):
            qkv_copy(-1, p, s).wait()
            for k, to in enumerate(others):
                qkv_copy(k, p, to).wait_recv()
        for weight in w_qkv:
            weight.start()
        w_out.start(out_in)
        up_copy(-1, s).wait()
        for k, to in enumerate(others):
            up_copy(k, to).wait_recv()
        w_up.start_far()
        for k, who in enumerate(others):
            remote(
                small_s.at[who], small_s.at[who], ss_send.at[k], ss_recv.at[k], who, f
            ).wait_recv()
        for b in range(4):
            for t in range(per):
                params[:, pl.ds((b * per + t) * 128, 128)] = small_s[b, t]
    else:
        ag_tok.start(tokens)
        params[...] = small_in[0:8]
        bias_row[...] = small_in[8:9, 0 : bias_row.shape[1]]

    zero_row = jnp.zeros((1, width), F32)

    def both(run, count):
        def step(h, carry):
            return tuple(a + b for a, b in zip(carry, run(h)))

        return lax.fori_loop(0, 2, step, (zero_row,) * count)

    def far_first(i):
        return (1 - i // 2) + 2 * (1 - i % 2)

    def param(i):
        return params[i : i + 1, :]

    tok_own.wait()
    if inside:
        w_qkv[0].relay()
    ag_tok.relay()

    def first_norm(b):
        unit, _s = unit_of(tok[b].astype(F32))
        normed[b] = (unit * param(0) + param(1)).astype(BF16)

    def norm_step(k, _):
        @pl.when(k == 1)
        def _():
            ag_tok.wait_x()

        @pl.when(k == 2)
        def _():
            ag_tok.wait_y()

        @pl.when(k == 3)
        def _():
            ag_tok.wait_d()

        first_norm(block(k))
        return 0

    lax.fori_loop(0, 1, norm_step, 0)
    if inside:
        w_qkv[1].relay()
        w_out.relay()
        w_up.start_near()
        w_down.start_far(down_in)
    lax.fori_loop(1, 4, norm_step, 0)
    if inside:
        for weight in w_qkv:
            weight.rest()
        for weight in w_qkv:
            weight.finish()
    else:
        for load in loads:
            load.wait()

    rest = normed[...].reshape(4 * rows, width)
    for p in range(pairs):
        value = dot(rest, qkv_w[:, :, p * 384 : (p + 1) * 384].reshape(width, 384))
        for q in range(3):
            piece = value[:, q * 128 : (q + 1) * 128]
            piece = piece if q else piece * 0.125
            at = slice((3 * p + q) * 128, (3 * p + q + 1) * 128)
            triple[:, :, at] = piece.astype(BF16).reshape(4, rows, 128)
    if inside:
        out_own.wait()
        w_out.rest()
        w_out.finish()

    seg_own.wait()
    for k, who in enumerate(others):
        remote(seg_in, segs.at[who], seg_send.at[k], seg_recv.at[k], who, f).wait_recv()
    seg_all = segs[...]

    def below(level):
        count = jnp.sum((seg_all < level).astype(F32), axis=0)
        return jnp.sum(count, axis=1, keepdims=True)

    bound_1, bound_2 = below(1), below(2)
    blocks = window // rows
    lane = lax.broadcasted_iota(jnp.int32, (1, 128), 1)
    left = (lane < HEAD_DIM).astype(F32)
    sides = (left.astype(BF16), (1.0 - left).astype(BF16))
    pick = lax.broadcasted_iota(jnp.int32, (rows, 128), 1) < HEAD_DIM

    def set_starts(r, _):
        i = (r * rows + lax.broadcasted_iota(jnp.int32, (rows, 128), 0)).astype(F32)
        starts[r] = jnp.where(i >= bound_2, bound_2, jnp.where(i >= bound_1, bound_1, 0.0))
        return 0

    lax.fori_loop(0, 4, set_starts, 0)

    def cut(r, part_at, p, count):
        at = pl.ds(pl.multiple_of((3 * p + part_at) * 128, 128), 128)
        return triple[pl.ds(r, count), :, at].reshape(count * rows, 128)

    def masked(scores, r, first, count):
        start = starts[r]
        tiles = []
        for t in range(count * rows // 128):
            j = lax.broadcasted_iota(jnp.int32, (rows, 128), 1) + t * 128
            keep = (first * rows + j).astype(F32) >= start
            if t * 128 >= (count - 1) * rows:
                i = lax.broadcasted_iota(jnp.int32, (rows, 128), 0)
                keep = keep & (j - (count - 1) * rows <= i)
            tiles.append(jnp.where(keep, scores[:, t * 128 : (t + 1) * 128], NEG))
        return jnp.concatenate(tiles, axis=1)

    rs_1 = Scatter(land_a, 0)

    def attend_pair(r, first, count, p):
        query, keys, vals = cut(r, 0, p, 1), cut(first, 1, p, count), cut(first, 2, p, count)
        outs = []
        for e in range(2):
            scores = masked(dot(query * sides[e], keys, NT), r, first, count)
            expo = jnp.exp(scores - jnp.max(scores, -1, keepdims=True))
            low = (expo * (1.0 / jnp.sum(expo, -1, keepdims=True))).astype(BF16)
            probs[r, 2 * p + e, :, 0 : count * rows] = low
            outs.append(dot(low, vals))
        attended[r, :, p * 128 : (p + 1) * 128] = jnp.where(pick, outs[0], outs[1]).astype(BF16)

    def attend(i, _):
        rel = far_first(i)
        r = block(rel)
        for count in range(1, blocks + 1):
            @pl.when(r + 1 >= count if count == blocks else r + 1 == count)
            def _(count=count):
                for p in range(pairs):
                    attend_pair(r, r + 1 - count, count, p)

        part[rel] = dot(attended[r], out_w[0]).astype(BF16)
        rs_1.step(rel)
        if inside:
            @pl.when(i == 1)
            def _():
                w_up.relay()
                w_down.start_near(down_in)

        return 0

    lax.fori_loop(0, 4, attend, 0)
    rs_1.relay()
    if inside:
        w_down.relay()
        w_up.rest()
    rs_1.wait()

    def mid_norm(h):
        at = half_rows(h)
        value = rs_1.total(h)
        branch[at] = value
        unit, _s = unit_of(value)
        mid = tok[s, at].astype(F32) + (unit * param(2) + param(3))
        middle[at] = mid
        unit, _s = unit_of(mid)
        inner[s, at] = (unit * param(4) + param(5)).astype(BF16)

    for h in range(2):
        mid_norm(h)
    ag_inner = Gather(inner, 1)
    ag_inner.start()
    rs_1.drain()
    if inside:
        w_up.finish()

    ff = up_w.shape[2]
    tile = 512
    rs_2 = Scatter(land_b, 1)

    def forward_step(k, _):
        ag_inner.step(k)
        r = block(k)

        def column(n, _):
            at = pl.ds(pl.multiple_of(n * tile, tile), tile)
            pre = dot(inner[r], up_w[:, :, at].reshape(width, tile)) + bias_row[:, at]
            square = pre * pre
            bend = jnp.tanh(0.7978845608028654 * pre * (1.0 + 0.044715 * square))
            near = 0.5 + 0.5 * bend
            activ[r, :, at] = (pre * near).astype(BF16)
            slope = near + pre * (0.5 - 0.5 * bend * bend) * (
                0.7978845608028654 + 0.10703222440890037 * square
            )
            dgelu[r, :, at] = slope.astype(BF16)
            return 0

        lax.fori_loop(0, ff // tile, column, 0)
        return 0

    lax.fori_loop(0, 4, forward_step, 0)
    if inside:
        down_own.wait()
        w_down.rest()
        w_down.finish()

    def down_step(i, _):
        rel = far_first(i)
        r = block(rel)

        part[rel] = dot(activ[r], down_w[...]).astype(BF16)
        rs_2.step(rel)
        return 0

    lax.fori_loop(0, 4, down_step, 0)
    rs_2.relay()
    cot_own.wait()
    rs_2.wait()

    def last_norm(h):
        at = half_rows(h)
        unit, scale = unit_of(rs_2.total(h))
        result_v[at] = (middle[at] + (unit * param(6) + param(7))).astype(BF16)
        grad = cot[at].astype(F32)
        gmix[s, at] = pull_of(grad, param(6), unit, scale).astype(BF16)
        return col_sum(grad * unit), col_sum(grad)

    grad_gain_d, grad_shift_d = both(last_norm, 2)
    sg_rows = [None] * 8
    sg_rows[6], sg_rows[7] = grad_gain_d, grad_shift_d
    ag_mix = Gather(gmix, 2)
    ag_mix.start()
    result_out = pltpu.make_async_copy(result_v, result, o_sem.at[2])
    result_out.start()
    rs_2.drain()

    rs_3 = Scatter(land_a, 2)
    sg_bias = bias_row

    def clear(n, _):
        at = pl.ds(pl.multiple_of(n * tile, tile), tile)
        sg_bias[:, at] = jnp.zeros((1, tile), F32)
        return 0

    lax.fori_loop(0, ff // tile, clear, 0)

    def back_step(k, _):
        ag_mix.step(k)
        r = block(k)

        def column(n, _):
            at = pl.ds(pl.multiple_of(n * tile, tile), tile)
            grad = dot(gmix[r], down_w[at], NT)
            low = (dgelu[r, :, at].astype(F32) * grad).astype(BF16)
            dgelu[r, :, at] = low
            sg_bias[:, at] = sg_bias[:, at] + col_sum(low.astype(F32))
            return 0

        lax.fori_loop(0, ff // tile, column, 0)
        return 0

    lax.fori_loop(0, 4, back_step, 0)

    def inner_step(i, _):
        rel = far_first(i)
        r = block(rel)

        part[rel] = dot(dgelu[r], up_w[...].reshape(width, ff), NT).astype(BF16)
        rs_3.step(rel)
        return 0

    lax.fori_loop(0, 4, inner_step, 0)

    TN = ((0,), (0,))

    def flat(ref, lanes=slice(None)):
        held = ref[:, :, lanes]
        return held.reshape(4 * rows, held.shape[2])

    def all_pairs(shed):
        for to_z in range(n_f // 2):
            shed.pair(to_z).start()

    def cut_grads(left, right, gw, shed, lanes=slice(None)):
        for b in range(4):
            value = dot(flat(left, slice(b * rows, (b + 1) * rows)), flat(right, lanes), TN)
            gw[:, b * high : (b + 1) * high, :] = value.astype(BF16).reshape(n_f, high, -1)
        all_pairs(shed)

    def row_grads(left, right, gw, shed):
        each = left.shape[2] // n_f
        most = max(each, 256)
        for b in range(left.shape[2] // most):
            value = dot(flat(left, slice(b * most, (b + 1) * most)), flat(right), TN)
            count = most // each
            gw[b * count : (b + 1) * count] = value.astype(BF16).reshape(count, each, -1)
        all_pairs(shed)

    if inside:
        shed_down = Shed(0, gw_down, lp_down, lz_down)
        shed_up = Shed(1, gw_up, lp_up, lz_up)
        shed_out = Shed(2, gw_out, lp_out, lz_out)
        shed_qkv = [
            Shed(3 + p, gw_qkv[p], lp_qkv[p], lz_qkv[p]) for p in range(pairs)
        ]
        ag_tok.drain()
    rs_3.relay()
    if inside:
        row_grads(activ, gmix, gw_down, shed_down)
        shed_down.first()
    rs_3.wait()

    def mid_back(h):
        at = half_rows(h)
        grad = rs_3.total(h)
        unit, scale = unit_of(middle[at])
        total = cot[at].astype(F32) + pull_of(grad, param(4), unit, scale)
        gmid[at] = total
        out = [col_sum(grad * unit), col_sum(grad)]
        unit, scale = unit_of(branch[at])
        gbr[s, at] = pull_of(total, param(2), unit, scale).astype(BF16)
        return out[0], out[1], col_sum(total * unit), col_sum(total)

    sg_rows[4], sg_rows[5], sg_rows[2], sg_rows[3] = both(mid_back, 4)
    ag_br = Gather(gbr, 3)
    ag_br.start()
    rs_3.drain()
    if inside:
        cut_grads(inner, dgelu, gw_up, shed_up)
    ag_br.relay()
    if inside:
        shed_up.first()
    if inside:
        shed_down.second()
    ag_br.wait_x()
    ag_br.wait_y()
    ag_br.wait_d()

    if inside:
        per = n_f * high // 128
        gdown_out = pltpu.make_async_copy(fin_down, gdown, o_sem.at[3])
        gout_out = pltpu.make_async_copy(fin_out, gout, o_sem.at[4])
        gup_out = pltpu.make_async_copy(gup_v, gup, o_sem.at[5])
        gqkv_out = pltpu.make_async_copy(gqkv_v, gqkv, o_sem.at[6])
        gsmall_out = pltpu.make_async_copy(small_sum, gsmall, o_sem.at[7])

        def ts_copy(k, to):
            return remote(sg_s.at[to], sg_land_s.at[k], ts_send.at[k], ts_recv.at[k], to, f)

        def tf_copy(d):
            to = (f + d) % n_f
            return remote(
                sg_f.at[to], sg_land_f.at[d - 1], tf_send.at[d], tf_recv.at[d], s, to
            )

        def small_first():
            for b in range(4):
                for t in range(per):
                    at = slice((b * per + t) * 128, (b * per + t + 1) * 128)
                    for i in range(8):
                        sg_s[b, t, i : i + 1, :] = sg_rows[i][:, at]
            for k, to in enumerate(others):
                ts_copy(k, to).start()

        def small_second():
            for k, to in enumerate(others):
                ts_copy(k, to).wait_recv()
            for who in range(n_f):
                t = who * high // 128
                sg_f[who, 0:8] = (
                    sg_s[s, t] + sg_land_s[0, t] + sg_land_s[1, t] + sg_land_s[2, t]
                )
                sg_f[who, 8:9] = sg_bias[:, who * 128 : (who + 1) * 128]
            for d in range(1, n_f):
                tf_copy(d).start()

        def small_third():
            for d in range(1, n_f):
                tf_copy(d).wait_recv()
            value = sg_f[f]
            for d in range(1, n_f):
                value = value + sg_land_f[d - 1]
            small_sum[...] = value
            gsmall_out.start()

        def gu_copy(k, to, who):
            dst = gup_v.at[:, pl.ds(pl.multiple_of(who * ff, 128), ff)]
            return remote(fin_up.at[to], dst, gu_send.at[k], gu_recv.at[k], to, f)

        def gc_at(p, who):
            start = pl.multiple_of((p % 3) * width + who * group + (p // 3) * 128, 128)
            return pl.ds(start, 128)

        def gc_copy(k, p, to, who):
            return remote(
                fin_qkv.at[to, :, pl.ds(p * 128, 128)], gqkv_v.at[:, gc_at(p, who)],
                gc_send.at[k, p], gc_recv.at[k, p], to, f,
            )

    def make_gatt(r, _):
        gatt[r] = dot(gbr[r], out_w[0], NT).astype(BF16)
        return 0

    lax.fori_loop(0, 4, make_gatt, 0)
    if inside:
        shed_up.second()

    def back_pair(p):
        lanes = slice(p * 128, (p + 1) * 128)
        for r in range(3, -1, -1):
            first = max(r + 1 - blocks, 0)
            count = r + 1 - first
            query, keys, vals = cut(r, 0, p, 1), cut(first, 1, p, count), cut(first, 2, p, count)
            grad = gatt[r, :, lanes]
            query_t, grad_t = query.T, grad.T
            outs, key_parts, value_parts = [], [], []
            for e in range(2):
                low = probs[r, 2 * p + e, :, 0 : count * rows]
                grad_probs = dot(grad * sides[e], vals, NT)
                full = low.astype(F32)
                inner_sum = jnp.sum(full * grad_probs, -1, keepdims=True)
                grad_scores = (full * (grad_probs - inner_sum)).astype(BF16)
                outs.append(dot(grad_scores, keys))
                side = slice(e * HEAD_DIM, (e + 1) * HEAD_DIM)
                here = slice(p * 128 + e * HEAD_DIM, p * 128 + (e + 1) * HEAD_DIM)
                key_part = dot(query_t[side], grad_scores)
                value_part = dot(grad_t[side], low)
                for n in range(count):
                    span = slice((first + n) * rows, (first + n + 1) * rows)
                    cols = slice(n * rows, (n + 1) * rows)
                    if r == 3 or (first + n) < 4 - blocks and r == first + n + blocks - 1:
                        dkt[here, span] = key_part[:, cols]
                        dvt[here, span] = value_part[:, cols]
                    else:
                        dkt[here, span] = dkt[here, span] + key_part[:, cols]
                        dvt[here, span] = dvt[here, span] + value_part[:, cols]
            at = slice(3 * p * 128, (3 * p + 1) * 128)
            gtri[r, :, at] = (jnp.where(pick, outs[0], outs[1]) * 0.125).astype(BF16)
        for b in range(4):
            span = slice(b * rows, (b + 1) * rows)
            at = slice((3 * p + 1) * 128, (3 * p + 2) * 128)
            gtri[b, :, at] = dkt[lanes, span].astype(BF16).T
            at = slice((3 * p + 2) * 128, (3 * p + 3) * 128)
            gtri[b, :, at] = dvt[lanes, span].astype(BF16).T

    for p in range(pairs):
        back_pair(p)
        if inside and p < pairs - 1:
            cut_grads(normed, gtri, gw_qkv[p], shed_qkv[p], slice(p * 384, (p + 1) * 384))

    rs_4 = Scatter(land_b, 3)

    def normed_step(i, carry):
        rel = far_first(i)
        r = block(rel)
        grad = dot(gtri[r], qkv_w[...].reshape(width, 3 * group), NT)
        part[rel] = grad.astype(BF16)
        rs_4.step(rel)
        unit, _s = unit_of(tok[r].astype(F32))
        return carry[0] + col_sum(grad * unit), carry[1] + col_sum(grad)

    sg_rows[0], sg_rows[1] = lax.fori_loop(0, 4, normed_step, (zero_row, zero_row))
    if inside:
        for p in range(pairs - 1):
            shed_qkv[p].first()
        p = pairs - 1
        cut_grads(normed, gtri, gw_qkv[p], shed_qkv[p], slice(p * 384, (p + 1) * 384))
        row_grads(attended, gbr, gw_out, shed_out)
        small_first()
        shed_qkv[p].first()
        shed_out.first()
    rs_4.relay()
    if inside:
        small_second()
        shed_qkv[0].second()
        shed_down.wait()
        fin_down[...] = shed_down.total(slice(None))
        gdown_out.start()
        shed_up.wait()
        for b in range(4):
            fin_up[b] = shed_up.total(slice(b * high, (b + 1) * high))
        for k, to in enumerate(others):
            gu_copy(k, to, s).start()
        gup_v[:, pl.ds(pl.multiple_of(s * ff, 128), ff)] = fin_up[s]
        for shed in shed_qkv[1:]:
            shed.second()
        shed_out.second()
        for q, shed in enumerate(shed_qkv):
            shed.wait()
            for b in range(4):
                fin_qkv[b, :, q * 384 : (q + 1) * 384] = shed.total(
                    slice(b * high, (b + 1) * high)
                )
            for p in range(3 * q, 3 * q + 3):
                for k, to in enumerate(others):
                    gc_copy(k, p, to, s).start()
                gqkv_v[:, gc_at(p, s)] = fin_qkv[s, :, p * 128 : (p + 1) * 128]
        shed_out.wait()
        fin_out[...] = shed_out.total(slice(None))
        gout_out.start()
        for k, who in enumerate(others):
            gu_copy(k, who, who).wait_recv()
        gup_out.start()
        small_third()
    rs_4.wait()

    def first_back(h, _):
        at = half_rows(h)
        unit, scale = unit_of(tok[s, at].astype(F32))
        gmid[at] = gmid[at] + pull_of(rs_4.total(h), param(0), unit, scale)
        pltpu.make_async_copy(gmid.at[at], tgrad.at[at], o_sem.at[h]).start()
        return 0

    lax.fori_loop(0, 2, first_back, 0)
    if inside:
        for k, who in enumerate(others):
            for p in range(n_cut):
                gc_copy(k, p, who, who).wait_recv()
        gqkv_out.start()

    for h in range(2):
        pltpu.make_async_copy(gmid.at[half_rows(h)], tgrad.at[half_rows(h)], o_sem.at[h]).wait()
    result_out.wait()
    if inside:
        gsmall_out.wait()
        gdown_out.wait()
        gout_out.wait()
        gup_out.wait()
        gqkv_out.wait()
        for k, to in enumerate(others):
            gu_copy(k, to, s).wait_send()
            ts_copy(k, to).wait_send()
            for p in range(n_cut):
                gc_copy(k, p, to, s).wait_send()
                qkv_copy(k, p, to).wait_send()
            up_copy(k, to).wait_send()
            small_wide(k, to).wait_send()
        for d in range(1, n_f):
            tf_copy(d).wait_send()
            small_copy(d).wait_send()
        for weight in (*w_qkv, w_out, w_up, w_down):
            weight.drain()
        for shed in (shed_down, shed_up, shed_out, *shed_qkv):
            shed.drain()
    else:
        for i in range(8):
            small_sum[i : i + 1, :] = sg_rows[i]
        small_sum[8:9, 0:ff] = sg_bias[...]
        gsmall_out = pltpu.make_async_copy(small_sum, gsmall, o_sem.at[7])
        gsmall_out.start()
        gsmall_out.wait()
    for k, to in enumerate(others):
        seg_copy(k, to).wait_send()
    for gather in (ag_inner, ag_mix, ag_br) + (() if inside else (ag_tok,)):
        gather.drain()
    rs_4.drain()


def finish_kernel(n_f, n_big, *refs):
    small, given = refs[0], refs[1 : 1 + n_big]
    made, minor = refs[1 + n_big : 1 + 2 * n_big], refs[1 + 2 * n_big : 10 + 2 * n_big]
    held, (in_sem, out_sem) = refs[10 + 2 * n_big : 10 + 3 * n_big], refs[10 + 3 * n_big :]
    cuts = []
    for i in range(n_big):
        tall = given[i].shape[0]
        for j in range(max(1, tall // 64)):
            at = pl.ds(j * min(tall, 64), min(tall, 64))
            cuts.append((i, at, len(cuts)))
    for i, at, n in cuts:
        pltpu.make_async_copy(given[i].at[at], held[i].at[at], in_sem.at[n]).start()
    each = minor[0].shape[1]
    place = lax.axis_index("fsdp") % (128 // each)
    for i in range(8):
        row = small[i : i + 1, :]
        value = row[:, 0:each]
        for q in range(1, 128 // each):
            value = jnp.where(place == q, row[:, q * each : (q + 1) * each], value)
        minor[i][...] = value
    minor[8][...] = small[8:9, :]
    for i, at, n in cuts:
        pltpu.make_async_copy(given[i].at[at], held[i].at[at], in_sem.at[n]).wait()
        pltpu.make_async_copy(held[i].at[at], made[i].at[at], out_sem.at[n]).start()
    for i, at, n in cuts:
        pltpu.make_async_copy(held[i].at[at], made[i].at[at], out_sem.at[n]).wait()


def finish(n_f, high, *made):
    big, small = made[:6], made[6]
    whole, anywhere = pl.BlockSpec(memory_space=pltpu.VMEM), pl.BlockSpec(memory_space=pl.ANY)
    count = sum(max(1, v.shape[0] // 64) for v in big)
    minor = [jax.ShapeDtypeStruct((1, high), F32)] * 8 + [jax.ShapeDtypeStruct((1, 128), F32)]
    out = pl.pallas_call(
        partial(finish_kernel, n_f, 6),
        out_shape=[jax.ShapeDtypeStruct(v.shape, v.dtype) for v in big] + minor,
        in_specs=[whole] + [anywhere] * 6,
        out_specs=[anywhere] * 6 + [whole] * 9,
        scratch_shapes=[pltpu.VMEM(v.shape, v.dtype) for v in big]
        + [pltpu.SemaphoreType.DMA((count,))] * 2,
    )(small, *big)
    result, tgrad, gqkv, gout, gup, gdown = out[:6]
    small = [v[0] for v in out[6:]]
    return (result[None], tgrad[None], gqkv, gout, gup, small[8], gdown, *small[:8])


def on_device(n_seq, n_f, *args):
    (tokens, segments, qkv_weight, out_weight, up_weight, up_bias, down_weight) = args[:7]
    vectors, cotangent = args[7:15], args[15]
    rows, width = tokens.shape[1:]
    high, high_d = qkv_weight.shape[0], down_weight.shape[0]
    length = n_seq * rows
    group = qkv_weight.shape[1] // 3 // n_seq
    heads = group // HEAD_DIM
    ff = up_weight.shape[1] // n_seq
    half = rows // 2
    window = rows * min(n_seq, 1 + -(-511 // rows))
    inside = n_f == 8 and high % 32 == 0
    f = lax.axis_index("fsdp")
    small = jnp.stack([v.astype(F32) for v in vectors])
    if inside:
        each = 128 // high
        lane = lax.broadcasted_iota(jnp.int32, (8, 128), 1) // high
        small = jnp.where(lane == f % each, jnp.tile(small, (1, each)), 0.0)
        small = jnp.concatenate([small, up_bias.astype(F32)[None], jnp.zeros((7, 128), F32)])
        weights = (qkv_weight, out_weight, up_weight, down_weight)
    else:
        small = lax.all_gather(small, ("seq", "fsdp"), axis=1, tiled=True)
        bias = lax.all_gather(up_bias.astype(F32), "fsdp", axis=0, tiled=True)
        bias = jnp.pad(bias[None], ((0, 7), (0, width - ff)))
        small = jnp.concatenate([small, bias])

        def columns(weight, parts):
            cut = weight.reshape(high, parts, n_seq, -1, 128).transpose(2, 0, 3, 1, 4)
            cut = cut.reshape(n_seq, high, -1)
            cut = lax.all_to_all(cut, "seq", split_axis=0, concat_axis=0, tiled=True)
            return lax.all_gather(cut, "fsdp", axis=1, tiled=True)

        weights = (
            columns(qkv_weight, 3),
            lax.all_gather(out_weight, "fsdp", axis=0, tiled=True)[None],
            columns(up_weight, 1),
            lax.all_gather(down_weight, "fsdp", axis=0, tiled=True),
        )
    vmem, anywhere, dma = pltpu.VMEM, pl.BlockSpec(memory_space=pl.ANY), pltpu.SemaphoreType.DMA
    whole = pl.BlockSpec(memory_space=pltpu.VMEM)
    full = (4, rows, width)
    saved = {
        "normed": (full, BF16), "inner": (full, BF16), "gmix": (full, BF16), "gbr": (full, BF16),
        "attended": ((4, rows, group), BF16), "activ": ((4, rows, ff), BF16),
        "dgelu": ((4, rows, ff), BF16), "gtri": ((4, rows, 3 * group), BF16),
    }
    n_cut = 3 * (group // 128)
    pieces = {"q0": (n_seq * high, 384), "q1": (n_seq * high, 384), "out": (high, width),
              "up": (n_seq * high, ff), "down": (high_d, width)}
    scratch = {
        "tok": vmem(full, BF16), "normed": None, "inner": None, "gmix": None, "gbr": None,
        "qkv_w": vmem((n_seq, rows, 3 * group), BF16), "out_w": vmem((1, group, width), BF16),
        "up_w": vmem((n_seq, rows, ff), BF16), "down_w": vmem((ff, width), BF16),
        "segs": vmem((4, 1, rows), jnp.int32),
        "small_f": vmem((n_f if inside else 1, 16, 128), F32), "small_s": vmem((4, width // 512, 8, 128), F32),
        "params": vmem((8, width), F32), "bias_row": vmem((1, ff), F32),
        "triple": vmem((4, rows, 3 * group), BF16), "probs": vmem((4, heads, rows, window), BF16),
        "attended": None, "starts": vmem((4, rows, 128), F32), "activ": None, "dgelu": None,
        "part": vmem(full, BF16), "land_a": vmem((6, half, width), BF16),
        "land_b": vmem((6, half, width), BF16),
        "branch": vmem((rows, width), F32), "middle": vmem((rows, width), F32),
        "gmid": vmem((rows, width), F32), "cot": vmem((rows, width), BF16),
        "gtri": None, "gatt": vmem((4, rows, group), BF16), "dkt": vmem((group, length), F32),
        "dvt": vmem((group, length), F32),
    }
    for name, (tall, wide) in pieces.items():
        scratch["gw_" + name] = vmem((n_f if inside else 1, tall if inside else 16, wide), BF16)
    for name, (tall, wide) in pieces.items():
        scratch["lp_" + name] = vmem((n_f // 2 if inside else 1, tall if inside else 16, wide), BF16)
    for name, (tall, wide) in pieces.items():
        scratch["lz_" + name] = vmem((n_f // 2 if inside else 1, tall if inside else 16, wide), BF16)
    scratch["result_v"] = vmem((rows, width), BF16)
    scratch["fin_qkv"] = vmem((4, high, 3 * group), F32)
    scratch["fin_up"] = vmem((4, high, ff), F32)
    scratch["fin_down"] = vmem((high_d, width), F32)
    scratch["fin_out"] = vmem((high, width), F32)
    scratch["gup_v"] = vmem((high, n_seq * ff), F32)
    scratch["gqkv_v"] = vmem((high, n_seq * 3 * group), F32)
    scratch["small_sum"] = vmem((16, 128 if inside else width), F32)
    tiles = width // 512
    scratch["sg_s"] = vmem((4, tiles, 8, 128), F32)
    scratch["sg_land_s"] = vmem((3, tiles, 8, 128), F32)
    scratch["sg_f"] = vmem((n_f if inside else 1, 16, 128), F32)
    scratch["sg_land_f"] = vmem((n_f - 1 if inside else 1, 16, 128), F32)
    for name, shape in (
        ("ag_send", (4, 6)), ("ag_recv", (4, 6)), ("rs_send", (4, 6)), ("rs_recv", (4, 6)),
        ("w_send", (5, 4)), ("w_recv", (5, 3)), ("p_send", (5, 4)), ("p_recv", (5, 4)),
        ("col_send", (3, n_cut)), ("col_recv", (3, n_cut)), ("col_local", (n_cut,)),
        ("upc_send", (3,)), ("upc_recv", (3,)), ("seg_send", (3,)), ("seg_recv", (3,)),
        ("sf_send", (8,)), ("sf_recv", (8,)), ("ss_send", (3,)), ("ss_recv", (3,)),
        ("loc_sem", (7,)), ("o_sem", (8,)),
        ("gp_send", (5, 4)), ("gp_recv", (5, 4)), ("gz_send", (5, 4)), ("gz_recv", (5, 4)),
        ("gc_send", (3, n_cut)), ("gc_recv", (3, n_cut)), ("gu_send", (3,)), ("gu_recv", (3,)),
        ("ts_send", (3,)), ("ts_recv", (3,)), ("tf_send", (8,)), ("tf_recv", (8,)),
    ):
        scratch[name] = dma(shape)
    outs = {
        "result": ((rows, width), BF16), "tgrad": ((rows, width), F32),
        "gqkv": ((high, n_seq * 3 * group), F32), "gout": ((high, width), F32),
        "gup": ((high, n_seq * ff), F32), "gdown": ((high_d, width), F32),
        "gsmall": ((16, 128 if inside else width), F32),
    }
    if inside:
        for name, shape in saved.items():
            scratch[name] = vmem(*shape)
        extra = []
    else:
        extra = list(saved)
    names = list(scratch)

    def kernel(*refs):
        given = refs[:8]
        made = refs[8 : 8 + len(outs)]
        more = dict(zip(extra, refs[8 + len(outs) :]))
        rest = refs[8 + len(outs) + len(extra) :]
        more.update(zip([n for n in names if scratch[n] is not None], rest))
        layer_kernel(inside, n_f, *given, *made, *[more[n] for n in names])

    shapes = [*outs.values(), *[saved[n] for n in extra]]
    made = pl.pallas_call(
        kernel,
        out_shape=[jax.ShapeDtypeStruct(*shape) for shape in shapes],
        in_specs=[anywhere, anywhere, whole, anywhere] + [anywhere] * 4,
        out_specs=[anywhere] * len(outs) + [whole] * len(extra),
        scratch_shapes=[scratch[n] for n in names if scratch[n] is not None],
        compiler_params=pltpu.CompilerParams(
            collective_id=0, has_side_effects=True, vmem_limit_bytes=67043328
        ),
    )(tokens[0], segments, small, cotangent[0], *weights)
    result, tgrad, gqkv, gout, gup, gdown, gsmall = made[:7]
    if inside:
        return finish(n_f, high, *made[:7])
    else:
        kept = {n: v.reshape(length, -1) for n, v in zip(extra, made[7:])}

        def turned_dot(left, right):
            return lax.dot_general(
                kept[left], kept[right], (((0,), (0,)), ((), ())), preferred_element_type=F32
            ).astype(BF16)

        def shed(value):
            return lax.psum_scatter(value, "fsdp", scatter_dimension=0, tiled=True)

        def columns_back(value, parts):
            cut = value.reshape(n_seq, n_f, high, -1).transpose(1, 0, 2, 3)
            cut = lax.all_to_all(shed(cut)[0], "seq", split_axis=0, concat_axis=0, tiled=True)
            cut = cut.reshape(n_seq, high, -1, parts, 128).transpose(1, 3, 0, 2, 4)
            return cut.reshape(high, -1).astype(F32)

        gqkv = columns_back(turned_dot("normed", "gtri"), 3)
        gout = shed(turned_dot("attended", "gbr")).astype(F32)
        gup = columns_back(turned_dot("inner", "dgelu"), 1)
        gdown = shed(turned_dot("activ", "gmix")).astype(F32)
        vectors = lax.psum_scatter(gsmall[:8], ("seq", "fsdp"), scatter_dimension=1, tiled=True)
        gbias = shed(gsmall[8, :ff])
    return (result[None], tgrad[None], gqkv, gout, gup, gbias, gdown, *vectors)


def solution(mesh):
    rows = P(("seq", "fsdp"), None)
    vector = P(("seq", "fsdp"))
    acts = P("fsdp", "seq", None)
    return jax.shard_map(
        partial(on_device, mesh.shape["seq"], mesh.shape["fsdp"]),
        mesh=mesh,
        in_specs=(acts, P("fsdp", "seq"), rows, rows, rows, vector, rows, *(vector,) * 8, acts),
        out_specs=(acts, acts, rows, rows, rows, vector, rows, *(vector,) * 8),
        check_vma=False,
    )
```

time: 245 us -> 215 us (0.88)
  Pallas kernels: 232 us -> 211 us
  local copies, waits for them, and re-layouts: 10.9 us -> 1.55 us
    pallas_call x1, Pallas kernels: 232 us -> 207 us  [on_device(): pl.pallas_call(kernel, out_shape=[jax.ShapeDtypeStruct(*shape) for shape...]
    unnamed x34 -> x18, local copies, waits for them, and re-layouts: 8.13 us -> 1.35 us
    pallas_call x0 -> x1, Pallas kernels: none -> 4.35 us  [finish(): pl.pallas_call(partial(finish_kernel, n_f, 6), out_shape=[jax.ShapeDtypeS...]
where the time goes in v3:
time: 215 us; the launch traced here: 214 us
  Pallas kernels  211 us (98%)
    pallas_call x1, Pallas kernels, on_device(): pl.pallas_call(kernel, out_shape=[jax.ShapeDtypeStruct(*shape) for shape...  207 us
    pallas_call x1, Pallas kernels, finish(): pl.pallas_call(partial(finish_kernel, n_f, 6), out_shape=[jax.ShapeDtypeS...  4.35 us

profile of v3, /device:TPU:0, one launch (start us, length us, event | category | flops | bytes accessed | tf_op | source)
XLA Modules:
  0.0 214.3 jit_solution(8911116744273715415)
XLA Ops:
  0.7 0.0 copy-start.8
  0.7 0.6 copy-done.8
  1.3 0.1 pad.2.clone
  1.4 0.0 copy-start.7
  1.4 0.0 copy-start.3
  1.4 0.0 copy-start.4
  1.4 0.0 copy-start.5
  1.4 0.0 copy-start.6
  1.5 0.0 copy-start
  1.5 0.0 copy-start.1
  1.5 0.0 copy-start.2
  1.5 0.6 copy-done.7
  2.1 0.0 copy-done.3
  2.1 0.0 copy-done.4
  2.1 0.0 copy-done.5
  2.1 0.0 copy-done.6
  2.1 0.0 copy-done
  2.1 0.0 copy-done.1
  2.2 0.0 copy-done.2
  2.2 0.1 tile.10
  2.3 0.7 maximum_maximum_fusion.refs_2_
  3.0 206.8 %shard_map.271 = (bf16[256,1024]{1,0:T(8,128)(2,1)}, f32[256,1024]{1,0:T(8,128)}, f32[32,3072]{1,0:T(8,128)}, f32[32,1024]{1,0:T(8,128)}, f32[32,4096]{1,0:T(8,1...) custom-call(bf16[256,1024]{1,0:T(8,128)(2,1)} %bitcast.24, s32[1,256]{1,0:T(1,128)} %refs_1_.1, ...), custom_call_target="tpu_custom_call" | custom-call | tf_op jit(solution)/shard_map/pallas_call | solution.py:1199
  209.8 4.3 %shard_map.272 = (bf16[256,1024]{1,0:T(8,128)(2,1)}, f32[256,1024]{1,0:T(8,128)}, f32[32,3072]{1,0:T(8,128)}, f32[32,1024]{1,0:T(8,128)}, f32[32,4096]{1,0:T(8,1...) custom-call(f32[16,128]{1,0:T(8,128)} %get-tuple-element.37.refs_0_,, ...), custom_call_target="tpu_custom_call" | custom-call | tf_op jit(solution)/shard_map/pallas_call | solution.py:1067
  (7 shorter events, 0.1 us)
Async XLA Ops:
  0.7 0.7 copy-start.8
  1.4 0.7 copy-start.7
  1.4 0.7 copy-start.3
  1.4 0.7 copy-start.4
  1.4 0.7 copy-start.5
  1.4 0.7 copy-start.6
  1.5 0.7 copy-start
  1.5 0.7 copy-start.1
  1.5 0.7 copy-start.2

commit v4 on v3

--- a/solution.py
+++ b/solution.py
@@ -51,7 +51,7 @@
     gw_q0, gw_q1, gw_out, gw_up, gw_down,
     lp_q0, lp_q1, lp_out, lp_up, lp_down,
     lz_q0, lz_q1, lz_out, lz_up, lz_down,
-    result_v, fin_qkv, fin_up, fin_down, fin_out, gup_v, gqkv_v, small_sum,
+    result_v, fin_qkv, fin_up, land_qkv, land_up, fin_down, fin_out, gup_v, gqkv_v, small_sum,
     sg_s, sg_land_s, sg_f, sg_land_f,
     ag_send, ag_recv, rs_send, rs_recv,
     w_send, w_recv, p_send, p_recv,
@@ -60,7 +60,7 @@
     loc_sem, o_sem,
     gp_send, gp_recv, gz_send, gz_recv,
     gc_send, gc_recv, gu_send, gu_recv,
-    ts_send, ts_recv, tf_send, tf_recv,
+    ts_send, ts_recv, tf_send, tf_recv, turn,
 ):
     gw_qkv, lp_qkv, lz_qkv = (gw_q0, gw_q1), (lp_q0, lp_q1), (lz_q0, lz_q1)
     rows, width = tokens.shape
@@ -84,6 +84,21 @@
             device_id=(to_s, to_f), device_id_type=pl.DeviceIdType.MESH,
         )
 
+    def my_turn(cores=(0, 1)):
+        if inside:
+            @pl.when(c >= cores[0])
+            def _():
+                pl.semaphore_wait(turn, 1)
+
+    def hand_over(cores=(0, 1)):
+        if inside:
+            @pl.when(c <= cores[1])
+            def _():
+                pl.semaphore_signal(
+                    turn, inc=1, device_id=(s, 2 * z + 1 - c),
+                    device_id_type=pl.DeviceIdType.MESH,
+                )
+
     class Gather:
         def __init__(self, full, index):
             self.full, self.index = full, index
@@ -112,6 +127,8 @@
             self.copy(4, sx, 0, sy).start()
             self.copy(1, sy, 1, sy).wait_recv()
             self.copy(5, sy, 1, sx).start()
+            if self.index:
+                hand_over()
 
         def wait_x(self):
             self.copy(2, sx, 1, sx).wait_recv()
@@ -183,6 +200,7 @@
                 total = part[rel, here].astype(F32) + self.land[arrived].astype(F32)
                 part[rel, here] = total.astype(BF16)
                 self.copy(i).start()
+            hand_over((0, 0) if self.index == 3 else (0, 1))
 
         def wait(self):
             for i in (1, 3, 4, 5):
@@ -255,7 +273,7 @@
             self.start_far(own)
             self.start_near(own)
 
-        def relay(self):
+        def relay(self, all_of_it=True):
             @pl.when(is_mid == 1)
             def _():
                 for k in (1, 2):
@@ -264,13 +282,19 @@
                 for k in (1, 2):
                     self.across(k, 2 * owners[k] + c).start()
 
+            if all_of_it:
+                self.relay_rest()
+
+        def relay_rest(self):
+            @pl.when(is_mid == 1)
+            def _():
+                self.piece(z, 0, 0, near).wait_recv()
+                self.across(0, 2 * near + c).start()
+
         def rest(self):
-            self.piece(z, 0, 0, near).wait_recv()
-            self.across(0, 2 * near + c).start()
-
             @pl.when(is_mid == 0)
             def _():
-                for k in (1, 2):
+                for k in (0, 1, 2):
                     self.piece(z, 0, k, owners[k]).wait_recv()
                     self.across(k, 2 * owners[k] + c).start()
 
@@ -353,6 +377,27 @@
             lax.fori_loop(0, n_f // 2, one, 0)
             for i in range(3):
                 self.along(i, near, near, 0).wait_send()
+
+    class Direct(Shed):
+        def first(self):
+            for d in (2, 1, 3):
+                to_z = (z + d) % (n_f // 2)
+                self.add_pair(to_z)
+                self.along(d - 1, to_z, to_z, d - 1).start()
+            self.add_pair(z)
+
+        def second(self):
+            pass
+
+        def wait(self):
+            for d in (1, 2, 3):
+                self.along(d - 1, near, z, d - 1).wait_recv()
+
+        def total(self, at):
+            value = self.gw[f, at].astype(F32)
+            for d in (1, 2, 3):
+                value = value + self.land_z[d - 1, at].astype(F32)
+            return value
 
     barrier = pltpu.get_barrier_semaphore()
     for who in (sx, sy, sd):
@@ -472,7 +517,6 @@
         up_copy(-1, s).wait()
         for k, to in enumerate(others):
             up_copy(k, to).wait_recv()
-        w_up.start_far()
         for k, who in enumerate(others):
             remote(
                 small_s.at[who], small_s.at[who], ss_send.at[k], ss_recv.at[k], who, f
@@ -503,6 +547,8 @@
     if inside:
         w_qkv[0].relay()
     ag_tok.relay()
+    if inside:
+        w_up.start_far()
 
     def first_norm(b):
         unit, _s = unit_of(tok[b].astype(F32))
@@ -527,7 +573,7 @@
     lax.fori_loop(0, 1, norm_step, 0)
     if inside:
         w_qkv[1].relay()
-        w_out.relay()
+        w_out.relay(False)
         w_up.start_near()
         w_down.start_far(down_in)
     lax.fori_loop(1, 4, norm_step, 0)
@@ -550,6 +596,7 @@
             triple[:, :, at] = piece.astype(BF16).reshape(4, rows, 128)
     if inside:
         out_own.wait()
+        w_out.relay_rest()
         w_out.rest()
         w_out.finish()
 
@@ -615,7 +662,11 @@
                     attend_pair(r, r + 1 - count, count, p)
 
         part[rel] = dot(attended[r], out_w[0]).astype(BF16)
-        rs_1.step(rel)
+
+        @pl.when(c == 0)
+        def _():
+            rs_1.step(rel)
+
         if inside:
             @pl.when(i == 1)
             def _():
@@ -625,10 +676,22 @@
         return 0
 
     lax.fori_loop(0, 4, attend, 0)
+
+    my_turn((1, 1))
+
+    @pl.when(c == 1)
+    def _():
+        for i in (0, 2, 1, 3):
+            rs_1.copy(i).start()
+
     rs_1.relay()
     if inside:
         w_down.relay()
-        w_up.rest()
+
+        @pl.when(c == 1)
+        def _():
+            w_up.rest()
+
     rs_1.wait()
 
     def mid_norm(h):
@@ -644,9 +707,14 @@
     for h in range(2):
         mid_norm(h)
     ag_inner = Gather(inner, 1)
+    my_turn()
     ag_inner.start()
     rs_1.drain()
     if inside:
+        @pl.when(c == 0)
+        def _():
+            w_up.rest()
+
         w_up.finish()
 
     ff = up_w.shape[2]
@@ -654,7 +722,27 @@
     rs_2 = Scatter(land_b, 1)
 
     def forward_step(k, _):
-        ag_inner.step(k)
+        if inside:
+            @pl.when((k == 1) & (c == 1))
+            def _():
+                ag_inner.relay()
+                w_down.rest()
+                ag_inner.wait_x()
+
+            @pl.when((k == 1) & (c == 0))
+            def _():
+                ag_inner.relay()
+                ag_inner.wait_x()
+
+            @pl.when((k == 2) & (c == 0))
+            def _():
+                w_down.rest()
+
+            @pl.when(k > 1)
+            def _():
+                ag_inner.step(k)
+        else:
+            ag_inner.step(k)
         r = block(k)
 
         def column(n, _):
@@ -676,7 +764,6 @@
     lax.fori_loop(0, 4, forward_step, 0)
     if inside:
         down_own.wait()
-        w_down.rest()
         w_down.finish()
 
     def down_step(i, _):
@@ -687,6 +774,7 @@
         rs_2.step(rel)
         return 0
 
+    my_turn()
     lax.fori_loop(0, 4, down_step, 0)
     rs_2.relay()
     cot_own.wait()
@@ -704,6 +792,7 @@
     sg_rows = [None] * 8
     sg_rows[6], sg_rows[7] = grad_gain_d, grad_shift_d
     ag_mix = Gather(gmix, 2)
+    my_turn()
     ag_mix.start()
     result_out = pltpu.make_async_copy(result_v, result, o_sem.at[2])
     result_out.start()
@@ -735,16 +824,6 @@
         return 0
 
     lax.fori_loop(0, 4, back_step, 0)
-
-    def inner_step(i, _):
-        rel = far_first(i)
-        r = block(rel)
-
-        part[rel] = dot(dgelu[r], up_w[...].reshape(width, ff), NT).astype(BF16)
-        rs_3.step(rel)
-        return 0
-
-    lax.fori_loop(0, 4, inner_step, 0)
 
     TN = ((0,), (0,))
 
@@ -776,13 +855,39 @@
         shed_up = Shed(1, gw_up, lp_up, lz_up)
         shed_out = Shed(2, gw_out, lp_out, lz_out)
         shed_qkv = [
-            Shed(3 + p, gw_qkv[p], lp_qkv[p], lz_qkv[p]) for p in range(pairs)
+            (Shed if p < pairs - 1 else Direct)(3 + p, gw_qkv[p], lp_qkv[p], lz_qkv[p])
+            for p in range(pairs)
         ]
         ag_tok.drain()
+        row_grads(activ, gmix, gw_down, shed_down)
+
+        @pl.when(c == 1)
+        def _():
+            shed_down.first()
+
+    def inner_step(i, _):
+        rel = far_first(i)
+        r = block(rel)
+
+        part[rel] = dot(dgelu[r], up_w[...].reshape(width, ff), NT).astype(BF16)
+        rs_3.step(rel)
+        return 0
+
+    my_turn()
+    lax.fori_loop(0, 4, inner_step, 0)
+
+    if inside:
+        cut_grads(inner, dgelu, gw_up, shed_up)
     rs_3.relay()
     if inside:
-        row_grads(activ, gmix, gw_down, shed_down)
-        shed_down.first()
+        @pl.when(c == 1)
+        def _():
+            shed_up.first()
+
+        @pl.when(c == 0)
+        def _():
+            shed_down.first()
+
     rs_3.wait()
 
     def mid_back(h):
@@ -798,18 +903,52 @@
 
     sg_rows[4], sg_rows[5], sg_rows[2], sg_rows[3] = both(mid_back, 4)
     ag_br = Gather(gbr, 3)
+    my_turn()
     ag_br.start()
     rs_3.drain()
-    if inside:
-        cut_grads(inner, dgelu, gw_up, shed_up)
-    ag_br.relay()
-    if inside:
-        shed_up.first()
-    if inside:
-        shed_down.second()
-    ag_br.wait_x()
-    ag_br.wait_y()
-    ag_br.wait_d()
+    def arrive(k, _):
+        if inside:
+            @pl.when(k == 1)
+            def _():
+                ag_br.relay()
+
+            @pl.when((k == 1) & (c == 0))
+            def _():
+                shed_up.first()
+
+            @pl.when(k == 1)
+            def _():
+                ag_br.wait_x()
+
+            @pl.when(k > 1)
+            def _():
+                ag_br.step(k)
+
+            @pl.when(k == 2)
+            def _():
+                shed_down.second()
+        else:
+            ag_br.step(k)
+
+        r = block(k)
+        gatt[r] = dot(gbr[r], out_w[0], NT).astype(BF16)
+        if inside:
+            value = dot(attended[r], gbr[r], TN)
+
+            @pl.when(k == 0)
+            def _():
+                branch[...] = value
+
+            @pl.when(k > 0)
+            def _():
+                branch[...] = branch[...] + value
+
+        return 0
+
+    lax.fori_loop(0, 4, arrive, 0)
+    if inside:
+        gw_out[...] = branch[...].astype(BF16).reshape(gw_out.shape)
+        all_pairs(shed_out)
 
     if inside:
         per = n_f * high // 128
@@ -859,8 +998,7 @@
             gsmall_out.start()
 
         def gu_copy(k, to, who):
-            dst = gup_v.at[:, pl.ds(pl.multiple_of(who * ff, 128), ff)]
-            return remote(fin_up.at[to], dst, gu_send.at[k], gu_recv.at[k], to, f)
+            return remote(fin_up.at[to], land_up.at[who], gu_send.at[k], gu_recv.at[k], to, f)
 
         def gc_at(p, who):
             start = pl.multiple_of((p % 3) * width + who * group + (p // 3) * 128, 128)
@@ -868,17 +1006,9 @@
 
         def gc_copy(k, p, to, who):
             return remote(
-                fin_qkv.at[to, :, pl.ds(p * 128, 128)], gqkv_v.at[:, gc_at(p, who)],
+                fin_qkv.at[p, to], land_qkv.at[p, who],
                 gc_send.at[k, p], gc_recv.at[k, p], to, f,
             )
-
-    def make_gatt(r, _):
-        gatt[r] = dot(gbr[r], out_w[0], NT).astype(BF16)
-        return 0
-
-    lax.fori_loop(0, 4, make_gatt, 0)
-    if inside:
-        shed_up.second()
 
     def back_pair(p):
         lanes = slice(p * 128, (p + 1) * 128)
@@ -920,8 +1050,10 @@
 
     for p in range(pairs):
         back_pair(p)
-        if inside and p < pairs - 1:
+        if inside:
             cut_grads(normed, gtri, gw_qkv[p], shed_qkv[p], slice(p * 384, (p + 1) * 384))
+            if p == 0:
+                shed_up.second()
 
     rs_4 = Scatter(land_b, 3)
 
@@ -934,49 +1066,54 @@
         unit, _s = unit_of(tok[r].astype(F32))
         return carry[0] + col_sum(grad * unit), carry[1] + col_sum(grad)
 
+    if inside:
+        @pl.when(c == 1)
+        def _():
+            for shed in (*shed_qkv, shed_out):
+                shed.first()
+
+    my_turn()
     sg_rows[0], sg_rows[1] = lax.fori_loop(0, 4, normed_step, (zero_row, zero_row))
     if inside:
-        for p in range(pairs - 1):
-            shed_qkv[p].first()
-        p = pairs - 1
-        cut_grads(normed, gtri, gw_qkv[p], shed_qkv[p], slice(p * 384, (p + 1) * 384))
-        row_grads(attended, gbr, gw_out, shed_out)
+        @pl.when(c == 0)
+        def _():
+            shed_qkv[0].first()
+
+    rs_4.relay()
+    if inside:
+        @pl.when(c == 0)
+        def _():
+            for shed in (*shed_qkv[1:], shed_out):
+                shed.first()
+
         small_first()
-        shed_qkv[p].first()
-        shed_out.first()
-    rs_4.relay()
-    if inside:
+        shed_qkv[0].second()
+        shed_up.wait()
+        for b in range(4):
+            fin_up[b] = shed_up.total(slice(b * high, (b + 1) * high)).astype(BF16)
+        for k, to in enumerate(others):
+            gu_copy(k, to, s).start()
+        at = pl.ds(pl.multiple_of(s * high, high), high)
+        gup_v[:, pl.ds(pl.multiple_of(s * ff, 128), ff)] = shed_up.total(at)
         small_second()
-        shed_qkv[0].second()
         shed_down.wait()
         fin_down[...] = shed_down.total(slice(None))
         gdown_out.start()
-        shed_up.wait()
-        for b in range(4):
-            fin_up[b] = shed_up.total(slice(b * high, (b + 1) * high))
-        for k, to in enumerate(others):
-            gu_copy(k, to, s).start()
-        gup_v[:, pl.ds(pl.multiple_of(s * ff, 128), ff)] = fin_up[s]
-        for shed in shed_qkv[1:]:
-            shed.second()
-        shed_out.second()
         for q, shed in enumerate(shed_qkv):
             shed.wait()
             for b in range(4):
-                fin_qkv[b, :, q * 384 : (q + 1) * 384] = shed.total(
-                    slice(b * high, (b + 1) * high)
-                )
-            for p in range(3 * q, 3 * q + 3):
-                for k, to in enumerate(others):
-                    gc_copy(k, p, to, s).start()
-                gqkv_v[:, gc_at(p, s)] = fin_qkv[s, :, p * 128 : (p + 1) * 128]
-        shed_out.wait()
-        fin_out[...] = shed_out.total(slice(None))
-        gout_out.start()
+                fin_qkv[q, b] = shed.total(slice(b * high, (b + 1) * high)).astype(BF16)
+            for k, to in enumerate(others):
+                gc_copy(k, q, to, s).start()
+            own = shed.total(at)
+            for p in range(3):
+                gqkv_v[:, gc_at(3 * q + p, s)] = own[:, p * 128 : (p + 1) * 128]
         for k, who in enumerate(others):
             gu_copy(k, who, who).wait_recv()
+            gup_v[:, pl.ds(pl.multiple_of(who * ff, 128), ff)] = land_up[who].astype(F32)
         gup_out.start()
         small_third()
+        shed_out.second()
     rs_4.wait()
 
     def first_back(h, _):
@@ -988,9 +1125,15 @@
 
     lax.fori_loop(0, 2, first_back, 0)
     if inside:
+        shed_out.wait()
+        fin_out[...] = shed_out.total(slice(None))
+        gout_out.start()
         for k, who in enumerate(others):
-            for p in range(n_cut):
-                gc_copy(k, p, who, who).wait_recv()
+            for q in range(pairs):
+                gc_copy(k, q, who, who).wait_recv()
+                for p in range(3):
+                    piece = land_qkv[q, who, :, p * 128 : (p + 1) * 128]
+                    gqkv_v[:, gc_at(3 * q + p, who)] = piece.astype(F32)
         gqkv_out.start()
 
     for h in range(2):
@@ -1005,8 +1148,9 @@
         for k, to in enumerate(others):
             gu_copy(k, to, s).wait_send()
             ts_copy(k, to).wait_send()
+            for q in range(pairs):
+                gc_copy(k, q, to, s).wait_send()
             for p in range(n_cut):
-                gc_copy(k, p, to, s).wait_send()
                 qkv_copy(k, p, to).wait_send()
             up_copy(k, to).wait_send()
             small_wide(k, to).wait_send()
@@ -1149,8 +1293,10 @@
     for name, (tall, wide) in pieces.items():
         scratch["lz_" + name] = vmem((n_f // 2 if inside else 1, tall if inside else 16, wide), BF16)
     scratch["result_v"] = vmem((rows, width), BF16)
-    scratch["fin_qkv"] = vmem((4, high, 3 * group), F32)
-    scratch["fin_up"] = vmem((4, high, ff), F32)
+    scratch["fin_qkv"] = vmem((group // 128, 4, high, 384), BF16)
+    scratch["fin_up"] = vmem((4, high, ff), BF16)
+    scratch["land_qkv"] = vmem((group // 128, 4, high, 384), BF16)
+    scratch["land_up"] = vmem((4, high, ff), BF16)
     scratch["fin_down"] = vmem((high_d, width), F32)
     scratch["fin_out"] = vmem((high, width), F32)
     scratch["gup_v"] = vmem((high, n_seq * ff), F32)
@@ -1169,10 +1315,11 @@
         ("sf_send", (8,)), ("sf_recv", (8,)), ("ss_send", (3,)), ("ss_recv", (3,)),
         ("loc_sem", (7,)), ("o_sem", (8,)),
         ("gp_send", (5, 4)), ("gp_recv", (5, 4)), ("gz_send", (5, 4)), ("gz_recv", (5, 4)),
-        ("gc_send", (3, n_cut)), ("gc_recv", (3, n_cut)), ("gu_send", (3,)), ("gu_recv", (3,)),
+        ("gc_send", (3, 2)), ("gc_recv", (3, 2)), ("gu_send", (3,)), ("gu_recv", (3,)),
         ("ts_send", (3,)), ("ts_recv", (3,)), ("tf_send", (8,)), ("tf_recv", (8,)),
     ):
         scratch[name] = dma(shape)
+    scratch["turn"] = pltpu.SemaphoreType.REGULAR
     outs = {
         "result": ((rows, width), BF16), "tgrad": ((rows, width), F32),
         "gqkv": ((high, n_seq * 3 * group), F32), "gout": ((high, width), F32),

time: 215 us -> 195 us (0.907)
  Pallas kernels: 211 us -> 191 us
    pallas_call x1, Pallas kernels: 207 us -> 187 us  [on_device(): pl.pallas_call(kernel, out_shape=[jax.ShapeDtypeStruct(*shape) for shape...]
where the time goes in v4:
time: 195 us
  Pallas kernels  191 us (98%)
    pallas_call x1, Pallas kernels, on_device(): pl.pallas_call(kernel, out_shape=[jax.ShapeDtypeStruct(*shape) for shape...  187 us
    pallas_call x1, Pallas kernels, finish(): pl.pallas_call(partial(finish_kernel, n_f, 6), out_shape=[jax.ShapeDtypeS...  4.35 us

profile of v4, /device:TPU:0, one launch (start us, length us, event | category | flops | bytes accessed | tf_op | source)
XLA Modules:
  0.0 194.6 jit_solution(1668091648460908493)
XLA Ops:
  0.7 0.0 copy-start.8
  0.7 0.6 copy-done.8
  1.3 0.1 pad.2.clone
  1.4 0.0 copy-start.7
  1.4 0.0 copy-start.3
  1.4 0.0 copy-start.4
  1.4 0.0 copy-start.5
  1.4 0.0 copy-start.6
  1.5 0.0 copy-start
  1.5 0.0 copy-start.1
  1.5 0.0 copy-start.2
  1.5 0.6 copy-done.7
  2.1 0.0 copy-done.3
  2.1 0.0 copy-done.4
  2.1 0.0 copy-done.5
  2.1 0.0 copy-done.6
  2.1 0.0 copy-done
  2.1 0.0 copy-done.1
  2.2 0.0 copy-done.2
  2.2 0.1 tile.10
  2.3 0.7 maximum_maximum_fusion.refs_2_
  3.0 187.1 %shard_map.271 = (bf16[256,1024]{1,0:T(8,128)(2,1)}, f32[256,1024]{1,0:T(8,128)}, f32[32,3072]{1,0:T(8,128)}, f32[32,1024]{1,0:T(8,128)}, f32[32,4096]{1,0:T(8,1...) custom-call(bf16[256,1024]{1,0:T(8,128)(2,1)} %bitcast.24, s32[1,256]{1,0:T(1,128)} %refs_1_.1, ...), custom_call_target="tpu_custom_call" | custom-call | tf_op jit(solution)/shard_map/pallas_call | solution.py:1346
  190.1 4.3 %shard_map.272 = (bf16[256,1024]{1,0:T(8,128)(2,1)}, f32[256,1024]{1,0:T(8,128)}, f32[32,3072]{1,0:T(8,128)}, f32[32,1024]{1,0:T(8,128)}, f32[32,4096]{1,0:T(8,1...) custom-call(f32[16,128]{1,0:T(8,128)} %get-tuple-element.37.refs_0_,, ...), custom_call_target="tpu_custom_call" | custom-call | tf_op jit(solution)/shard_map/pallas_call | solution.py:1211
  (7 shorter events, 0.1 us)
Async XLA Ops:
  0.7 0.7 copy-start.8
  1.4 0.7 copy-start.7
  1.4 0.7 copy-start.3
  1.4 0.7 copy-start.4
  1.4 0.7 copy-start.5
  1.4 0.7 copy-start.6
  1.5 0.7 copy-start
  1.5 0.7 copy-start.1
  1.5 0.7 copy-start.2

commit v5 on v4

--- a/solution.py
+++ b/solution.py
@@ -255,17 +255,17 @@
                 p_send.at[self.index, k], p_recv.at[self.index, k], s, partner,
             )
 
-        def start_far(self, own=None):
+        def start_far(self, own=None, across=True):
             self.piece(mid_o, 1, seen_as, z, own).start()
-
-            @pl.when(is_mid == 0)
-            def _():
-                self.piece(near, 0, 0, z, own).start()
-
-            self.across(3, f, own).start()
-
-        def start_near(self, own=None):
-            @pl.when(is_mid == 1)
+            if across:
+                @pl.when(is_mid == 0)
+                def _():
+                    self.piece(near, 0, 0, z, own).start()
+
+                self.across(3, f, own).start()
+
+        def start_near(self, own=None, everyone=False):
+            @pl.when((is_mid == 1) | everyone)
             def _():
                 self.piece(near, 0, 0, z, own).start()
 
@@ -339,18 +339,17 @@
             self.pair(to_z).wait_recv()
             self.add(2 * to_z + c, self.land_p, to_z)
 
-        def first(self):
-            for slot, of_z in ((1, mid_o), (2, end_o), (0, near)):
+        def far(self):
+            for slot, of_z in ((1, mid_o), (2, end_o)):
                 self.add_pair(of_z)
 
                 @pl.when(is_mid == 0)
                 def _(slot=slot, of_z=of_z):
                     self.along(slot, near, of_z, slot).start()
 
-            @pl.when(is_mid == 1)
-            def _():
-                self.along(0, near, near, 0).start()
-
+        def close(self):
+            self.add_pair(near)
+            self.along(0, near, near, 0).start()
             self.add_pair(z)
 
         def second(self):
@@ -377,27 +376,6 @@
             lax.fori_loop(0, n_f // 2, one, 0)
             for i in range(3):
                 self.along(i, near, near, 0).wait_send()
-
-    class Direct(Shed):
-        def first(self):
-            for d in (2, 1, 3):
-                to_z = (z + d) % (n_f // 2)
-                self.add_pair(to_z)
-                self.along(d - 1, to_z, to_z, d - 1).start()
-            self.add_pair(z)
-
-        def second(self):
-            pass
-
-        def wait(self):
-            for d in (1, 2, 3):
-                self.along(d - 1, near, z, d - 1).wait_recv()
-
-        def total(self, at):
-            value = self.gw[f, at].astype(F32)
-            for d in (1, 2, 3):
-                value = value + self.land_z[d - 1, at].astype(F32)
-            return value
 
     barrier = pltpu.get_barrier_semaphore()
     for who in (sx, sy, sd):
@@ -455,8 +433,7 @@
         for p in range(n_cut):
             for k, to in enumerate(others):
                 qkv_copy(k, p, to).start()
-        for k, to in enumerate(others):
-            up_copy(k, to).start()
+        ag_tok.start(tokens)
         for p in range(n_cut):
             qkv_copy(-1, p, s).start()
         up_copy(-1, s).start()
@@ -506,17 +483,46 @@
 
         for k, to in enumerate(others):
             small_wide(k, to).start()
-        ag_tok.start(tokens)
         for p in range(n_cut):
             qkv_copy(-1, p, s).wait()
             for k, to in enumerate(others):
                 qkv_copy(k, p, to).wait_recv()
         for weight in w_qkv:
-            weight.start()
+            weight.start_far(across=False)
+        for weight in w_qkv:
+            weight.start_near(everyone=True)
+            weight.across(3, f).start()
         w_out.start(out_in)
-        up_copy(-1, s).wait()
+        w_down.start_far(down_in)
+    else:
+        ag_tok.start(tokens)
+        params[...] = small_in[0:8]
+        bias_row[...] = small_in[8:9, 0 : bias_row.shape[1]]
+
+    zero_row = jnp.zeros((1, width), F32)
+
+    def both(run, count):
+        def step(h, carry):
+            return tuple(a + b for a, b in zip(carry, run(h)))
+
+        return lax.fori_loop(0, 2, step, (zero_row,) * count)
+
+    def far_first(i):
+        return (1 - i // 2) + 2 * (1 - i % 2)
+
+    def param(i):
+        return params[i : i + 1, :]
+
+    tok_own.wait()
+    if inside:
+        w_qkv[0].relay()
+    ag_tok.relay()
+    if inside:
         for k, to in enumerate(others):
-            up_copy(k, to).wait_recv()
+            up_copy(k, to).start()
+        w_qkv[1].relay()
+        w_out.relay(False)
+        w_down.start_near(down_in)
         for k, who in enumerate(others):
             remote(
                 small_s.at[who], small_s.at[who], ss_send.at[k], ss_recv.at[k], who, f
@@ -524,31 +530,6 @@
         for b in range(4):
             for t in range(per):
                 params[:, pl.ds((b * per + t) * 128, 128)] = small_s[b, t]
-    else:
-        ag_tok.start(tokens)
-        params[...] = small_in[0:8]
-        bias_row[...] = small_in[8:9, 0 : bias_row.shape[1]]
-
-    zero_row = jnp.zeros((1, width), F32)
-
-    def both(run, count):
-        def step(h, carry):
-            return tuple(a + b for a, b in zip(carry, run(h)))
-
-        return lax.fori_loop(0, 2, step, (zero_row,) * count)
-
-    def far_first(i):
-        return (1 - i // 2) + 2 * (1 - i % 2)
-
-    def param(i):
-        return params[i : i + 1, :]
-
-    tok_own.wait()
-    if inside:
-        w_qkv[0].relay()
-    ag_tok.relay()
-    if inside:
-        w_up.start_far()
 
     def first_norm(b):
         unit, _s = unit_of(tok[b].astype(F32))
@@ -570,21 +551,14 @@
         first_norm(block(k))
         return 0
 
-    lax.fori_loop(0, 1, norm_step, 0)
-    if inside:
-        w_qkv[1].relay()
-        w_out.relay(False)
-        w_up.start_near()
-        w_down.start_far(down_in)
-    lax.fori_loop(1, 4, norm_step, 0)
+    lax.fori_loop(0, 3, norm_step, 0)
     if inside:
         for weight in w_qkv:
             weight.rest()
+    lax.fori_loop(3, 4, norm_step, 0)
+    if inside:
         for weight in w_qkv:
             weight.finish()
-    else:
-        for load in loads:
-            load.wait()
 
     rest = normed[...].reshape(4 * rows, width)
     for p in range(pairs):
@@ -594,11 +568,13 @@
             piece = piece if q else piece * 0.125
             at = slice((3 * p + q) * 128, (3 * p + q + 1) * 128)
             triple[:, :, at] = piece.astype(BF16).reshape(4, rows, 128)
-    if inside:
-        out_own.wait()
-        w_out.relay_rest()
-        w_out.rest()
-        w_out.finish()
+
+    if inside:
+        up_copy(-1, s).wait()
+        for k, to in enumerate(others):
+            up_copy(k, to).wait_recv()
+        w_up.start_far()
+        w_up.start_near()
 
     seg_own.wait()
     for k, who in enumerate(others):
@@ -661,6 +637,14 @@
                 for p in range(pairs):
                     attend_pair(r, r + 1 - count, count, p)
 
+        if inside:
+            @pl.when(i == 0)
+            def _():
+                out_own.wait()
+                w_out.relay_rest()
+                w_out.rest()
+                w_out.finish()
+
         part[rel] = dot(attended[r], out_w[0]).astype(BF16)
 
         @pl.when(c == 0)
@@ -670,8 +654,7 @@
         if inside:
             @pl.when(i == 1)
             def _():
-                w_up.relay()
-                w_down.start_near(down_in)
+                w_down.relay()
 
         return 0
 
@@ -686,11 +669,11 @@
 
     rs_1.relay()
     if inside:
-        w_down.relay()
+        w_up.relay()
 
         @pl.when(c == 1)
         def _():
-            w_up.rest()
+            w_down.rest()
 
     rs_1.wait()
 
@@ -711,8 +694,15 @@
     ag_inner.start()
     rs_1.drain()
     if inside:
+        @pl.when(c == 1)
+        def _():
+            w_up.rest()
+
+    ag_inner.relay()
+    if inside:
         @pl.when(c == 0)
         def _():
+            w_down.rest()
             w_up.rest()
 
         w_up.finish()
@@ -722,27 +712,14 @@
     rs_2 = Scatter(land_b, 1)
 
     def forward_step(k, _):
-        if inside:
-            @pl.when((k == 1) & (c == 1))
-            def _():
-                ag_inner.relay()
-                w_down.rest()
-                ag_inner.wait_x()
-
-            @pl.when((k == 1) & (c == 0))
-            def _():
-                ag_inner.relay()
-                ag_inner.wait_x()
-
-            @pl.when((k == 2) & (c == 0))
-            def _():
-                w_down.rest()
-
-            @pl.when(k > 1)
-            def _():
-                ag_inner.step(k)
-        else:
+        @pl.when(k == 1)
+        def _():
+            ag_inner.wait_x()
+
+        @pl.when(k > 1)
+        def _():
             ag_inner.step(k)
+
         r = block(k)
 
         def column(n, _):
@@ -808,7 +785,51 @@
 
     lax.fori_loop(0, ff // tile, clear, 0)
 
+    TN = ((0,), (0,))
+
+    def flat(ref, lanes=slice(None)):
+        held = ref[:, :, lanes]
+        return held.reshape(4 * rows, held.shape[2])
+
+    def all_pairs(shed):
+        for to_z in range(n_f // 2):
+            shed.pair(to_z).start()
+
+    def cut_grads(left, right, gw, shed, lanes=slice(None)):
+        for b in range(4):
+            value = dot(flat(left, slice(b * rows, (b + 1) * rows)), flat(right, lanes), TN)
+            gw[:, b * high : (b + 1) * high, :] = value.astype(BF16).reshape(n_f, high, -1)
+        all_pairs(shed)
+
+    def down_grads(rels):
+        each = ff // n_f
+        count = 256 // each
+        for b in range(n_f // count):
+            at = slice(b * count, (b + 1) * count)
+            cols = slice(b * 256, (b + 1) * 256)
+            value = dot(activ[block(rels[0]), :, cols], gmix[block(rels[0])], TN)
+            for rel in rels[1:]:
+                value = value + dot(activ[block(rel), :, cols], gmix[block(rel)], TN)
+            if len(rels) == 1:
+                value = value + gw_down[at].astype(F32).reshape(256, width)
+            gw_down[at] = value.astype(BF16).reshape(count, each, width)
+
+    if inside:
+        shed_down = Shed(0, gw_down, lp_down, lz_down)
+        shed_up = Shed(1, gw_up, lp_up, lz_up)
+        shed_out = Shed(2, gw_out, lp_out, lz_out)
+        shed_qkv = [
+            Shed(3 + p, gw_qkv[p], lp_qkv[p], lz_qkv[p])
+            for p in range(pairs)
+        ]
+        ag_tok.drain()
+
     def back_step(k, _):
+        if inside:
+            @pl.when(k == 3)
+            def _():
+                down_grads((0, 1, 2))
+
         ag_mix.step(k)
         r = block(k)
 
@@ -825,45 +846,13 @@
 
     lax.fori_loop(0, 4, back_step, 0)
 
-    TN = ((0,), (0,))
-
-    def flat(ref, lanes=slice(None)):
-        held = ref[:, :, lanes]
-        return held.reshape(4 * rows, held.shape[2])
-
-    def all_pairs(shed):
-        for to_z in range(n_f // 2):
-            shed.pair(to_z).start()
-
-    def cut_grads(left, right, gw, shed, lanes=slice(None)):
-        for b in range(4):
-            value = dot(flat(left, slice(b * rows, (b + 1) * rows)), flat(right, lanes), TN)
-            gw[:, b * high : (b + 1) * high, :] = value.astype(BF16).reshape(n_f, high, -1)
-        all_pairs(shed)
-
-    def row_grads(left, right, gw, shed):
-        each = left.shape[2] // n_f
-        most = max(each, 256)
-        for b in range(left.shape[2] // most):
-            value = dot(flat(left, slice(b * most, (b + 1) * most)), flat(right), TN)
-            count = most // each
-            gw[b * count : (b + 1) * count] = value.astype(BF16).reshape(count, each, -1)
-        all_pairs(shed)
-
-    if inside:
-        shed_down = Shed(0, gw_down, lp_down, lz_down)
-        shed_up = Shed(1, gw_up, lp_up, lz_up)
-        shed_out = Shed(2, gw_out, lp_out, lz_out)
-        shed_qkv = [
-            (Shed if p < pairs - 1 else Direct)(3 + p, gw_qkv[p], lp_qkv[p], lz_qkv[p])
-            for p in range(pairs)
-        ]
-        ag_tok.drain()
-        row_grads(activ, gmix, gw_down, shed_down)
+    if inside:
+        down_grads((3,))
+        all_pairs(shed_down)
 
         @pl.when(c == 1)
         def _():
-            shed_down.first()
+            shed_down.far()
 
     def inner_step(i, _):
         rel = far_first(i)
@@ -882,11 +871,13 @@
     if inside:
         @pl.when(c == 1)
         def _():
-            shed_up.first()
+            shed_up.far()
+            shed_down.close()
+            shed_up.close()
 
         @pl.when(c == 0)
         def _():
-            shed_down.first()
+            shed_down.far()
 
     rs_3.wait()
 
@@ -914,7 +905,9 @@
 
             @pl.when((k == 1) & (c == 0))
             def _():
-                shed_up.first()
+                shed_up.far()
+                shed_down.close()
+                shed_up.close()
 
             @pl.when(k == 1)
             def _():
@@ -1048,12 +1041,32 @@
             at = slice((3 * p + 2) * 128, (3 * p + 3) * 128)
             gtri[b, :, at] = dvt[lanes, span].astype(BF16).T
 
+    def qkv_grads(p):
+        cut_grads(normed, gtri, gw_qkv[p], shed_qkv[p], slice(p * 384, (p + 1) * 384))
+
     for p in range(pairs):
         back_pair(p)
-        if inside:
-            cut_grads(normed, gtri, gw_qkv[p], shed_qkv[p], slice(p * 384, (p + 1) * 384))
-            if p == 0:
-                shed_up.second()
+        if inside and p == 0:
+            qkv_grads(p)
+            shed_up.second()
+
+            @pl.when(c == 1)
+            def _():
+                shed_out.far()
+                shed_qkv[0].far()
+
+    if inside:
+        @pl.when(c == 1)
+        def _():
+            qkv_grads(1)
+            shed_qkv[1].far()
+            for shed in (shed_out, *shed_qkv):
+                shed.close()
+
+        @pl.when(c == 0)
+        def _():
+            shed_out.far()
+            shed_qkv[0].far()
 
     rs_4 = Scatter(land_b, 3)
 
@@ -1066,39 +1079,54 @@
         unit, _s = unit_of(tok[r].astype(F32))
         return carry[0] + col_sum(grad * unit), carry[1] + col_sum(grad)
 
-    if inside:
-        @pl.when(c == 1)
-        def _():
-            for shed in (*shed_qkv, shed_out):
-                shed.first()
-
     my_turn()
     sg_rows[0], sg_rows[1] = lax.fori_loop(0, 4, normed_step, (zero_row, zero_row))
     if inside:
+        small_first()
+
         @pl.when(c == 0)
         def _():
-            shed_qkv[0].first()
+            qkv_grads(1)
 
     rs_4.relay()
     if inside:
         @pl.when(c == 0)
         def _():
-            for shed in (*shed_qkv[1:], shed_out):
-                shed.first()
-
-        small_first()
-        shed_qkv[0].second()
+            shed_qkv[1].far()
+            for shed in (shed_out, *shed_qkv):
+                shed.close()
+
+        for shed in (shed_out, *shed_qkv):
+            shed.second()
+        small_second()
+        at = pl.ds(pl.multiple_of(s * high, high), high)
         shed_up.wait()
         for b in range(4):
             fin_up[b] = shed_up.total(slice(b * high, (b + 1) * high)).astype(BF16)
-        for k, to in enumerate(others):
-            gu_copy(k, to, s).start()
-        at = pl.ds(pl.multiple_of(s * high, high), high)
         gup_v[:, pl.ds(pl.multiple_of(s * ff, 128), ff)] = shed_up.total(at)
-        small_second()
+
+        def give_up():
+            for k, to in enumerate(others):
+                gu_copy(k, to, s).start()
+
+        @pl.when(c == 1)
+        def _():
+            give_up()
+
         shed_down.wait()
         fin_down[...] = shed_down.total(slice(None))
         gdown_out.start()
+    rs_4.wait()
+
+    def first_back(h, _):
+        at = half_rows(h)
+        unit, scale = unit_of(tok[s, at].astype(F32))
+        gmid[at] = gmid[at] + pull_of(rs_4.total(h), param(0), unit, scale)
+        pltpu.make_async_copy(gmid.at[at], tgrad.at[at], o_sem.at[h]).start()
+        return 0
+
+    lax.fori_loop(0, 2, first_back, 0)
+    if inside:
         for q, shed in enumerate(shed_qkv):
             shed.wait()
             for b in range(4):
@@ -1108,26 +1136,19 @@
             own = shed.total(at)
             for p in range(3):
                 gqkv_v[:, gc_at(3 * q + p, s)] = own[:, p * 128 : (p + 1) * 128]
+
+        @pl.when(c == 0)
+        def _():
+            give_up()
+
         for k, who in enumerate(others):
             gu_copy(k, who, who).wait_recv()
             gup_v[:, pl.ds(pl.multiple_of(who * ff, 128), ff)] = land_up[who].astype(F32)
         gup_out.start()
-        small_third()
-        shed_out.second()
-    rs_4.wait()
-
-    def first_back(h, _):
-        at = half_rows(h)
-        unit, scale = unit_of(tok[s, at].astype(F32))
-        gmid[at] = gmid[at] + pull_of(rs_4.total(h), param(0), unit, scale)
-        pltpu.make_async_copy(gmid.at[at], tgrad.at[at], o_sem.at[h]).start()
-        return 0
-
-    lax.fori_loop(0, 2, first_back, 0)
-    if inside:
         shed_out.wait()
         fin_out[...] = shed_out.total(slice(None))
         gout_out.start()
+        small_third()
         for k, who in enumerate(others):
             for q in range(pairs):
                 gc_copy(k, q, who, who).wait_recv()

time: 195 us -> 189 us (0.969)
  Pallas kernels: 191 us -> 184 us
    pallas_call x1, Pallas kernels: 187 us -> 180 us  [on_device(): pl.pallas_call(kernel, out_shape=[jax.ShapeDtypeStruct(*shape) for shape...]
where the time goes in v5:
time: 189 us; the launch traced here: 187 us
  Pallas kernels  184 us (97%)
    pallas_call x1, Pallas kernels, on_device(): pl.pallas_call(kernel, out_shape=[jax.ShapeDtypeStruct(*shape) for shape...  180 us
    pallas_call x1, Pallas kernels, finish(): pl.pallas_call(partial(finish_kernel, n_f, 6), out_shape=[jax.ShapeDtypeS...  4.35 us

profile of v5, /device:TPU:0, one launch (start us, length us, event | category | flops | bytes accessed | tf_op | source)
XLA Modules:
  0.0 187.2 jit_solution(12505386852817444578)
XLA Ops:
  0.7 0.0 copy-start.8
  0.7 0.6 copy-done.8
  1.3 0.1 pad.2.clone
  1.4 0.0 copy-start.7
  1.4 0.0 copy-start.3
  1.4 0.0 copy-start.4
  1.4 0.0 copy-start.5
  1.4 0.0 copy-start.6
  1.5 0.0 copy-start
  1.5 0.0 copy-start.1
  1.5 0.0 copy-start.2
  1.5 0.6 copy-done.7
  2.1 0.0 copy-done.3
  2.1 0.0 copy-done.4
  2.1 0.0 copy-done.5
  2.1 0.0 copy-done.6
  2.1 0.0 copy-done
  2.1 0.0 copy-done.1
  2.2 0.0 copy-done.2
  2.2 0.1 tile.10
  2.3 0.7 maximum_maximum_fusion.refs_2_
  3.0 179.7 %shard_map.271 = (bf16[256,1024]{1,0:T(8,128)(2,1)}, f32[256,1024]{1,0:T(8,128)}, f32[32,3072]{1,0:T(8,128)}, f32[32,1024]{1,0:T(8,128)}, f32[32,4096]{1,0:T(8,1...) custom-call(bf16[256,1024]{1,0:T(8,128)(2,1)} %bitcast.24, s32[1,256]{1,0:T(1,128)} %refs_1_.1, ...), custom_call_target="tpu_custom_call" | custom-call | tf_op jit(solution)/shard_map/pallas_call | solution.py:1367
  182.7 4.3 %shard_map.272 = (bf16[256,1024]{1,0:T(8,128)(2,1)}, f32[256,1024]{1,0:T(8,128)}, f32[32,3072]{1,0:T(8,128)}, f32[32,1024]{1,0:T(8,128)}, f32[32,4096]{1,0:T(8,1...) custom-call(f32[16,128]{1,0:T(8,128)} %get-tuple-element.37.refs_0_,, ...), custom_call_target="tpu_custom_call" | custom-call | tf_op jit(solution)/shard_map/pallas_call | solution.py:1232
  (7 shorter events, 0.1 us)
Async XLA Ops:
  0.7 0.7 copy-start.8
  1.4 0.7 copy-start.7
  1.4 0.7 copy-start.3
  1.4 0.7 copy-start.4
  1.4 0.7 copy-start.5
  1.4 0.7 copy-start.6
  1.5 0.7 copy-start
  1.5 0.7 copy-start.1
  1.5 0.7 copy-start.2

commit v6 on v5

--- a/solution.py
+++ b/solution.py
@@ -39,7 +39,7 @@
 def layer_kernel(
     inside,
     n_f,
-    tokens, seg_in, small_in, cot_in, qkv_in, out_in, up_in, down_in,
+    tokens, seg_in, small_given, cot_in, qkv_in, out_in, up_in, down_in,
     result, tgrad, gqkv, gout, gup, gdown, gsmall,
     tok, normed, inner, gmix, gbr,
     qkv_w, out_w, up_w, down_w,
@@ -61,6 +61,7 @@
     gp_send, gp_recv, gz_send, gz_recv,
     gc_send, gc_recv, gu_send, gu_recv,
     ts_send, ts_recv, tf_send, tf_recv, turn,
+    small_raw, bias_raw, small_rows, small_tile, raw_sem,
 ):
     gw_qkv, lp_qkv, lz_qkv = (gw_q0, gw_q1), (lp_q0, lp_q1), (lz_q0, lz_q1)
     rows, width = tokens.shape
@@ -377,6 +378,15 @@
             for i in range(3):
                 self.along(i, near, near, 0).wait_send()
 
+    if inside:
+        fetch = [
+            pltpu.make_async_copy(ref, small_raw.at[i], raw_sem.at[i])
+            for i, ref in enumerate(small_given[:8])
+        ]
+        fetch.append(pltpu.make_async_copy(small_given[8], bias_raw, raw_sem.at[8]))
+        for one in fetch:
+            one.start()
+
     barrier = pltpu.get_barrier_semaphore()
     for who in (sx, sy, sd):
         pl.semaphore_signal(barrier, inc=1, device_id=(who, f), device_id_type=pl.DeviceIdType.MESH)
@@ -387,6 +397,20 @@
                 barrier, inc=1, device_id=(s, (f + d) % n_f), device_id_type=pl.DeviceIdType.MESH
             )
         n_peers += n_f - 1
+    if inside:
+        for one in fetch:
+            one.wait()
+        for i in range(8):
+            small_rows[i : i + 1, :] = small_raw[i].astype(F32)
+        tall = small_rows.shape[1]
+        lanes = lax.broadcasted_iota(jnp.int32, (tall, 128), 1)
+        places = lax.broadcasted_iota(jnp.int32, (tall, 128), 0) + (f % (128 // tall)) * tall
+        chosen = jnp.where(lanes == places, 1.0, 0.0).astype(BF16)
+        small_in = small_tile
+        small_in[0:8] = dot(small_rows[...].astype(BF16), chosen)
+        small_in[8:9] = bias_raw[...].astype(F32)
+    else:
+        small_in = small_given[0]
     pl.semaphore_wait(barrier, n_peers)
 
     others = (sx, sy, sd)
@@ -641,8 +665,6 @@
             @pl.when(i == 0)
             def _():
                 out_own.wait()
-                w_out.relay_rest()
-                w_out.rest()
                 w_out.finish()
 
         part[rel] = dot(attended[r], out_w[0]).astype(BF16)
@@ -650,6 +672,10 @@
         @pl.when(c == 0)
         def _():
             rs_1.step(rel)
+
+        @pl.when((c == 1) & (i == 2))
+        def _():
+            rs_1.step(3)
 
         if inside:
             @pl.when(i == 1)
@@ -658,13 +684,16 @@
 
         return 0
 
+    if inside:
+        w_out.relay_rest()
+        w_out.rest()
     lax.fori_loop(0, 4, attend, 0)
 
     my_turn((1, 1))
 
     @pl.when(c == 1)
     def _():
-        for i in (0, 2, 1, 3):
+        for i in (1, 3):
             rs_1.copy(i).start()
 
     rs_1.relay()
@@ -708,7 +737,7 @@
         w_up.finish()
 
     ff = up_w.shape[2]
-    tile = 512
+    tile = ff
     rs_2 = Scatter(land_b, 1)
 
     def forward_step(k, _):
@@ -942,6 +971,11 @@
     if inside:
         gw_out[...] = branch[...].astype(BF16).reshape(gw_out.shape)
         all_pairs(shed_out)
+
+        @pl.when(c == 1)
+        def _():
+            shed_out.far()
+            shed_out.close()
 
     if inside:
         per = n_f * high // 128
@@ -1052,7 +1086,6 @@
 
             @pl.when(c == 1)
             def _():
-                shed_out.far()
                 shed_qkv[0].far()
 
     if inside:
@@ -1060,7 +1093,7 @@
         def _():
             qkv_grads(1)
             shed_qkv[1].far()
-            for shed in (shed_out, *shed_qkv):
+            for shed in shed_qkv:
                 shed.close()
 
         @pl.when(c == 0)
@@ -1255,18 +1288,15 @@
     window = rows * min(n_seq, 1 + -(-511 // rows))
     inside = n_f == 8 and high % 32 == 0
     f = lax.axis_index("fsdp")
-    small = jnp.stack([v.astype(F32) for v in vectors])
-    if inside:
-        each = 128 // high
-        lane = lax.broadcasted_iota(jnp.int32, (8, 128), 1) // high
-        small = jnp.where(lane == f % each, jnp.tile(small, (1, each)), 0.0)
-        small = jnp.concatenate([small, up_bias.astype(F32)[None], jnp.zeros((7, 128), F32)])
+    if inside:
+        small = [v[None] for v in (*vectors, up_bias)]
         weights = (qkv_weight, out_weight, up_weight, down_weight)
     else:
+        small = jnp.stack([v.astype(F32) for v in vectors])
         small = lax.all_gather(small, ("seq", "fsdp"), axis=1, tiled=True)
         bias = lax.all_gather(up_bias.astype(F32), "fsdp", axis=0, tiled=True)
         bias = jnp.pad(bias[None], ((0, 7), (0, width - ff)))
-        small = jnp.concatenate([small, bias])
+        small = [jnp.concatenate([small, bias])]
 
         def columns(weight, parts):
             cut = weight.reshape(high, parts, n_seq, -1, 128).transpose(2, 0, 3, 1, 4)
@@ -1341,6 +1371,11 @@
     ):
         scratch[name] = dma(shape)
     scratch["turn"] = pltpu.SemaphoreType.REGULAR
+    scratch["small_raw"] = vmem((8, 1, high), BF16)
+    scratch["bias_raw"] = vmem((1, up_bias.shape[0]), BF16)
+    scratch["small_rows"] = vmem((8, high), F32)
+    scratch["small_tile"] = vmem((16, 128), F32)
+    scratch["raw_sem"] = dma((9,))
     outs = {
         "result": ((rows, width), BF16), "tgrad": ((rows, width), F32),
         "gqkv": ((high, n_seq * 3 * group), F32), "gout": ((high, width), F32),
@@ -1356,10 +1391,11 @@
     names = list(scratch)
 
     def kernel(*refs):
-        given = refs[:8]
-        made = refs[8 : 8 + len(outs)]
-        more = dict(zip(extra, refs[8 + len(outs) :]))
-        rest = refs[8 + len(outs) + len(extra) :]
+        n_in = 7 + len(small)
+        given = (*refs[:2], refs[2 : 2 + len(small)], *refs[2 + len(small) : n_in])
+        made = refs[n_in : n_in + len(outs)]
+        more = dict(zip(extra, refs[n_in + len(outs) :]))
+        rest = refs[n_in + len(outs) + len(extra) :]
         more.update(zip([n for n in names if scratch[n] is not None], rest))
         layer_kernel(inside, n_f, *given, *made, *[more[n] for n in names])
 
@@ -1367,13 +1403,13 @@
     made = pl.pallas_call(
         kernel,
         out_shape=[jax.ShapeDtypeStruct(*shape) for shape in shapes],
-        in_specs=[anywhere, anywhere, whole, anywhere] + [anywhere] * 4,
+        in_specs=[anywhere] * 2 + [anywhere if inside else whole] * len(small) + [anywhere] * 5,
         out_specs=[anywhere] * len(outs) + [whole] * len(extra),
         scratch_shapes=[scratch[n] for n in names if scratch[n] is not None],
         compiler_params=pltpu.CompilerParams(
             collective_id=0, has_side_effects=True, vmem_limit_bytes=67043328
         ),
-    )(tokens[0], segments, small, cotangent[0], *weights)
+    )(tokens[0], segments, *small, cotangent[0], *weights)
     result, tgrad, gqkv, gout, gup, gdown, gsmall = made[:7]
     if inside:
         return finish(n_f, high, *made[:7])

time: 189 us -> 186 us (0.984)
  no operation moved by 1% of the time
where the time goes in v6:
time: 186 us; the launch traced here: 183 us
  Pallas kernels  183 us (98%)
    pallas_call x1, Pallas kernels, on_device(): pl.pallas_call(kernel, out_shape=[jax.ShapeDtypeStruct(*shape) for shape...  178 us
    pallas_call x1, Pallas kernels, finish(): pl.pallas_call(partial(finish_kernel, n_f, 6), out_shape=[jax.ShapeDtypeS...  4.35 us

profile of v6, /device:TPU:0, one launch (start us, length us, event | category | flops | bytes accessed | tf_op | source)
XLA Modules:
  0.0 183.5 jit_solution(2485171322827525809)
XLA Ops:
  0.7 178.3 %shard_map.271 = (bf16[256,1024]{1,0:T(8,128)(2,1)}, f32[256,1024]{1,0:T(8,128)}, f32[32,3072]{1,0:T(8,128)}, f32[32,1024]{1,0:T(8,128)}, f32[32,4096]{1,0:T(8,1...) custom-call(bf16[256,1024]{1,0:T(8,128)(2,1)} %bitcast.22, s32[1,256]{1,0:T(1,128)} %refs_1_.1, bf16[1,32]{1,0:T(2,128)(2,1)} %bitcast.24, ...), custom_call_target="tpu_custom_call" | custom-call | tf_op jit(solution)/shard_map/pallas_call | solution.py:1403
  178.9 4.3 %shard_map.272 = (bf16[256,1024]{1,0:T(8,128)(2,1)}, f32[256,1024]{1,0:T(8,128)}, f32[32,3072]{1,0:T(8,128)}, f32[32,1024]{1,0:T(8,128)}, f32[32,4096]{1,0:T(8,1...) custom-call(f32[16,128]{1,0:T(8,128)} %get-tuple-element.37.refs_0_,, ...), custom_call_target="tpu_custom_call" | custom-call | tf_op jit(solution)/shard_map/pallas_call | solution.py:1265

commit v7 on v6

--- a/solution.py
+++ b/solution.py
@@ -51,7 +51,7 @@
     gw_q0, gw_q1, gw_out, gw_up, gw_down,
     lp_q0, lp_q1, lp_out, lp_up, lp_down,
     lz_q0, lz_q1, lz_out, lz_up, lz_down,
-    result_v, fin_qkv, fin_up, land_qkv, land_up, fin_down, fin_out, gup_v, gqkv_v, small_sum,
+    fin_qkv, land_qkv, small_sum,
     sg_s, sg_land_s, sg_f, sg_land_f,
     ag_send, ag_recv, rs_send, rs_recv,
     w_send, w_recv, p_send, p_recv,
@@ -641,16 +641,23 @@
 
     rs_1 = Scatter(land_a, 0)
 
-    def attend_pair(r, first, count, p):
-        query, keys, vals = cut(r, 0, p, 1), cut(first, 1, p, count), cut(first, 2, p, count)
-        outs = []
-        for e in range(2):
-            scores = masked(dot(query * sides[e], keys, NT), r, first, count)
-            expo = jnp.exp(scores - jnp.max(scores, -1, keepdims=True))
-            low = (expo * (1.0 / jnp.sum(expo, -1, keepdims=True))).astype(BF16)
-            probs[r, 2 * p + e, :, 0 : count * rows] = low
-            outs.append(dot(low, vals))
-        attended[r, :, p * 128 : (p + 1) * 128] = jnp.where(pick, outs[0], outs[1]).astype(BF16)
+    def attend_heads(r, first, count):
+        scores, values = [], []
+        for p in range(pairs):
+            query, keys = cut(r, 0, p, 1), cut(first, 1, p, count)
+            for e in range(2):
+                scores.append(masked(dot(query * sides[e], keys, NT), r, first, count))
+                values.append(cut(first, 2, p, count))
+        tops = [jnp.max(score, -1, keepdims=True) for score in scores]
+        expos = [jnp.exp(score - top) for score, top in zip(scores, tops)]
+        sums = [jnp.sum(expo, -1, keepdims=True) for expo in expos]
+        lows = [(expo * (1.0 / total)).astype(BF16) for expo, total in zip(expos, sums)]
+        for n, low in enumerate(lows):
+            probs[r, n, :, 0 : count * rows] = low
+        outs = [dot(low, value) for low, value in zip(lows, values)]
+        for p in range(pairs):
+            both_sides = jnp.where(pick, outs[2 * p], outs[2 * p + 1])
+            attended[r, :, p * 128 : (p + 1) * 128] = both_sides.astype(BF16)
 
     def attend(i, _):
         rel = far_first(i)
@@ -658,8 +665,7 @@
         for count in range(1, blocks + 1):
             @pl.when(r + 1 >= count if count == blocks else r + 1 == count)
             def _(count=count):
-                for p in range(pairs):
-                    attend_pair(r, r + 1 - count, count, p)
+                attend_heads(r, r + 1 - count, count)
 
         if inside:
             @pl.when(i == 0)
@@ -789,7 +795,7 @@
     def last_norm(h):
         at = half_rows(h)
         unit, scale = unit_of(rs_2.total(h))
-        result_v[at] = (middle[at] + (unit * param(6) + param(7))).astype(BF16)
+        gbr[s, at] = (middle[at] + (unit * param(6) + param(7))).astype(BF16)
         grad = cot[at].astype(F32)
         gmix[s, at] = pull_of(grad, param(6), unit, scale).astype(BF16)
         return col_sum(grad * unit), col_sum(grad)
@@ -800,7 +806,7 @@
     ag_mix = Gather(gmix, 2)
     my_turn()
     ag_mix.start()
-    result_out = pltpu.make_async_copy(result_v, result, o_sem.at[2])
+    result_out = pltpu.make_async_copy(gbr.at[s], result, o_sem.at[2])
     result_out.start()
     rs_2.drain()
 
@@ -910,6 +916,8 @@
 
     rs_3.wait()
 
+    result_out.wait()
+
     def mid_back(h):
         at = half_rows(h)
         grad = rs_3.total(h)
@@ -979,10 +987,27 @@
 
     if inside:
         per = n_f * high // 128
+        fin_down = branch.at[0:high_d]
+        fin_out = branch.at[high_d : high_d + high]
         gdown_out = pltpu.make_async_copy(fin_down, gdown, o_sem.at[3])
         gout_out = pltpu.make_async_copy(fin_out, gout, o_sem.at[4])
-        gup_out = pltpu.make_async_copy(gup_v, gup, o_sem.at[5])
-        gqkv_out = pltpu.make_async_copy(gqkv_v, gqkv, o_sem.at[6])
+
+        def rows_at(n):
+            return pl.ds(pl.multiple_of(n * high, high), high)
+
+        gup_out = [
+            pltpu.make_async_copy(
+                middle.at[rows_at(b)], gup.at[:, b * ff : (b + 1) * ff], o_sem.at[8 + b]
+            )
+            for b in range(4)
+        ]
+        gqkv_out = [
+            pltpu.make_async_copy(
+                middle.at[rows_at(4 + p)], gqkv.at[:, p * width : (p + 1) * width],
+                o_sem.at[12 + p],
+            )
+            for p in range(3)
+        ]
         gsmall_out = pltpu.make_async_copy(small_sum, gsmall, o_sem.at[7])
 
         def ts_copy(k, to):
@@ -1025,11 +1050,16 @@
             gsmall_out.start()
 
         def gu_copy(k, to, who):
-            return remote(fin_up.at[to], land_up.at[who], gu_send.at[k], gu_recv.at[k], to, f)
-
-        def gc_at(p, who):
-            start = pl.multiple_of((p % 3) * width + who * group + (p // 3) * 128, 128)
-            return pl.ds(start, 128)
+            return remote(
+                cot.at[rows_at(to)], cot.at[rows_at(4 + who)],
+                gu_send.at[k], gu_recv.at[k], to, f,
+            )
+
+        def put_qkv(q, who, value):
+            lanes = pl.ds(pl.multiple_of(who * group + q * 128, 128), 128)
+            for p in range(3):
+                piece = value[:, p * 128 : (p + 1) * 128]
+                middle[rows_at(4 + p), lanes] = piece.astype(F32)
 
         def gc_copy(k, p, to, who):
             return remote(
@@ -1037,30 +1067,39 @@
                 gc_send.at[k, p], gc_recv.at[k, p], to, f,
             )
 
-    def back_pair(p):
+    def back_rows(p, r_group):
         lanes = slice(p * 128, (p + 1) * 128)
-        for r in range(3, -1, -1):
+        items = []
+        for r in r_group:
             first = max(r + 1 - blocks, 0)
             count = r + 1 - first
-            query, keys, vals = cut(r, 0, p, 1), cut(first, 1, p, count), cut(first, 2, p, count)
-            grad = gatt[r, :, lanes]
-            query_t, grad_t = query.T, grad.T
-            outs, key_parts, value_parts = [], [], []
+            query, grad = cut(r, 0, p, 1), gatt[r, :, lanes]
+            keys, vals = cut(first, 1, p, count), cut(first, 2, p, count)
             for e in range(2):
                 low = probs[r, 2 * p + e, :, 0 : count * rows]
-                grad_probs = dot(grad * sides[e], vals, NT)
-                full = low.astype(F32)
-                inner_sum = jnp.sum(full * grad_probs, -1, keepdims=True)
-                grad_scores = (full * (grad_probs - inner_sum)).astype(BF16)
-                outs.append(dot(grad_scores, keys))
+                items.append((r, e, first, count, query, keys, grad, low, vals))
+        pulled = [dot(grad * sides[e], vals, NT) for _, e, _, _, _, _, grad, _, vals in items]
+        sums = [
+            jnp.sum(item[7].astype(F32) * pull, -1, keepdims=True)
+            for item, pull in zip(items, pulled)
+        ]
+        slopes = [
+            (item[7].astype(F32) * (pull - total)).astype(BF16)
+            for item, pull, total in zip(items, pulled, sums)
+        ]
+        for n in range(0, len(items), 2):
+            r, _, first, count, query, keys, grad, _, _ = items[n]
+            query_t, grad_t = query.T, grad.T
+            outs = [dot(slopes[n + e], keys) for e in range(2)]
+            for e in range(2):
                 side = slice(e * HEAD_DIM, (e + 1) * HEAD_DIM)
                 here = slice(p * 128 + e * HEAD_DIM, p * 128 + (e + 1) * HEAD_DIM)
-                key_part = dot(query_t[side], grad_scores)
-                value_part = dot(grad_t[side], low)
-                for n in range(count):
-                    span = slice((first + n) * rows, (first + n + 1) * rows)
-                    cols = slice(n * rows, (n + 1) * rows)
-                    if r == 3 or (first + n) < 4 - blocks and r == first + n + blocks - 1:
+                key_part = dot(query_t[side], slopes[n + e])
+                value_part = dot(grad_t[side], items[n + e][7])
+                for m in range(count):
+                    span = slice((first + m) * rows, (first + m + 1) * rows)
+                    cols = slice(m * rows, (m + 1) * rows)
+                    if r == 3 or (first + m) < 4 - blocks and r == first + m + blocks - 1:
                         dkt[here, span] = key_part[:, cols]
                         dvt[here, span] = value_part[:, cols]
                     else:
@@ -1068,6 +1107,17 @@
                         dvt[here, span] = dvt[here, span] + value_part[:, cols]
             at = slice(3 * p * 128, (3 * p + 1) * 128)
             gtri[r, :, at] = (jnp.where(pick, outs[0], outs[1]) * 0.125).astype(BF16)
+
+    def back_pair(p):
+        lanes = slice(p * 128, (p + 1) * 128)
+        for r_group in ((3, 2), (1, 0)):
+            back_rows(p, r_group)
+            if inside and p and r_group[0] == 3:
+                @pl.when(c == 0)
+                def _():
+                    shed_out.far()
+                    shed_out.close()
+
         for b in range(4):
             span = slice(b * rows, (b + 1) * rows)
             at = slice((3 * p + 1) * 128, (3 * p + 2) * 128)
@@ -1098,7 +1148,6 @@
 
         @pl.when(c == 0)
         def _():
-            shed_out.far()
             shed_qkv[0].far()
 
     rs_4 = Scatter(land_b, 3)
@@ -1126,7 +1175,7 @@
         @pl.when(c == 0)
         def _():
             shed_qkv[1].far()
-            for shed in (shed_out, *shed_qkv):
+            for shed in shed_qkv:
                 shed.close()
 
         for shed in (shed_out, *shed_qkv):
@@ -1135,8 +1184,8 @@
         at = pl.ds(pl.multiple_of(s * high, high), high)
         shed_up.wait()
         for b in range(4):
-            fin_up[b] = shed_up.total(slice(b * high, (b + 1) * high)).astype(BF16)
-        gup_v[:, pl.ds(pl.multiple_of(s * ff, 128), ff)] = shed_up.total(at)
+            cot[rows_at(b)] = shed_up.total(slice(b * high, (b + 1) * high)).astype(BF16)
+        middle[rows_at(s)] = shed_up.total(at)
 
         def give_up():
             for k, to in enumerate(others):
@@ -1167,8 +1216,7 @@
             for k, to in enumerate(others):
                 gc_copy(k, q, to, s).start()
             own = shed.total(at)
-            for p in range(3):
-                gqkv_v[:, gc_at(3 * q + p, s)] = own[:, p * 128 : (p + 1) * 128]
+            put_qkv(q, s, own)
 
         @pl.when(c == 0)
         def _():
@@ -1176,8 +1224,9 @@
 
         for k, who in enumerate(others):
             gu_copy(k, who, who).wait_recv()
-            gup_v[:, pl.ds(pl.multiple_of(who * ff, 128), ff)] = land_up[who].astype(F32)
-        gup_out.start()
+            middle[rows_at(who)] = cot[rows_at(4 + who)].astype(F32)
+        for one in gup_out:
+            one.start()
         shed_out.wait()
         fin_out[...] = shed_out.total(slice(None))
         gout_out.start()
@@ -1185,20 +1234,18 @@
         for k, who in enumerate(others):
             for q in range(pairs):
                 gc_copy(k, q, who, who).wait_recv()
-                for p in range(3):
-                    piece = land_qkv[q, who, :, p * 128 : (p + 1) * 128]
-                    gqkv_v[:, gc_at(3 * q + p, who)] = piece.astype(F32)
-        gqkv_out.start()
+                put_qkv(q, who, land_qkv[q, who])
+        for one in gqkv_out:
+            one.start()
 
     for h in range(2):
         pltpu.make_async_copy(gmid.at[half_rows(h)], tgrad.at[half_rows(h)], o_sem.at[h]).wait()
-    result_out.wait()
     if inside:
         gsmall_out.wait()
         gdown_out.wait()
         gout_out.wait()
-        gup_out.wait()
-        gqkv_out.wait()
+        for one in (*gup_out, *gqkv_out):
+            one.wait()
         for k, to in enumerate(others):
             gu_copy(k, to, s).wait_send()
             ts_copy(k, to).wait_send()
@@ -1286,7 +1333,7 @@
     ff = up_weight.shape[1] // n_seq
     half = rows // 2
     window = rows * min(n_seq, 1 + -(-511 // rows))
-    inside = n_f == 8 and high % 32 == 0
+    inside = n_f == 8 and high % 32 == 0 and ff == width and 8 * high <= rows
     f = lax.axis_index("fsdp")
     if inside:
         small = [v[None] for v in (*vectors, up_bias)]
@@ -1343,15 +1390,8 @@
         scratch["lp_" + name] = vmem((n_f // 2 if inside else 1, tall if inside else 16, wide), BF16)
     for name, (tall, wide) in pieces.items():
         scratch["lz_" + name] = vmem((n_f // 2 if inside else 1, tall if inside else 16, wide), BF16)
-    scratch["result_v"] = vmem((rows, width), BF16)
     scratch["fin_qkv"] = vmem((group // 128, 4, high, 384), BF16)
-    scratch["fin_up"] = vmem((4, high, ff), BF16)
     scratch["land_qkv"] = vmem((group // 128, 4, high, 384), BF16)
-    scratch["land_up"] = vmem((4, high, ff), BF16)
-    scratch["fin_down"] = vmem((high_d, width), F32)
-    scratch["fin_out"] = vmem((high, width), F32)
-    scratch["gup_v"] = vmem((high, n_seq * ff), F32)
-    scratch["gqkv_v"] = vmem((high, n_seq * 3 * group), F32)
     scratch["small_sum"] = vmem((16, 128 if inside else width), F32)
     tiles = width // 512
     scratch["sg_s"] = vmem((4, tiles, 8, 128), F32)
@@ -1364,7 +1404,7 @@
         ("col_send", (3, n_cut)), ("col_recv", (3, n_cut)), ("col_local", (n_cut,)),
         ("upc_send", (3,)), ("upc_recv", (3,)), ("seg_send", (3,)), ("seg_recv", (3,)),
         ("sf_send", (8,)), ("sf_recv", (8,)), ("ss_send", (3,)), ("ss_recv", (3,)),
-        ("loc_sem", (7,)), ("o_sem", (8,)),
+        ("loc_sem", (7,)), ("o_sem", (16,)),
         ("gp_send", (5, 4)), ("gp_recv", (5, 4)), ("gz_send", (5, 4)), ("gz_recv", (5, 4)),
         ("gc_send", (3, 2)), ("gc_recv", (3, 2)), ("gu_send", (3,)), ("gu_recv", (3,)),
         ("ts_send", (3,)), ("ts_recv", (3,)), ("tf_send", (8,)), ("tf_recv", (8,)),

time: 186 us -> 182 us (0.978)
  Pallas kernels: 183 us -> 180 us
    pallas_call x1, Pallas kernels: 178 us -> 176 us  [on_device(): pl.pallas_call(kernel, out_shape=[jax.ShapeDtypeStruct(*shape) for shape...]
where the time goes in v7:
time: 182 us; the launch traced here: 181 us
  Pallas kernels  180 us (99%)
    pallas_call x1, Pallas kernels, on_device(): pl.pallas_call(kernel, out_shape=[jax.ShapeDtypeStruct(*shape) for shape...  176 us
    pallas_call x1, Pallas kernels, finish(): pl.pallas_call(partial(finish_kernel, n_f, 6), out_shape=[jax.ShapeDtypeS...  4.35 us

profile of v7, /device:TPU:0, one launch (start us, length us, event | category | flops | bytes accessed | tf_op | source)
XLA Modules:
  0.0 180.9 jit_solution(14624854478020355385)
XLA Ops:
  0.7 175.7 %shard_map.271 = (bf16[256,1024]{1,0:T(8,128)(2,1)}, f32[256,1024]{1,0:T(8,128)}, f32[32,3072]{1,0:T(8,128)}, f32[32,1024]{1,0:T(8,128)}, f32[32,4096]{1,0:T(8,1...) custom-call(bf16[256,1024]{1,0:T(8,128)(2,1)} %bitcast.22, s32[1,256]{1,0:T(1,128)} %refs_1_.1, bf16[1,32]{1,0:T(2,128)(2,1)} %bitcast.24, ...), custom_call_target="tpu_custom_call" | custom-call | tf_op jit(solution)/shard_map/pallas_call | solution.py:1443
  176.4 4.3 %shard_map.272 = (bf16[256,1024]{1,0:T(8,128)(2,1)}, f32[256,1024]{1,0:T(8,128)}, f32[32,3072]{1,0:T(8,128)}, f32[32,1024]{1,0:T(8,128)}, f32[32,4096]{1,0:T(8,1...) custom-call(f32[16,128]{1,0:T(8,128)} %get-tuple-element.37.refs_0_,, ...), custom_call_target="tpu_custom_call" | custom-call | tf_op jit(solution)/shard_map/pallas_call | solution.py:1312

commit v8 on v7

--- a/solution.py
+++ b/solution.py
@@ -1145,6 +1145,7 @@
             shed_qkv[1].far()
             for shed in shed_qkv:
                 shed.close()
+            shed_out.second()
 
         @pl.when(c == 0)
         def _():
@@ -1170,6 +1171,10 @@
         def _():
             qkv_grads(1)
 
+        @pl.when(c == 1)
+        def _():
+            shed_qkv[0].second()
+
     rs_4.relay()
     if inside:
         @pl.when(c == 0)
@@ -1178,8 +1183,12 @@
             for shed in shed_qkv:
                 shed.close()
 
-        for shed in (shed_out, *shed_qkv):
-            shed.second()
+        @pl.when(c == 0)
+        def _():
+            shed_out.second()
+            shed_qkv[0].second()
+
+        shed_qkv[1].second()
         small_second()
         at = pl.ds(pl.multiple_of(s * high, high), high)
         shed_up.wait()
@@ -1198,6 +1207,21 @@
         shed_down.wait()
         fin_down[...] = shed_down.total(slice(None))
         gdown_out.start()
+
+        def give_qkv(q):
+            shed = shed_qkv[q]
+            shed.wait()
+            for b in range(4):
+                fin_qkv[q, b] = shed.total(slice(b * high, (b + 1) * high)).astype(BF16)
+            for k, to in enumerate(others):
+                gc_copy(k, q, to, s).start()
+            put_qkv(q, s, shed.total(at))
+
+        @pl.when(c == 1)
+        def _():
+            give_qkv(0)
+            give_qkv(1)
+
     rs_4.wait()
 
     def first_back(h, _):
@@ -1209,18 +1233,11 @@
 
     lax.fori_loop(0, 2, first_back, 0)
     if inside:
-        for q, shed in enumerate(shed_qkv):
-            shed.wait()
-            for b in range(4):
-                fin_qkv[q, b] = shed.total(slice(b * high, (b + 1) * high)).astype(BF16)
-            for k, to in enumerate(others):
-                gc_copy(k, q, to, s).start()
-            own = shed.total(at)
-            put_qkv(q, s, own)
-
         @pl.when(c == 0)
         def _():
             give_up()
+            give_qkv(0)
+            give_qkv(1)
 
         for k, who in enumerate(others):
             gu_copy(k, who, who).wait_recv()

time: 182 us -> 181 us (level)
  no operation moved by 1% of the time
where the time goes in v8:
time: 181 us; the launch traced here: 180 us
  Pallas kernels  179 us (99%)
    pallas_call x1, Pallas kernels, on_device(): pl.pallas_call(kernel, out_shape=[jax.ShapeDtypeStruct(*shape) for shape...  175 us
    pallas_call x1, Pallas kernels, finish(): pl.pallas_call(partial(finish_kernel, n_f, 6), out_shape=[jax.ShapeDtypeS...  4.35 us

profile of v8, /device:TPU:0, one launch (start us, length us, event | category | flops | bytes accessed | tf_op | source)
XLA Modules:
  0.0 180.3 jit_solution(2758689716952139097)
XLA Ops:
  0.7 175.1 %shard_map.271 = (bf16[256,1024]{1,0:T(8,128)(2,1)}, f32[256,1024]{1,0:T(8,128)}, f32[32,3072]{1,0:T(8,128)}, f32[32,1024]{1,0:T(8,128)}, f32[32,4096]{1,0:T(8,1...) custom-call(bf16[256,1024]{1,0:T(8,128)(2,1)} %bitcast.22, s32[1,256]{1,0:T(1,128)} %refs_1_.1, bf16[1,32]{1,0:T(2,128)(2,1)} %bitcast.24, ...), custom_call_target="tpu_custom_call" | custom-call | tf_op jit(solution)/shard_map/pallas_call | solution.py:1460
  175.8 4.3 %shard_map.272 = (bf16[256,1024]{1,0:T(8,128)(2,1)}, f32[256,1024]{1,0:T(8,128)}, f32[32,3072]{1,0:T(8,128)}, f32[32,1024]{1,0:T(8,128)}, f32[32,4096]{1,0:T(8,1...) custom-call(f32[16,128]{1,0:T(8,128)} %get-tuple-element.37.refs_0_,, ...), custom_call_target="tpu_custom_call" | custom-call | tf_op jit(solution)/shard_map/pallas_call | solution.py:1329

commit v9 on v8

--- a/solution.py
+++ b/solution.py
@@ -126,10 +126,10 @@
         def relay(self):
             self.copy(0, sx, 0, sx).wait_recv()
             self.copy(4, sx, 0, sy).start()
+            if self.index:
+                hand_over()
             self.copy(1, sy, 1, sy).wait_recv()
             self.copy(5, sy, 1, sx).start()
-            if self.index:
-                hand_over()
 
         def wait_x(self):
             self.copy(2, sx, 1, sx).wait_recv()

time: 181 us -> 181 us (level)
  no operation moved by 1% of the time
where the time goes in v9:
time: 181 us; the launch traced here: 180 us
  Pallas kernels  179 us (99%)
    pallas_call x1, Pallas kernels, on_device(): pl.pallas_call(kernel, out_shape=[jax.ShapeDtypeStruct(*shape) for shape...  175 us
    pallas_call x1, Pallas kernels, finish(): pl.pallas_call(partial(finish_kernel, n_f, 6), out_shape=[jax.ShapeDtypeS...  4.35 us

profile of v9, /device:TPU:0, one launch (start us, length us, event | category | flops | bytes accessed | tf_op | source)
XLA Modules:
  0.0 180.3 jit_solution(3900107095797802207)
XLA Ops:
  0.7 175.1 %shard_map.271 = (bf16[256,1024]{1,0:T(8,128)(2,1)}, f32[256,1024]{1,0:T(8,128)}, f32[32,3072]{1,0:T(8,128)}, f32[32,1024]{1,0:T(8,128)}, f32[32,4096]{1,0:T(8,1...) custom-call(bf16[256,1024]{1,0:T(8,128)(2,1)} %bitcast.22, s32[1,256]{1,0:T(1,128)} %refs_1_.1, bf16[1,32]{1,0:T(2,128)(2,1)} %bitcast.24, ...), custom_call_target="tpu_custom_call" | custom-call | tf_op jit(solution)/shard_map/pallas_call | solution.py:1460
  175.8 4.3 %shard_map.272 = (bf16[256,1024]{1,0:T(8,128)(2,1)}, f32[256,1024]{1,0:T(8,128)}, f32[32,3072]{1,0:T(8,128)}, f32[32,1024]{1,0:T(8,128)}, f32[32,4096]{1,0:T(8,1...) custom-call(f32[16,128]{1,0:T(8,128)} %get-tuple-element.37.refs_0_,, ...), custom_call_target="tpu_custom_call" | custom-call | tf_op jit(solution)/shard_map/pallas_call | solution.py:1329
